TPU v7x, 512 devices: a whole 4x8x8 slice. The times are simulated.
512 devices in a mesh: query: 16 (over y, x_lo), train: 16 (over x_hi, z), mp: 2 (over core).
Axes of the slice: x: 4 (x_hi: 2, x_lo: 2; x = x_hi * 2 + x_lo), y: 8, z: 8, core: 2. Of those that a mesh axis runs over, the one named last changes fastest.
Arguments:
- residual: bfloat16 [2048, 8192], P('train'), may hold values from -6 to 6
- norm_gain: float32 [8192], replicated, may hold values from 0.1 to 1.9
- gate_weight: bfloat16 [8192, 14336], P('train', ('query', 'mp')), may hold values from -0.0625 to 0.0625
- up_weight: bfloat16 [8192, 14336], P('train', ('query', 'mp')), may hold values from -0.0625 to 0.0625
- out_grad: bfloat16 [2048, 8192], P('train', ('query', 'mp')), may hold values from -6 to 6
- left_factor: bfloat16 [32, 32, 14336], P(('query', 'mp')), may hold values from -0.0078125 to 0.0078125
- right_factor: bfloat16 [32, 32, 8192], P(('query', 'mp')), may hold values from -0.0625 to 0.0625
Outputs:
- scores: float32 [32, 2048], P(('query', 'mp'), 'train')
All inputs are finite; a program needn't handle non-finite values.
Results may differ from a plain program's by a relative error of at most 0.023.
Values may be sent and summed in bfloat16 or wider, within the bound.
No kernel may reach another device: no remote copies, remote signals or barrier semaphores. Data moves between devices by JAX's collectives and lax.ppermute only.
A program may use at most 64 MiB of HBM per device.

v0:
```python
import jax
import jax.numpy as jnp
from jax import lax
from jax.sharding import Mesh
from jax.sharding import PartitionSpec as P

TRAIN = ("train_0", "train_1")


norm_eps = 1e-05


def sum_in_order(tiles, axes, sequence):
    dims = [lax.axis_size(a) for a in axes]
    tiles = tiles.reshape(*dims, *tiles.shape[1:])
    tiles = tiles.transpose(*sequence, *range(len(axes), tiles.ndim))
    tiles = tiles.reshape(-1, *tiles.shape[len(axes) :])
    for k in sequence:
        tiles = lax.psum_scatter(tiles, axes[k], scatter_dimension=0, tiled=True)
    return tiles[0]


def split_up(value, dim, peers):
    before, after = (value.shape[:dim], value.shape[dim + 1 :])
    return jnp.moveaxis(value.reshape(*before, peers, -1, *after), dim, 0)


def summed_rows(value, axes, sequence, dim):
    peers = lax.axis_size(axes)
    return sum_in_order(split_up(value, dim, peers), axes, sequence)


def sent_to_all(value, axis):
    copies = jnp.broadcast_to(value, (lax.axis_size(axis), *value.shape))
    return lax.all_to_all(copies, axis, split_axis=0, concat_axis=0, tiled=True)


def laid_out(tiles, dim):
    dims = list(tiles.shape[1:])
    dims[dim] *= tiles.shape[0]
    return jnp.moveaxis(tiles, 0, dim).reshape(dims)


def collect(value, axis, dim):
    tiles = sent_to_all(value, axis)
    return laid_out(tiles, dim)


def on_device(residual, norm_gain, gate_weight, up_weight, out_grad, left_factor, right_factor):
    values = residual.astype(jnp.float32)
    mean_sq = jnp.mean(values * values, axis=1, keepdims=True)
    normed = (values * lax.rsqrt(mean_sq + norm_eps) * norm_gain[None, :]).astype(jnp.bfloat16)
    tok_rows = normed.shape[0]
    hidden_cols = gate_weight.shape[1]
    all_rows = lax.all_to_all(normed, TRAIN, split_axis=1, concat_axis=0, tiled=True)
    paired = jnp.concatenate([gate_weight, up_weight], axis=1)
    summed = summed_rows(
        jnp.dot(all_rows, paired, preferred_element_type=jnp.float32).astype(jnp.bfloat16),
        TRAIN,
        (1, 0),
        0,
    ).astype(jnp.float32)
    activation = (jax.nn.silu(summed[:, :hidden_cols]) * summed[:, hidden_cols:]).astype(
        jnp.bfloat16
    )
    queries = left_factor.shape[0]
    factor_rank = left_factor.shape[1]
    contract = (((1,), (1,)), ((), ()))
    left_flat = left_factor.reshape(queries * factor_rank, left_factor.shape[2])
    columns = left_flat
    projected = lax.dot_general(
        columns,
        lax.all_gather(activation, ("query", "mp"), axis=1, tiled=True),
        contract,
        preferred_element_type=jnp.float32,
    )
    right_flat = right_factor.reshape(queries * factor_rank, right_factor.shape[2])
    columns = right_flat
    sensed = lax.dot_general(
        columns, collect(out_grad, ("query", "mp"), 1), contract, preferred_element_type=jnp.float32
    )
    return jnp.sum((projected * sensed).reshape(queries, factor_rank, tok_rows), axis=1)


def solution(mesh):
    torus = Mesh(
        mesh.devices.reshape(mesh.shape["query"], 2, 8, mesh.shape["mp"]),
        ("query", "train_0", "train_1", "mp"),
    )
    placed = (
        P(TRAIN, None),
        P(),
        P(TRAIN, ("query", "mp")),
        P(TRAIN, ("query", "mp")),
        P(TRAIN, ("query", "mp")),
        P(("query", "mp"), None, None),
        P(("query", "mp"), None, None),
    )
    return jax.shard_map(
        on_device, mesh=torus, in_specs=placed, out_specs=P(("query", "mp"), TRAIN), check_vma=False
    )
```

profile of v0, /device:TPU:1, one launch (start us, length us, event | category | flops | bytes accessed | tf_op | source)
XLA Modules:
  0.0 259.8 jit_solution(11499937530667813829)
XLA Ops:
  6.5 0.0 copy-start
  6.5 0.0 reduce-scatter.3.cloned.1.call-start
  6.5 3.3 %copy.14 = bf16[128,8192]{0,1:T(8,128)(2,1)S(1)} copy(bf16[128,8192]{1,0:T(8,128)(2,1)} %param.7) | data formatting | bytes 4194304 | tf_op args[0]
  9.8 0.0 copy-start.3
  9.9 1.1 fusion
  11.0 0.0 copy-done.3
  11.0 3.5 %fusion.2 = bf16[128,8192]{0,1:T(8,128)(2,1)S(1)} fusion(bf16[128,8192]{0,1:T(8,128)(2,1)S(1)} %copy.14, f32[8192]{0:T(1024)S(1)} %copy-done.3, f32[128]{0:T(128)S(1)} %add_rsqrt_fusion), kind=kLoop, calls=%fused_computation.4 | loop fusion | flops 4194304 | bytes 4227584 | tf_op jit(solution)/shard_map/convert_element_type | solution.py:52
  14.5 62.2 %all_to_all.24 = bf16[128,16,512]{0,2,1:T(8,128)(2,1)S(1)} all-to-all(bf16[128,16,512]{0,2,1:T(8,128)(2,1)S(1)} %bitcast.31), channel_id=1, replica_groups=mesh['query'=16,'train_0'=2,'train_1'=8,'mp'=2] {'train_0','train_1'}, dimensions={1} | all-to-all | bytes 4194304 | tf_op jit(solution)/shard_map/all_to_all | solution.py:55
  76.6 2.6 %copy.15 = bf16[16,128,512]{2,1,0:T(8,128)(2,1)} copy(bf16[16,128,512]{1,2,0:T(8,128)(2,1)S(1)} %bitcast.32) | data formatting | bytes 4194304 | tf_op jit(solution)/shard_map/all_to_all | solution.py:55
  79.2 0.0 copy-done.4
  79.2 4.0 %convolution_convert_fusion = bf16[2048,896]{1,0:T(8,128)(2,1)S(1)} fusion(bf16[2048,512]{1,0:T(8,128)(2,1)} %bitcast.34, bf16[512,448]{0,1:T(8,128)(2,1)S(1)} %copy-done.4, bf16[512,448]{0,1:T(8,128)(2,1)} %param.9), kind=kOutput, calls=%fused_computation.5 | convolution fusion | flops 1882718208 | bytes 6684672 | tf_op jit(solution)/shard_map/dot_general | solution.py:58
  83.3 2.2 copy.16
  85.4 0.0 reduce-scatter.3.cloned.1.call-update
  85.4 0.0 reduce-scatter.5.cloned.1.call-start
  85.5 52.5 %reduce-scatter.3.cloned.1.call-done = bf16[2,128,896]{2,1,0:T(8,128)(2,1)} async-done(((bf16[16,128,896]{2,1,0:T(8,128)(2,1)}), bf16[2,128,896]{2,1,0:T(8,128)(2,1)}) %reduce-scatter.3.cloned.1.call-update) | async-done | bytes 458768 | tf_op jit(solution)/shard_map/reduce_scatter | solution.py:19
  138.0 0.0 reduce-scatter.5.cloned.1.call-update
  138.0 0.0 all-gather.2.cloned.1.call-start
  138.1 24.4 %reduce-scatter.5.cloned.1.call-done = bf16[1,128,896]{2,1,0:T(8,128)(2,1)} async-done(((bf16[2,128,896]{2,1,0:T(8,128)(2,1)}), bf16[1,128,896]{2,1,0:T(8,128)(2,1)}) %reduce-scatter.5.cloned.1.call-update) | async-done | bytes 229392 | tf_op jit(solution)/shard_map/reduce_scatter | solution.py:19
  162.5 1.0 bitcast_convert_fusion
  163.5 0.1 fusion.11
  163.6 0.8 copy.17
  164.4 0.0 all-gather.2.cloned.1.call-update
  164.4 0.0 copy-done.2
  164.4 0.1 copy.18
  164.5 0.5 broadcast_in_dim.2
  165.0 0.0 copy-start.1
  165.0 72.9 %all_to_all.25 = bf16[32,128,256]{1,2,0:T(8,128)(2,1)S(1)} all-to-all(bf16[32,128,256]{1,2,0:T(8,128)(2,1)S(1)} %broadcast_in_dim.2), channel_id=1, replica_groups=mesh['query'=16,'train_0'=2,'train_1'=8,'mp'=2] {'query','mp'}, dimensions={0} | all-to-all | bytes 4194304 | tf_op jit(solution)/shard_map/all_to_all | solution.py:35
  237.9 0.0 copy-done.1
  237.9 0.4 fusion.9
  238.3 11.7 %all-gather.2.cloned.1.call-done = bf16[128,14336]{0,1:T(8,128)(2,1)} async-done(((bf16[128,448]{0,1:T(8,128)(2,1)}), bf16[128,14336]{0,1:T(8,128)(2,1)}) %all-gather.2.cloned.1.call-update) | async-done | bytes 3670032 | tf_op jit(solution)/shard_map/all_gather | solution.py:73
  250.0 0.0 copy-done
  250.0 3.2 %fusion.4 = f32[128]{0:T(128)} fusion(f32[32,128]{1,0:T(8,128)S(1)} %fusion.9, bf16[128,14336]{0,1:T(8,128)(2,1)} %all-gather.2.cloned.1.call-done, bf16[1,32,14336]{2,1,0:T(8,128)(2,1)S(1)} %copy-done), kind=kOutput, calls=%fused_computation.8 | convolution fusion | flops 117448576 | bytes 4604416 | tf_op jit(solution)/shard_map/dot_general | solution.py:71
  (3 shorter events, 0.0 us)
Async XLA Ops:
  6.5 243.5 %copy-start = (bf16[1,32,14336]{2,1,0:T(8,128)(2,1)S(1)}, bf16[1,32,14336]{2,1,0:T(8,128)(2,1)}, u32[]{:S(2)}) copy-start(bf16[1,32,14336]{2,1,0:T(8,128)(2,1)} %param.12) | copy-start | bytes 2752516
  6.5 131.5 %reduce-scatter.3.cloned.1.call-start = ((), (), s32[]{:S(2)}) async-start(), calls=%async_computation.4 | async-start | bytes 4128768 | tf_op jit(solution)/shard_map/reduce_scatter | solution.py:19
  9.8 1.1 copy-start.3
  76.6 2.6 %copy-start.4 = (bf16[512,448]{0,1:T(8,128)(2,1)S(1)}, bf16[512,448]{0,1:T(8,128)(2,1)}, u32[]{:S(2)}) copy-start(bf16[512,448]{0,1:T(8,128)(2,1)} %param.10) | copy-start | bytes 1376260
  85.4 79.0 %copy-start.2 = (bf16[128,256]{1,0:T(8,128)(2,1)S(1)}, bf16[128,256]{1,0:T(8,128)(2,1)}, u32[]{:S(2)}) copy-start(bf16[128,256]{1,0:T(8,128)(2,1)} %param.11) | copy-start | bytes 196612
  85.4 77.0 %reduce-scatter.5.cloned.1.call-start = ((), (), s32[]{:S(2)}) async-start(), calls=%async_computation.5 | async-start | bytes 688128 | tf_op jit(solution)/shard_map/reduce_scatter | solution.py:19
  138.0 112.0 %all-gather.2.cloned.1.call-start = ((), (), s32[]{:S(2)}) async-start(), calls=%async_computation.6 | async-start | bytes 3784704 | tf_op jit(solution)/shard_map/all_gather | solution.py:73
  165.0 72.9 %copy-start.1 = (bf16[1,32,8192]{2,1,0:T(8,128)(2,1)S(1)}, bf16[1,32,8192]{2,1,0:T(8,128)(2,1)}, u32[]{:S(2)}) copy-start(bf16[1,32,8192]{2,1,0:T(8,128)(2,1)} %param.13) | copy-start | bytes 1572868
Sparse Core Ops, SparseCore 0:
  85.6 52.3 reduce-scatter.2
  140.8 21.6 reduce-scatter.4
  164.9 85.1 all-gather.1
where the time goes:
time: 260 us
  blocking collectives  135 us (52%)
  waiting for transfers between devices  88.6 us (34%)
  between operations  13.2 us (5%)
  local copies, waits for them, and re-layouts  9.42 us (4%)
  matrix products  7.71 us (3%)
  other arithmetic  5.69 us (2%)
    reduce_scatter x2, waiting for transfers between devices, sum_in_order(): tiles = lax.psum_scatter(tiles, axes[k], scatter_dimension=0, tiled=True)  76.9 us
    all_to_all x1, blocking collectives, sent_to_all(): return lax.all_to_all(copies, axis, split_axis=0, concat_axis=0, tiled=True)  72.9 us
    all_to_all x1, blocking collectives, on_device(): lax.all_to_all(normed, TRAIN, split_axis=1, concat_axis=0, tiled=True)  62.2 us
    all_gather x1, waiting for transfers between devices, on_device(): lax.all_gather(activation, ('query', 'mp'), axis=1, tiled=True)  11.7 us
  transfers between devices with their start and end apart: 3, of which 3 were waited for; matrix products, arithmetic and copies ran while one was open for 0% of the time, Pallas kernels for 0%

commit v1 on v0

v1 whole, which is shorter than its diff:
```python
import functools

import jax
import jax.numpy as jnp
from jax import lax
from jax.experimental import pallas as pl
from jax.experimental.pallas import tpu as pltpu
from jax.sharding import Mesh
from jax.sharding import PartitionSpec as P

TRAIN = ("xh", "z")
QM = ("y", "xl", "c")
CHIPS = ("y", "xl")
SWAP = ((0, 1), (1, 0))

norm_eps = 1e-05


def norm_kernel(half_ref, res_ref, gain_ref, out_ref):
    values = res_ref[...].astype(jnp.float32)
    mean_sq = jnp.mean(values * values, axis=1, keepdims=True)
    scale = lax.rsqrt(mean_sq + norm_eps)
    peers, _, width = out_ref.shape
    rows = width // 2
    for xh in range(2):
        for k in range(peers):
            at = (xh * peers + k) * rows
            piece = res_ref[:, at : at + rows].astype(jnp.float32)
            piece = piece * scale * gain_ref[:, at : at + rows]
            out_ref[k, :, xh * rows : (xh + 1) * rows] = piece.astype(out_ref.dtype)


def normed_by_peer(residual, norm_gain, half, peers):
    tokens, width = residual.shape
    mine, slab = tokens // 2, 16
    steps = mine // slab
    return pl.pallas_call(
        norm_kernel,
        out_shape=jax.ShapeDtypeStruct((peers, mine, width // peers), jnp.bfloat16),
        grid_spec=pltpu.PrefetchScalarGridSpec(
            num_scalar_prefetch=1,
            grid=(steps,),
            in_specs=[
                pl.BlockSpec((slab, width), lambda i, h: (h[0] * steps + i, 0)),
                pl.BlockSpec((1, width), lambda i, h: (0, 0)),
            ],
            out_specs=pl.BlockSpec((peers, slab, width // peers), lambda i, h: (0, i, 0)),
        ),
        compiler_params=pltpu.CompilerParams(vmem_limit_bytes=32 << 20),
        cost_estimate=pl.CostEstimate(flops=4 * mine * width, bytes_accessed=4 * mine * width, transcendentals=mine),
        name="norm_rows",
    )(half.reshape(1), residual, norm_gain.reshape(1, width))


def both(own, other, index, dim):
    first = jnp.where(index == 0, own, other)
    second = jnp.where(index == 0, other, own)
    return jnp.concatenate([first, second], axis=dim)


def on_device(residual, norm_gain, gate_weight, up_weight, out_grad, left_factor, right_factor):
    c, xh = lax.axis_index("c"), lax.axis_index("xh")
    peers, chips = lax.axis_size("z"), lax.axis_size(CHIPS)
    tokens = residual.shape[0]
    half = tokens // 2
    cols = gate_weight.shape[1]
    rank = left_factor.shape[1]

    normed = normed_by_peer(residual, norm_gain, c, peers)
    rows = lax.all_to_all(normed, "z", 0, 0, tiled=True)
    rows_flat = rows.reshape(peers * half, -1)

    mine = jnp.concatenate([gate_weight.T, up_weight.T], axis=0)
    theirs = lax.ppermute(mine, "xh", SWAP)
    paired = both(mine, theirs, xh, 1)
    neighbour = lax.ppermute(paired, "c", SWAP)
    gate = both(paired[:cols], neighbour[:cols], c, 0)
    up = both(paired[cols:], neighbour[cols:], c, 0)
    weight = jnp.concatenate([gate, up], axis=0)

    contract = (((1,), (1,)), ((), ()))
    term = lax.dot_general(rows_flat, weight, contract, preferred_element_type=jnp.float32)
    term = term.astype(jnp.bfloat16).reshape(peers, half, -1)
    summed = lax.psum_scatter(term, "z", scatter_dimension=0, tiled=True)

    left = left_factor.reshape(rank, chips, -1)
    right = right_factor.reshape(rank, chips, -1)
    hidden = left.shape[2]
    packed = jnp.concatenate([left, right], axis=2).transpose(1, 0, 2)
    packed, rows = lax.optimization_barrier((packed, rows))
    got = lax.all_to_all(packed, CHIPS, 0, 0, tiled=True)
    beside = lax.ppermute(got, "c", SWAP)
    first = jnp.where(c == 0, got, beside)
    second = jnp.where(c == 0, beside, got)
    factors = jnp.stack([first, second], axis=1).reshape(chips * 2 * rank, -1)

    keep = lax.dynamic_slice_in_dim(out_grad, c * half, half, 0)
    give = lax.dynamic_slice_in_dim(out_grad, (1 - c) * half, half, 0)
    grad = both(keep, lax.ppermute(give, "c", SWAP), c, 1)
    sensed = lax.dot_general(factors[:, hidden:], grad, contract, preferred_element_type=jnp.float32)

    summed = summed[0].astype(jnp.float32)
    activation = (jax.nn.silu(summed[:, :hidden]) * summed[:, hidden:]).astype(jnp.bfloat16)
    projected = lax.dot_general(factors[:, :hidden], activation, contract, preferred_element_type=jnp.float32)

    parts = jnp.concatenate([projected, sensed], axis=1).astype(jnp.bfloat16)
    parts = parts.reshape(2 * chips, rank, 2 * half)
    parts = lax.all_to_all(parts, QM, 0, 0, tiled=True)
    whole = jnp.sum(parts.reshape(chips, 2, rank, 2 * half).astype(jnp.float32), axis=0)
    scores = jnp.sum(whole[:, :, :half] * whole[:, :, half:], axis=1)
    return scores.reshape(1, tokens)


def solution(mesh):
    torus = Mesh(mesh.devices.reshape(8, 2, 2, 8, 2), ("y", "xl", "xh", "z", "c"))
    placed = (
        P(TRAIN, None),
        P(),
        P(TRAIN, QM),
        P(TRAIN, QM),
        P(TRAIN, QM),
        P(QM, None, None),
        P(QM, None, None),
    )
    return jax.shard_map(on_device, mesh=torus, in_specs=placed, out_specs=P(QM, TRAIN), check_vma=False)
```

time: 260 us -> 145 us (0.56)
  blocking collectives: 135 us -> 23.6 us
  waiting for transfers between devices: 88.6 us -> 45 us
  starting transfers between devices: 0.08 us -> 38.2 us
  local copies, waits for them, and re-layouts: 9.42 us -> 4.17 us
    all_to_all x2 -> x1, blocking collectives: 135 us -> 23.6 us  [on_device(): parts = lax.all_to_all(parts, QM, 0, 0, tiled=True)]
    reduce_scatter x2 -> x1, waiting for transfers between devices: 76.9 us -> 2.29 us  [on_device(): summed = lax.psum_scatter(term, 'z', scatter_dimension=0, tiled=True)]
    all_to_all x0 -> x2, waiting for transfers between devices: none -> 38.8 us  [the longest x1 22.6 us: on_device(): got = lax.all_to_all(packed, CHIPS, 0, 0, tiled=True)]
    ppermute x0 -> x4, starting transfers between devices: none -> 21.1 us  [the longest x1 6.84 us: on_device(): neighbour = lax.ppermute(paired, 'c', SWAP)]
    all_to_all x0 -> x2, starting transfers between devices: none -> 17.1 us  [the longest x1 10.2 us: on_device(): rows = lax.all_to_all(normed, 'z', 0, 0, tiled=True)]
    all_gather x1 -> x0, waiting for transfers between devices: 11.7 us -> none  [on_device(): lax.all_gather(activation, ('query', 'mp'), axis=1, tiled=True)]
    ppermute x0 -> x4, waiting for transfers between devices: none -> 3.9 us  [the longest x1 2.73 us: on_device(): theirs = lax.ppermute(mine, 'xh', SWAP)]
    convert_element_type x3 -> x1, other arithmetic: 4.59 us -> 0.97 us  [on_device(): summed = summed[0].astype(jnp.float32)]
  transfers between devices with their start and end apart: 3 -> 7, of which waited for: 3 -> 5; matrix products, arithmetic and copies ran while one was open for 0% -> 11% of each run, Pallas kernels for 0% -> 1%
where the time goes in v1:
time: 145 us; the launch traced here: 144 us
  waiting for transfers between devices  45 us (31%)
  starting transfers between devices  38.2 us (26%)
  blocking collectives  23.6 us (16%)
  between operations  13.6 us (9%)
  matrix products  9.3 us (6%)
  other arithmetic  8.28 us (6%)
  local copies, waits for them, and re-layouts  4.17 us (3%)
  Pallas kernels  2.07 us (1%)
    all_to_all x1, blocking collectives, on_device(): parts = lax.all_to_all(parts, QM, 0, 0, tiled=True)  23.6 us
    all_to_all x1, waiting for transfers between devices, on_device(): got = lax.all_to_all(packed, CHIPS, 0, 0, tiled=True)  22.6 us
    all_to_all x1, waiting for transfers between devices, on_device(): rows = lax.all_to_all(normed, 'z', 0, 0, tiled=True)  16.2 us
    all_to_all x1, starting transfers between devices, on_device(): rows = lax.all_to_all(normed, 'z', 0, 0, tiled=True)  10.2 us
    dot_general x1, matrix products, on_device(): lax.dot_general(rows_flat, weight, contract, preferred_element_type=jnp.f...  8.18 us
    all_to_all x1, starting transfers between devices, on_device(): got = lax.all_to_all(packed, CHIPS, 0, 0, tiled=True)  6.95 us
    ppermute x1, starting transfers between devices, on_device(): neighbour = lax.ppermute(paired, 'c', SWAP)  6.84 us
    ppermute x1, starting transfers between devices, on_device(): beside = lax.ppermute(got, 'c', SWAP)  6.82 us
  transfers between devices with their start and end apart: 7, of which 5 were waited for; matrix products, arithmetic and copies ran while one was open for 11% of the time, Pallas kernels for 1%

profile of v1, /device:TPU:1, one launch (start us, length us, event | category | flops | bytes accessed | tf_op | source)
XLA Modules:
  0.0 144.3 jit_solution(1160375411623078917)
XLA Ops:
  6.5 1.2 pad_maximum_fusion.2
  7.8 5.5 %collective-permute-start.1 = (bf16[896,512]{1,0:T(8,128)(2,1)S(1)}, bf16[896,512]{1,0:T(8,128)(2,1)}, u32[]{:S(2)}, u32[]{:S(2)}) collective-permute-start(bf16[896,512]{1,0:T(8,128)(2,1)S(1)} %pad_maximum_fusion.2), channel_id=1, source_target_pairs={{0,16},{16,0},{1,17},{17,1},{2,18},{18,2},{3,19},{19,3},{4,20},{20... | collective-permute-start | bytes 2752520 | tf_op jit(solution)/shard_map/ppermute | solution.py:74
  13.3 1.6 %copy-done = bf16[128,8192]{1,0:T(8,128)(2,1)S(1)} copy-done((bf16[128,8192]{1,0:T(8,128)(2,1)S(1)}, bf16[128,8192]{1,0:T(8,128)(2,1)}, u32[]{:S(2)}) %copy-start) | copy-done | bytes 2097176
  14.9 2.1 %norm_rows.1 = bf16[8,64,1024]{2,1,0:T(8,128)(2,1)} custom-call(s32[1]{0:T(128)} %bitcast.1.half_ref, bf16[128,8192]{1,0:T(8,128)(2,1)S(1)} %copy-done, f32[1,8192]{1,0:T(1,128)S(1)} %bitcast.29), custom_call_target="tpu_custom_call" | custom-call | flops 2097152 | bytes 2097152 | tf_op jit(solution)/shard_map/norm_rows/pallas_call | solution.py:37
  16.9 10.2 %all-to-all-start = ((bf16[8,64,1024]{2,1,0:T(8,128)(2,1)}), bf16[8,64,1024]{2,1,0:T(8,128)(2,1)}, u32[]{:S(2)}, u32[]{:S(2)}) async-start(bf16[8,64,1024]{2,1,0:T(8,128)(2,1)} %norm_rows.1), calls=%async_computation | async-start | bytes 2097152 | tf_op jit(solution)/shard_map/all_to_all | solution.py:70
  27.1 2.7 %collective-permute-done.1 = bf16[896,512]{1,0:T(8,128)(2,1)} collective-permute-done((bf16[896,512]{1,0:T(8,128)(2,1)S(1)}, bf16[896,512]{1,0:T(8,128)(2,1)}, u32[]{:S(2)}, u32[]{:S(2)}) %collective-permute-start.1) | collective-permute-done | bytes 917536 | tf_op jit(solution)/shard_map/ppermute | solution.py:74
  29.8 1.5 %broadcast_select_fusion.1 = (bf16[896,512]{1,0:T(8,128)(2,1)S(1)}, bf16[896,512]{1,0:T(8,128)(2,1)S(1)}) fusion(bf16[896,512]{1,0:T(8,128)(2,1)} %collective-permute-done.1, pred[]{:T(512)S(6)} %eq.5, bf16[448,512]{1,0:T(8,128)(2,1)S(1)} %bitcast.36, bf16[448,512]{1,0:T(8,128)(2,1)S(1)} %bitcast.38), kind=kLoop, calls=%fused_computation.27 | loop fusion | flops 2752512 | bytes 3670017 | tf_op jit(solution)/shard_map/jit(_where)/select_n | solution.py:56
  31.4 1.5 %pad_maximum_fusion.1 = bf16[896,1024]{1,0:T(8,128)(2,1)} fusion(bf16[896,512]{1,0:T(8,128)(2,1)S(1)} %get-tuple-element.14, bf16[896,512]{1,0:T(8,128)(2,1)S(1)} %get-tuple-element.13), kind=kLoop, calls=%fused_computation.12 | loop fusion | flops 3670016 | bytes 3670016 | tf_op jit(solution)/shard_map/concatenate | solution.py:58
  32.9 6.8 %collective-permute-start.2 = (bf16[896,1024]{1,0:T(8,128)(2,1)}, bf16[896,1024]{1,0:T(8,128)(2,1)}, u32[]{:S(2)}, u32[]{:S(2)}) collective-permute-start(bf16[896,1024]{1,0:T(8,128)(2,1)} %pad_maximum_fusion.1), channel_id=1, source_target_pairs={{0,1},{1,0},{2,3},{3,2},{4,5},{5,4},{6,7},{7,6},{8,9},{9,8},{10,11... | collective-permute-start | bytes 5505032 | tf_op jit(solution)/shard_map/ppermute | solution.py:76
  39.8 0.1 copy.22
  39.9 0.2 copy.23
  40.1 0.1 maximum_bitcast_fusion
  40.2 16.2 %all-to-all-done = bf16[8,64,1024]{2,1,0:T(8,128)(2,1)} async-done(((bf16[8,64,1024]{2,1,0:T(8,128)(2,1)}), bf16[8,64,1024]{2,1,0:T(8,128)(2,1)}, u32[]{:S(2)}, u32[]{:S(2)}) %all-to-all-start) | async-done | bytes 1048608 | tf_op jit(solution)/shard_map/all_to_all | solution.py:70
  56.4 1.4 copy.18
  57.8 7.0 %all-to-all-start.1 = ((bf16[16,32,1408]{2,1,0:T(8,128)(2,1)}), bf16[16,32,1408]{2,1,0:T(8,128)(2,1)S(1)}, u32[]{:S(2)}, u32[]{:S(2)}) async-start(bf16[16,32,1408]{2,1,0:T(8,128)(2,1)} %copy.18), calls=%async_computation.1 | async-start | bytes 2883584 | tf_op jit(solution)/shard_map/all_to_all | solution.py:91
  64.8 2.0 %broadcast_select_fusion.5 = (bf16[448,1024]{1,0:T(8,128)(2,1)S(1)}, bf16[448,1024]{1,0:T(8,128)(2,1)S(1)}, bf16[448,1024]{1,0:T(8,128)(2,1)S(1)}, bf16[448,1024]{1,0:T(8,128)(2,1)S(1)}) fusion(pred[]{:T(512)S(6)} %eq.4, bf16[896,1024]{1,0:T(8,128)(2,1)} %collective-permute-done.2, bf16[896,512]{1,0:T(8,128)(2,1)S(1)} %get-tuple-element.14, ...), kind=kLoop, calls=%fused_computation.31 | loop fusion | flops 9175040 | bytes 7340033 | tf_op jit(solution)/shard_map/jit(_where)/select_n | solution.py:56
  66.8 8.2 %fusion.8 = bf16[512,1792]{1,0:T(8,128)(2,1)} fusion(bf16[512,1024]{1,0:T(8,128)(2,1)} %bitcast.7, bf16[448,1024]{1,0:T(8,128)(2,1)S(1)} %get-tuple-element.10, bf16[448,1024]{1,0:T(8,128)(2,1)S(1)} %get-tuple-element.9, bf16[448,1024]{1,0:T(8,128)(2,1)S(1)} %get-tuple-element.8, bf16[448,1024]{1,0:T(8,128)(2,1)S(1)} %get-tuple-element.7), kind=kOutput, calls=%fused_computation.8 | convolution fusion | flops 1894645760 | bytes 6553600 | tf_op jit(solution)/shard_map/dot_general | solution.py:82
  75.0 22.6 %all-to-all-done.1 = bf16[16,32,1408]{2,1,0:T(8,128)(2,1)S(1)} async-done(((bf16[16,32,1408]{2,1,0:T(8,128)(2,1)}), bf16[16,32,1408]{2,1,0:T(8,128)(2,1)S(1)}, u32[]{:S(2)}, u32[]{:S(2)}) %all-to-all-start.1) | async-done | bytes 1441824 | tf_op jit(solution)/shard_map/all_to_all | solution.py:91
  97.6 6.8 %collective-permute-start = (bf16[16,32,1408]{2,1,0:T(8,128)(2,1)S(1)}, bf16[16,32,1408]{2,1,0:T(8,128)(2,1)S(1)}, u32[]{:S(2)}, u32[]{:S(2)}) collective-permute-start(bf16[16,32,1408]{2,1,0:T(8,128)(2,1)S(1)} %all-to-all-done.1), channel_id=1, source_target_pairs={{0,1},{1,0},{2,3},{3,2},{4,5},{5,4},{6,7},{7,6},{8,9},{9,8},{10,11... | collective-permute-start | bytes 4325384 | tf_op jit(solution)/shard_map/ppermute | solution.py:92
  104.5 1.9 %collective-permute-start.3 = (bf16[64,256]{1,0:T(8,128)(2,1)S(1)}, bf16[64,256]{1,0:T(8,128)(2,1)S(1)}, u32[]{:S(2)}, u32[]{:S(2)}) collective-permute-start(bf16[64,256]{1,0:T(8,128)(2,1)S(1)} %constant_dynamic-slice_fusion), channel_id=1, source_target_pairs={{0,1},{1,0},{2,3},{3,2},{4,5},{5,4},{6,7},{7,6},{8,9},{9,8},{10,11... | collective-permute-start | bytes 98312 | tf_op jit(solution)/shard_map/ppermute | solution.py:99
  106.4 1.2 collective-permute-done.3
  107.6 0.3 select_bitcast_fusion.1
  107.9 0.3 pad_maximum_fusion
  108.2 0.4 convolution_convert_fusion
  108.6 0.2 copy.21
  108.8 2.3 %reduce-scatter.2.cloned.1.call-done = bf16[1,64,1792]{2,1,0:T(8,128)(2,1)} async-done(((bf16[8,64,1792]{2,1,0:T(8,128)(2,1)}), bf16[1,64,1792]{2,1,0:T(8,128)(2,1)}) %reduce-scatter.2.cloned.1.call-update) | async-done | bytes 229392 | tf_op jit(solution)/shard_map/reduce_scatter | solution.py:84
  111.1 1.0 bitcast_convert_fusion
  112.1 0.7 fusion.13
  112.8 0.2 copy.20
  112.9 0.1 pad_maximum_fusion.3
  113.1 23.6 %all_to_all.15 = bf16[32,32,128]{2,1,0:T(8,128)(2,1)S(1)} all-to-all(bf16[32,32,128]{2,1,0:T(8,128)(2,1)S(1)} %pad_maximum_fusion.3), channel_id=1, replica_groups=mesh['y'=8,'xl'=2,'xh'=2,'z'=8,'c'=2] {'y','xl','c'}, dimensions={0} | all-to-all | bytes 524288 | tf_op jit(solution)/shard_map/all_to_all | solution.py:108
  136.9 0.6 reshape.41
  (21 shorter events, 0.2 us)
Async XLA Ops:
  6.5 6.7 %copy-start.1 = (f32[8192]{0:T(1024)S(1)}, f32[8192]{0:T(1024)}, u32[]{:S(2)}) copy-start(f32[8192]{0:T(1024)} %param.8) | copy-start | bytes 98308
  7.8 22.1 %collective-permute-start.1 = (bf16[896,512]{1,0:T(8,128)(2,1)S(1)}, bf16[896,512]{1,0:T(8,128)(2,1)}, u32[]{:S(2)}, u32[]{:S(2)}) collective-permute-start(bf16[896,512]{1,0:T(8,128)(2,1)S(1)} %pad_maximum_fusion.2), channel_id=1, source_target_pairs={{0,16},{16,0},{1,17},{17,1},{2,18},{18,2},{3,19},{19,3},{4,20},{20... | collective-permute-start | bytes 2752520 | tf_op jit(solution)/shard_map/ppermute | solution.py:74
  13.3 1.6 %copy-start = (bf16[128,8192]{1,0:T(8,128)(2,1)S(1)}, bf16[128,8192]{1,0:T(8,128)(2,1)}, u32[]{:S(2)}) copy-start(bf16[128,8192]{1,0:T(8,128)(2,1)} %res_ref.1) | copy-start | bytes 6291460
  16.9 12.9 %copy-start.2 = (bf16[512,448]{0,1:T(8,128)(2,1)S(1)}, bf16[512,448]{0,1:T(8,128)(2,1)}, u32[]{:S(2)}) copy-start(bf16[512,448]{0,1:T(8,128)(2,1)} %param.10) | copy-start | bytes 1376260
  16.9 12.9 %copy-start.3 = (bf16[512,448]{0,1:T(8,128)(2,1)S(1)}, bf16[512,448]{0,1:T(8,128)(2,1)}, u32[]{:S(2)}) copy-start(bf16[512,448]{0,1:T(8,128)(2,1)} %param.9) | copy-start | bytes 1376260
  16.9 39.5 %all-to-all-start = ((bf16[8,64,1024]{2,1,0:T(8,128)(2,1)}), bf16[8,64,1024]{2,1,0:T(8,128)(2,1)}, u32[]{:S(2)}, u32[]{:S(2)}) async-start(bf16[8,64,1024]{2,1,0:T(8,128)(2,1)} %norm_rows.1), calls=%async_computation | async-start | bytes 2097152 | tf_op jit(solution)/shard_map/all_to_all | solution.py:70
  31.4 8.4 %copy-start.4 = (bf16[1,32,14336]{2,1,0:T(8,128)(2,1)S(1)}, bf16[1,32,14336]{2,1,0:T(8,128)(2,1)}, u32[]{:S(2)}) copy-start(bf16[1,32,14336]{2,1,0:T(8,128)(2,1)} %param.12) | copy-start | bytes 2752516
  32.9 7.0 %copy-start.5 = (bf16[1,32,8192]{2,1,0:T(8,128)(2,1)S(1)}, bf16[1,32,8192]{2,1,0:T(8,128)(2,1)}, u32[]{:S(2)}) copy-start(bf16[1,32,8192]{2,1,0:T(8,128)(2,1)} %param.13) | copy-start | bytes 1572868
  32.9 31.8 %collective-permute-start.2 = (bf16[896,1024]{1,0:T(8,128)(2,1)}, bf16[896,1024]{1,0:T(8,128)(2,1)}, u32[]{:S(2)}, u32[]{:S(2)}) collective-permute-start(bf16[896,1024]{1,0:T(8,128)(2,1)} %pad_maximum_fusion.1), channel_id=1, source_target_pairs={{0,1},{1,0},{2,3},{3,2},{4,5},{5,4},{6,7},{7,6},{8,9},{9,8},{10,11... | collective-permute-start | bytes 5505032 | tf_op jit(solution)/shard_map/ppermute | solution.py:76
  57.8 39.9 %all-to-all-start.1 = ((bf16[16,32,1408]{2,1,0:T(8,128)(2,1)}), bf16[16,32,1408]{2,1,0:T(8,128)(2,1)S(1)}, u32[]{:S(2)}, u32[]{:S(2)}) async-start(bf16[16,32,1408]{2,1,0:T(8,128)(2,1)} %copy.18), calls=%async_computation.1 | async-start | bytes 2883584 | tf_op jit(solution)/shard_map/all_to_all | solution.py:91
  64.7 46.4 %reduce-scatter.2.cloned.1.call-start = ((), (), s32[]{:S(2)}) async-start(), calls=%async_computation.4 | async-start | bytes 2064384 | tf_op jit(solution)/shard_map/reduce_scatter | solution.py:84
  75.0 29.5 %copy-start.6 = (bf16[128,256]{1,0:T(8,128)(2,1)S(1)}, bf16[128,256]{1,0:T(8,128)(2,1)}, u32[]{:S(2)}) copy-start(bf16[128,256]{1,0:T(8,128)(2,1)} %param.11) | copy-start | bytes 196612
  97.6 10.0 %collective-permute-start = (bf16[16,32,1408]{2,1,0:T(8,128)(2,1)S(1)}, bf16[16,32,1408]{2,1,0:T(8,128)(2,1)S(1)}, u32[]{:S(2)}, u32[]{:S(2)}) collective-permute-start(bf16[16,32,1408]{2,1,0:T(8,128)(2,1)S(1)} %all-to-all-done.1), channel_id=1, source_target_pairs={{0,1},{1,0},{2,3},{3,2},{4,5},{5,4},{6,7},{7,6},{8,9},{9,8},{10,11... | collective-permute-start | bytes 4325384 | tf_op jit(solution)/shard_map/ppermute | solution.py:92
  104.5 3.1 %collective-permute-start.3 = (bf16[64,256]{1,0:T(8,128)(2,1)S(1)}, bf16[64,256]{1,0:T(8,128)(2,1)S(1)}, u32[]{:S(2)}, u32[]{:S(2)}) collective-permute-start(bf16[64,256]{1,0:T(8,128)(2,1)S(1)} %constant_dynamic-slice_fusion), channel_id=1, source_target_pairs={{0,1},{1,0},{2,3},{3,2},{4,5},{5,4},{6,7},{7,6},{8,9},{9,8},{10,11... | collective-permute-start | bytes 98312 | tf_op jit(solution)/shard_map/ppermute | solution.py:99
Sparse Core Ops, SparseCore 0:
  75.2 35.9 reduce-scatter.1

commit v2 on v1

v2 whole, which is shorter than its diff:
```python
import jax
import jax.numpy as jnp
from jax import lax
from jax.experimental import pallas as pl
from jax.experimental.pallas import tpu as pltpu
from jax.sharding import Mesh
from jax.sharding import PartitionSpec as P

TRAIN = ("xh", "z")
QM = ("y", "xl", "c")
CHIPS = ("y", "xl")
SWAP = ((0, 1), (1, 0))
RING = 8
STEPS = RING // 2 + 1
EARLY = (3, 2, 1)


def away(step, xh):
    sign = 1 if step % 2 else -1
    return step if step in (0, RING // 2) else sign * step * (1 - 2 * xh)


norm_eps = 1e-05


def norm_kernel(core_ref, pair_ref, own_ref, other_ref, own_gain_ref, other_gain_ref, out_ref):
    halves = [ref[...].astype(jnp.float32) for ref in (own_ref, other_ref)]
    gains = [ref[...] for ref in (own_gain_ref, other_gain_ref)]
    peers, _, width = out_ref.shape
    square = sum(jnp.sum(h * h, axis=1, keepdims=True) for h in halves)
    scale = lax.rsqrt(square / (peers * width) + norm_eps)
    rows = width // 2
    for part in range(2):
        normed = (halves[part] * scale * gains[part]).astype(out_ref.dtype)
        for k in range(peers):
            out_ref[k, :, part * rows : (part + 1) * rows] = normed[:, k * rows : (k + 1) * rows]


def normed_by_peer(residual, norm_gain, core, pair, peers):
    tokens, width = residual.shape
    mine, slab = tokens // 2, 32
    steps = mine // slab
    gain = norm_gain.reshape(1, width)
    return pl.pallas_call(
        norm_kernel,
        out_shape=jax.ShapeDtypeStruct((peers, mine, width // peers), jnp.bfloat16),
        grid_spec=pltpu.PrefetchScalarGridSpec(
            num_scalar_prefetch=2,
            grid=(steps,),
            in_specs=[
                pl.BlockSpec((slab, width // 2), lambda i, c, x: (c[0] * steps + i, x[0])),
                pl.BlockSpec((slab, width // 2), lambda i, c, x: (c[0] * steps + i, 1 - x[0])),
                pl.BlockSpec((1, width // 2), lambda i, c, x: (0, x[0])),
                pl.BlockSpec((1, width // 2), lambda i, c, x: (0, 1 - x[0])),
            ],
            out_specs=pl.BlockSpec((peers, slab, width // peers), lambda i, c, x: (0, i, 0)),
        ),
        compiler_params=pltpu.CompilerParams(vmem_limit_bytes=60 << 20),
        cost_estimate=pl.CostEstimate(flops=4 * mine * width, bytes_accessed=4 * mine * width, transcendentals=mine),
        name="norm_rows",
    )(core.reshape(1), pair.reshape(1), residual, residual, gain, gain)


def term_kernel(rows_ref, weight_ref, out_ref):
    peers, half, width = rows_ref.shape
    rows = rows_ref[...].reshape(peers * half, width)
    cols = weight_ref.shape[0] // 2
    for core in range(2):
        at = slice(core * cols, (core + 1) * cols)
        total = lax.dot_general(rows, weight_ref[at], (((1,), (1,)), ((), ())), preferred_element_type=jnp.float32)
        out_ref[:, :, at] = total.astype(out_ref.dtype).reshape(peers, half, cols)


def terms_of(rows, weight):
    peers, half, width = rows.shape
    cols = weight.shape[0]
    return pl.pallas_call(
        term_kernel,
        out_shape=jax.ShapeDtypeStruct((peers, half, cols), jnp.bfloat16),
        compiler_params=pltpu.CompilerParams(vmem_limit_bytes=24 << 20),
        cost_estimate=pl.CostEstimate(
            flops=2 * peers * half * width * cols, bytes_accessed=2 * cols * width + 6 * peers * half * width, transcendentals=0
        ),
        name="terms",
    )(rows, weight)


def whole_kernel(body, scalars, inputs, outputs, name):
    size = sum(v.size * v.dtype.itemsize for v in (*inputs, *outputs))
    vmem = pl.BlockSpec(memory_space=pltpu.VMEM)
    return pl.pallas_call(
        body,
        out_shape=outputs,
        in_specs=[pl.BlockSpec(memory_space=pltpu.SMEM)] * len(scalars) + [vmem] * len(inputs),
        out_specs=[vmem] * len(outputs),
        compiler_params=pltpu.CompilerParams(vmem_limit_bytes=24 << 20),
        cost_estimate=pl.CostEstimate(flops=0, bytes_accessed=size, transcendentals=0),
        name=name,
    )(*(v.reshape(1) for v in scalars), *inputs)


def weight_kernel(mine_ref, theirs_ref, beside_ref, across_ref, out_ref):
    cols, depth = mine_ref.shape
    for row, refs in enumerate(((mine_ref, theirs_ref), (beside_ref, across_ref))):
        for col, ref in enumerate(refs):
            out_ref[row * cols : (row + 1) * cols, col * depth : (col + 1) * depth] = ref[...]


def pack_kernel(y_ref, xh_ref, left_ref, right_ref, *out_refs):
    rank, hidden = left_ref.shape[0], left_ref.shape[1] // (2 * RING)
    features = right_ref.shape[1] // (2 * RING)
    for step, out_ref in enumerate(out_refs):
        to = lax.rem(y_ref[0] + RING + away(step, xh_ref[0]), RING)
        for xl in range(2):
            at = pl.multiple_of((to * 2 + xl) * hidden, 128)
            out_ref[xl, :, :hidden] = left_ref[:, pl.ds(at, hidden)]
            at = pl.multiple_of((to * 2 + xl) * features, 128)
            out_ref[xl, :, hidden:] = right_ref[:, pl.ds(at, features)]


def give_kernel(xl_ref, *refs):
    arrived, (aside_ref, across_ref, apart_ref) = refs[:-3], refs[-3:]
    xl = xl_ref[0]
    for step, ref in enumerate(arrived):
        aside_ref[step] = ref[1 - xl]
        if step > 0:
            across_ref[step - 1] = ref[xl]
            apart_ref[step - 1] = ref[1 - xl]


def gather_kernel(c_ref, xl_ref, y_ref, xh_ref, *refs):
    arrived, refs = refs[:STEPS], refs[STEPS:]
    aside_ref, far_ref, across_ref, apart_ref, grad_ref, beside_ref, left_ref, sensed_ref, right_ref = refs
    hidden = left_ref.shape[-1]
    xl = xl_ref[0]
    for step, ref in enumerate(arrived):
        source = lax.rem(y_ref[0] + RING - away(step, xh_ref[0]), RING)
        found = [(source, xl, ref[xl]), (source, 1 - xl, (aside_ref[step] if step < STEPS - 1 else far_ref[...]))]
        if 0 < step < STEPS - 1:
            source = lax.rem(y_ref[0] + RING + away(step, xh_ref[0]), RING)
            found += [(source, xl, across_ref[step - 1]), (source, 1 - xl, apart_ref[step - 1])]
        for source, at, value in found:
            left_ref[source, at] = value[:, :hidden]
            right_ref[source, at] = value[:, hidden:]
    ring, _, rank, features = right_ref.shape
    total = jnp.zeros(sensed_ref.shape, jnp.float32)
    for core, ref in ((c_ref[0], grad_ref), (1 - c_ref[0], beside_ref)):
        at = pl.ds(pl.multiple_of(core * (features // 2), 128), features // 2)
        factor = right_ref[:, :, :, at].reshape(2 * ring * rank, features // 2)
        total += lax.dot_general(factor, ref[...], (((1,), (1,)), ((), ())), preferred_element_type=jnp.float32)
    sensed_ref[...] = total.astype(sensed_ref.dtype)


def in_order(own, other, index, dim):
    return jnp.concatenate([jnp.where(index == 0, own, other), jnp.where(index == 0, other, own)], axis=dim)


def on_device(residual, norm_gain, gate_weight, up_weight, out_grad, left_factor, right_factor):
    c, xh, xl, y = (lax.axis_index(name) for name in ("c", "xh", "xl", "y"))
    peers, chips = lax.axis_size("z"), lax.axis_size(CHIPS)
    tokens = residual.shape[0]
    cols = gate_weight.shape[1]
    rank = left_factor.shape[1]
    hidden, features = left_factor.shape[2] // chips, right_factor.shape[2] // chips
    packed = hidden + features
    always = c >= 0

    def fenced(work, *inputs):
        shapes = jax.eval_shape(work, *inputs)
        return lax.cond(always, work, lambda *_: jax.tree.map(lambda s: jnp.zeros(s.shape, s.dtype), shapes), *inputs)

    def like(*shape):
        return jax.ShapeDtypeStruct(shape, jnp.bfloat16)

    def along_y(piece, step):
        pairs = [(i * 2 + h, (i + RING + away(step, h)) % RING * 2 + h) for i in range(RING) for h in range(2)]
        return lax.ppermute(piece, ("y", "xh"), pairs)

    def beside_tokens(gate_weight, up_weight, out_grad, left_factor, right_factor):
        mine = jnp.concatenate([gate_weight.T, up_weight.T], axis=0)
        theirs = lax.ppermute(mine, "xh", SWAP)
        pieces = whole_kernel(
            pack_kernel, (y, xh), (left_factor[0], right_factor[0]), [like(2, rank, packed)] * STEPS, "pack_factors"
        )
        early = tuple(along_y(pieces[step], step) for step in EARLY)
        theirs, early = lax.optimization_barrier((theirs, early))
        beside = (lax.ppermute(mine, "c", SWAP), lax.ppermute(theirs, "c", SWAP))
        (weight,) = whole_kernel(
            weight_kernel, (), (mine, theirs, *beside), [like(4 * cols, 2 * gate_weight.shape[0])], "weights"
        )
        late = (pieces[0], pieces[STEPS - 1])
        return weight, early, late, lax.ppermute(out_grad, "c", SWAP)

    def beside_sums(early, late, out_grad, beside_grad):
        far = along_y(late[1], STEPS - 1)
        near = [late[0]] + [early[EARLY.index(step)] for step in range(1, STEPS - 1)]
        pieces = [like(STEPS - 1, rank, packed)] + [like(STEPS - 2, rank, packed)] * 2
        aside, across, apart = whole_kernel(give_kernel, (xl,), near, pieces, "give")
        across = lax.ppermute(across, "xh", SWAP)
        apart = lax.ppermute(apart, ("xl", "xh"), [(i, 3 - i) for i in range(4)])
        aside = lax.ppermute(aside, "xl", SWAP)
        beyond = lax.ppermute(lax.dynamic_index_in_dim(far, 1 - xl, 0, keepdims=False), "xl", SWAP)
        outputs = [like(RING, 2, rank, hidden), like(chips * rank, tokens), like(RING, 2, rank, features)]
        inputs = (*near, far, aside, beyond, across, apart, out_grad, beside_grad)
        left, sensed, _ = whole_kernel(gather_kernel, (c, xl, y, xh), inputs, outputs, "gather_factors")
        return left.reshape(chips * rank, hidden), sensed

    normed = normed_by_peer(residual, norm_gain, c, xh, peers)
    inputs, normed = lax.optimization_barrier(((gate_weight, up_weight, out_grad, left_factor, right_factor), normed))
    rows = lax.all_to_all(normed, "z", 0, 0, tiled=True)
    weight, early, late, beside_grad = fenced(beside_tokens, *inputs)

    term = terms_of(rows, weight)
    inputs, term = lax.optimization_barrier(((early, late, out_grad, beside_grad), term))
    summed = lax.all_to_all(term, "z", 0, 0, tiled=True)
    factors, sensed = fenced(beside_sums, *inputs)

    summed = jnp.sum(summed.astype(jnp.float32), axis=0)
    active = [
        (jax.nn.silu(summed[:, at : at + cols]) * summed[:, at + cols : at + 2 * cols]).astype(jnp.bfloat16)
        for at in (0, 2 * cols)
    ]
    active = in_order(*active, c, 1)
    active, factors, sensed = lax.optimization_barrier((active, factors, sensed))
    active = in_order(active, lax.ppermute(active, "c", SWAP), c, 0)
    projected = lax.dot_general(factors, active, (((1,), (1,)), ((), ())), preferred_element_type=jnp.float32)

    parts = [v.reshape(chips, rank, tokens) for v in (projected.astype(jnp.bfloat16), sensed)]
    parts = lax.all_to_all(jnp.concatenate(parts, axis=1), CHIPS, 0, 0, tiled=True)
    whole = jnp.sum(parts.astype(jnp.float32), axis=0)
    return jnp.sum(whole[:rank] * whole[rank:], axis=0, keepdims=True)


def solution(mesh):
    torus = Mesh(mesh.devices.reshape(8, 2, 2, 8, 2), ("y", "xl", "xh", "z", "c"))
    placed = (
        P(TRAIN, None),
        P(),
        P(TRAIN, QM),
        P(TRAIN, QM),
        P(TRAIN, QM),
        P(QM, None, None),
        P(QM, None, None),
    )
    return jax.shard_map(on_device, mesh=torus, in_specs=placed, out_specs=P(QM, TRAIN), check_vma=False)
```

time: 145 us -> 131 us (0.903)
  starting transfers between devices: 38.2 us -> 64.7 us
  waiting for transfers between devices: 45 us -> 31.5 us
  between operations: 13.6 us -> 0.1 us
  Pallas kernels: 2.07 us -> 13.5 us
  matrix products: 9.3 us -> 0.41 us
  blocking collectives: 23.6 us -> 16.4 us
  other arithmetic: 8.28 us -> 3.75 us
  local copies, waits for them, and re-layouts: 4.17 us -> 0.03 us
    ppermute x4 -> x13, starting transfers between devices: 21.1 us -> 47 us  [the longest x4 17.3 us: along_y(): return lax.ppermute(piece, ('y', 'xh'), pairs)]
    ppermute x4 -> x13, waiting for transfers between devices: 3.9 us -> 20.4 us  [the longest x4 7.58 us: along_y(): return lax.ppermute(piece, ('y', 'xh'), pairs)]
    all_to_all x1, waiting for transfers between devices: 16.2 us -> 0.01 us  [on_device(): rows = lax.all_to_all(normed, 'z', 0, 0, tiled=True)]
    all_to_all x1, waiting for transfers between devices: 22.6 us -> 11.1 us  [on_device(): summed = lax.all_to_all(term, 'z', 0, 0, tiled=True)]
    pallas_call x0 -> x5, Pallas kernels: none -> 11 us  [the longest x1 5.67 us: terms_of(): pl.pallas_call(term_kernel, out_shape=jax.ShapeDtypeStruct((peers, half,...]
    dot_general x3 -> x1, matrix products: 9.3 us -> 0.41 us  [on_device(): lax.dot_general(factors, active, (((1,), (1,)), ((), ())), preferred_elem...]
    all_to_all x1, blocking collectives: 23.6 us -> 16.4 us  [on_device(): lax.all_to_all(jnp.concatenate(parts, axis=1), CHIPS, 0, 0, tiled=True)]
    select_n x3, other arithmetic: 3.58 us -> 0.18 us  [the longest x2 0.17 us: in_order(): jnp.where(index == 0, own, other)]
  transfers between devices with their start and end apart: 7 -> 15, of which waited for: 5 -> 6; matrix products, arithmetic and copies ran while one was open for 11% -> 1% of each run, Pallas kernels for 1% -> 4%
where the time goes in v2:
time: 131 us; the launch traced here: 130 us
  starting transfers between devices  64.7 us (49%)
  waiting for transfers between devices  31.5 us (24%)
  blocking collectives  16.4 us (13%)
  Pallas kernels  13.5 us (10%)
  other arithmetic  3.75 us (3%)
    ppermute x4, starting transfers between devices, along_y(): return lax.ppermute(piece, ('y', 'xh'), pairs)  17.3 us
    all_to_all x1, blocking collectives, on_device(): lax.all_to_all(jnp.concatenate(parts, axis=1), CHIPS, 0, 0, tiled=True)  16.4 us
    all_to_all x1, waiting for transfers between devices, on_device(): summed = lax.all_to_all(term, 'z', 0, 0, tiled=True)  11.1 us
    all_to_all x1, starting transfers between devices, on_device(): rows = lax.all_to_all(normed, 'z', 0, 0, tiled=True)  11 us
    ppermute x4, waiting for transfers between devices, along_y(): return lax.ppermute(piece, ('y', 'xh'), pairs)  7.58 us
    ppermute x1, waiting for transfers between devices, beside_sums(): across = lax.ppermute(across, 'xh', SWAP)  6.87 us
    all_to_all x1, starting transfers between devices, on_device(): summed = lax.all_to_all(term, 'z', 0, 0, tiled=True)  6.64 us
    ppermute x2, starting transfers between devices, beside_tokens(): beside = (lax.ppermute(mine, 'c', SWAP), lax.ppermute(theirs, 'c', SWAP))  6.38 us
  transfers between devices with their start and end apart: 15, of which 6 were waited for; matrix products, arithmetic and copies ran while one was open for 1% of the time, Pallas kernels for 4%

profile of v2, /device:TPU:1, one launch (start us, length us, event | category | flops | bytes accessed | tf_op | source)
XLA Modules:
  0.0 130.4 jit_solution(10304554702615795729)
XLA Ops:
  0.0 2.5 %norm_rows.1 = bf16[8,64,1024]{2,1,0:T(8,128)(2,1)} custom-call(s32[1]{0:T(128)} %bitcast.12.core_ref, s32[1]{0:T(128)} %bitcast.13.pair_ref, bf16[128,8192]{1,0:T(8,128)(2,1)} %other_ref.1, bf16[128,8192]{1,0:T(8,128)(2,1)} %other_ref.1, f32[1,8192]{1,0:T(1,128)} %bitcast.26, f32[1,8192]{1,0:T(1,128)} %bitcast.27), custom_call_target="tpu_custom_call" | custom-call | flops 2097152 | bytes 2097152 | tf_op jit(solution)/shard_map/norm_rows/pallas_call | solution.py:44
  2.5 11.0 %all-to-all-start = ((bf16[8,64,1024]{2,1,0:T(8,128)(2,1)}), bf16[8,64,1024]{2,1,0:T(8,128)(2,1)S(1)}, u32[]{:S(2)}, u32[]{:S(2)}) async-start(bf16[8,64,1024]{2,1,0:T(8,128)(2,1)} %norm_rows.1), calls=%async_computation | async-start | bytes 2097152 | tf_op jit(solution)/shard_map/all_to_all | solution.py:210
  13.5 35.6 %conditional.2 = (bf16[1792,1024]{1,0:T(8,128)(2,1)}, bf16[2,32,1408]{2,1,0:T(8,128)(2,1)}, bf16[2,32,1408]{2,1,0:T(8,128)(2,1)}, bf16[2,32,1408]{2,1,0:T(8,128)...) conditional(s32[]{:T(128)} %convert_element_type.19, () %tuple.25, ...), branch_computations={%region_0.0_spmd, %region_1.0_spmd} | conditional | flops 1835008 | bytes 24953168 | solution.py:170
  13.6 1.1 pad_maximum_fusion.mine_ref
  14.6 4.7 %collective-permute-start = (bf16[896,512]{1,0:T(8,128)(2,1)S(1)}, bf16[896,512]{1,0:T(8,128)(2,1)S(1)}, u32[]{:S(2)}, u32[]{:S(2)}) collective-permute-start(bf16[896,512]{1,0:T(8,128)(2,1)S(1)} %pad_maximum_fusion.mine_ref), channel_id=1, source_target_pairs={{0,16},{16,0},{1,17},{17,1},{2,18},{18,2},{3,19},{19,3},{4,20},{20... | collective-permute-start | bytes 2752520 | tf_op jit(solution)/shard_map/cond/branch_1_fun/ppermute | solution.py:181
  19.4 5.2 %collective-permute-start.1 = (bf16[2,32,1408]{2,1,0:T(8,128)(2,1)S(1)}, bf16[2,32,1408]{2,1,0:T(8,128)(2,1)}, u32[]{:S(2)}, u32[]{:S(2)}) collective-permute-start(bf16[2,32,1408]{2,1,0:T(8,128)(2,1)S(1)} %get-tuple-element.47), channel_id=1, source_target_pairs={{0,192},{16,336},{64,256},{80,400},{128,320},{144,464},{192,384},{... | collective-permute-start | bytes 540680 | tf_op jit(solution)/shard_map/cond/branch_1_fun/ppermute | solution.py:177
  24.6 3.2 %collective-permute-start.2 = (bf16[2,32,1408]{2,1,0:T(8,128)(2,1)S(1)}, bf16[2,32,1408]{2,1,0:T(8,128)(2,1)}, u32[]{:S(2)}, u32[]{:S(2)}) collective-permute-start(bf16[2,32,1408]{2,1,0:T(8,128)(2,1)S(1)} %get-tuple-element.48), channel_id=1, source_target_pairs={{0,384},{16,144},{64,448},{80,208},{128,0},{144,272},{192,64},{208... | collective-permute-start | bytes 540680 | tf_op jit(solution)/shard_map/cond/branch_1_fun/ppermute | solution.py:177
  27.8 3.2 %collective-permute-start.3 = (bf16[2,32,1408]{2,1,0:T(8,128)(2,1)S(1)}, bf16[2,32,1408]{2,1,0:T(8,128)(2,1)}, u32[]{:S(2)}, u32[]{:S(2)}) collective-permute-start(bf16[2,32,1408]{2,1,0:T(8,128)(2,1)S(1)} %get-tuple-element.49), channel_id=1, source_target_pairs={{0,64},{16,464},{64,128},{80,16},{128,192},{144,80},{192,256},{208... | collective-permute-start | bytes 540680 | tf_op jit(solution)/shard_map/cond/branch_1_fun/ppermute | solution.py:177
  31.0 4.0 %collective-permute-start.4 = (bf16[896,512]{1,0:T(8,128)(2,1)S(1)}, bf16[896,512]{1,0:T(8,128)(2,1)S(1)}, u32[]{:S(2)}, u32[]{:S(2)}) collective-permute-start(bf16[896,512]{1,0:T(8,128)(2,1)S(1)} %pad_maximum_fusion.mine_ref), channel_id=1, source_target_pairs={{0,1},{1,0},{2,3},{3,2},{4,5},{5,4},{6,7},{7,6},{8,9},{9,8},{10,11... | collective-permute-start | bytes 2752520 | tf_op jit(solution)/shard_map/cond/branch_1_fun/ppermute | solution.py:187
  35.0 7.6 %collective-permute-done.3 = bf16[2,32,1408]{2,1,0:T(8,128)(2,1)} collective-permute-done((bf16[2,32,1408]{2,1,0:T(8,128)(2,1)S(1)}, bf16[2,32,1408]{2,1,0:T(8,128)(2,1)}, u32[]{:S(2)}, u32[]{:S(2)}) %collective-permute-start.3) | collective-permute-done | bytes 180256 | tf_op jit(solution)/shard_map/cond/branch_1_fun/ppermute | solution.py:177
  42.6 2.4 %collective-permute-start.5 = (bf16[896,512]{1,0:T(8,128)(2,1)S(1)}, bf16[896,512]{1,0:T(8,128)(2,1)S(1)}, u32[]{:S(2)}, u32[]{:S(2)}) collective-permute-start(bf16[896,512]{1,0:T(8,128)(2,1)S(1)} %collective-permute-done.theirs_ref), channel_id=1, source_target_pairs={{0,1},{1,0},{2,3},{3,2},{4,5},{5,4},{6,7},{7,6},{8,9},{9,8},{10,11... | collective-permute-start | bytes 2752520 | tf_op jit(solution)/shard_map/cond/branch_1_fun/ppermute | solution.py:187
  45.0 1.9 %collective-permute-start.6 = (bf16[128,256]{1,0:T(8,128)(2,1)S(1)}, bf16[128,256]{1,0:T(8,128)(2,1)}, u32[]{:S(2)}, u32[]{:S(2)}) collective-permute-start(bf16[128,256]{1,0:T(8,128)(2,1)S(1)} %get-tuple-element.56), channel_id=1, source_target_pairs={{0,1},{1,0},{2,3},{3,2},{4,5},{5,4},{6,7},{7,6},{8,9},{9,8},{10,11... | collective-permute-start | bytes 196616 | tf_op jit(solution)/shard_map/cond/branch_1_fun/ppermute | solution.py:192
  47.1 2.1 %weights.1 = bf16[1792,1024]{1,0:T(8,128)(2,1)} custom-call(bf16[896,512]{1,0:T(8,128)(2,1)S(1)} %pad_maximum_fusion.mine_ref, bf16[896,512]{1,0:T(8,128)(2,1)S(1)} %collective-permute-done.theirs_ref, bf16[896,512]{1,0:T(8,128)(2,1)S(1)} %collective-permute-done.4.beside_ref, bf16[896,512]{1,0:T(8,128)(2,1)S(1)} %collective-permute-done.5.across_ref), custom_call_target="tpu_custom_call" | custom-call | bytes 7340032 | tf_op jit(solution)/shard_map/cond/branch_1_fun/weights/pallas_call | solution.py:91
  49.2 5.7 %terms.1 = bf16[8,64,1792]{2,1,0:T(8,128)(2,1)} custom-call(bf16[8,64,1024]{2,1,0:T(8,128)(2,1)S(1)} %all-to-all-done.rows_ref, bf16[1792,1024]{1,0:T(8,128)(2,1)} %get-tuple-element.111.weight_ref), custom_call_target="tpu_custom_call" | custom-call | flops 1879048192 | bytes 6815744 | tf_op jit(solution)/shard_map/terms/pallas_call | solution.py:77
  54.8 6.6 %all-to-all-start.1 = ((bf16[8,64,1792]{2,1,0:T(8,128)(2,1)}), bf16[8,64,1792]{2,1,0:T(8,128)(2,1)}, u32[]{:S(2)}, u32[]{:S(2)}) async-start(bf16[8,64,1792]{2,1,0:T(8,128)(2,1)} %terms.1), calls=%async_computation.1 | async-start | bytes 3670016 | tf_op jit(solution)/shard_map/all_to_all | solution.py:215
  61.5 32.2 %conditional.3 = (bf16[512,896]{1,0:T(8,128)(2,1)S(1)}, bf16[512,128]{1,0:T(8,128)(2,1)S(1)}) conditional(s32[]{:T(128)} %convert_element_type.19, () %tuple.29, (s32[]{:T(128)}, s32[]{:T(128)}, s32[]{:T(128)}, s32[]{:T(128)}, bf16[2,32,1408]{2,1,0:T(8,128)(2,1)S(1)}, /*index=5*/bf16[2,32,1408]{2,1,0:T(8,128)(2,1)S(1)}, ...), branch_computations={%region_3.4_spmd, %region_4.5_spmd} | conditional | flops 4 | bytes 10084618 | solution.py:170
  61.5 5.7 %collective-permute-start.7 = (bf16[2,32,1408]{2,1,0:T(8,128)(2,1)S(1)}, bf16[2,32,1408]{2,1,0:T(8,128)(2,1)S(1)}, u32[]{:S(2)}, u32[]{:S(2)}) collective-permute-start(bf16[2,32,1408]{2,1,0:T(8,128)(2,1)S(1)} %get-tuple-element.65), channel_id=1, source_target_pairs={{0,256},{16,272},{64,320},{80,336},{128,384},{144,400},{192,448},{... | collective-permute-start | bytes 540680 | tf_op jit(solution)/shard_map/cond/branch_1_fun/ppermute | solution.py:177
  67.2 1.2 give.1
  68.4 2.5 %collective-permute-start.8 = (bf16[4,32,1408]{2,1,0:T(8,128)(2,1)S(1)}, bf16[4,32,1408]{2,1,0:T(8,128)(2,1)S(1)}, u32[]{:S(2)}, u32[]{:S(2)}) collective-permute-start(bf16[4,32,1408]{2,1,0:T(8,128)(2,1)S(1)} %get-tuple-element.66), channel_id=1, source_target_pairs={{0,32},{32,0},{1,33},{33,1},{2,34},{34,2},{3,35},{35,3},{4,36},{36... | collective-permute-start | bytes 1081352 | tf_op jit(solution)/shard_map/cond/branch_1_fun/ppermute | solution.py:201
  70.9 4.4 %collective-permute-start.10 = (bf16[3,32,1408]{2,1,0:T(8,128)(2,1)S(1)}, bf16[3,32,1408]{2,1,0:T(8,128)(2,1)S(1)}, u32[]{:S(2)}, u32[]{:S(2)}) collective-permute-start(bf16[3,32,1408]{2,1,0:T(8,128)(2,1)S(1)} %get-tuple-element.67), channel_id=1, source_target_pairs={{0,16},{16,0},{1,17},{17,1},{2,18},{18,2},{3,19},{19,3},{4,20},{20... | collective-permute-start | bytes 811016 | tf_op jit(solution)/shard_map/cond/branch_1_fun/ppermute | solution.py:199
  75.3 2.7 %collective-permute-start.11 = (bf16[3,32,1408]{2,1,0:T(8,128)(2,1)S(1)}, bf16[3,32,1408]{2,1,0:T(8,128)(2,1)S(1)}, u32[]{:S(2)}, u32[]{:S(2)}) collective-permute-start(bf16[3,32,1408]{2,1,0:T(8,128)(2,1)S(1)} %get-tuple-element.68), channel_id=1, source_target_pairs={{0,48},{16,32},{32,16},{48,0},{1,49},{17,33},{33,17},{49,1},{2,50}... | collective-permute-start | bytes 811016 | tf_op jit(solution)/shard_map/cond/branch_1_fun/ppermute | solution.py:200
  78.0 1.9 %collective-permute-start.9 = (bf16[32,1408]{1,0:T(8,128)(2,1)S(1)}, bf16[32,1408]{1,0:T(8,128)(2,1)S(1)}, u32[]{:S(2)}, u32[]{:S(2)}) collective-permute-start(bf16[32,1408]{1,0:T(8,128)(2,1)S(1)} %dynamic-slice_bitcast_fusion), channel_id=1, source_target_pairs={{0,32},{32,0},{1,33},{33,1},{2,34},{34,2},{3,35},{35,3},{4,36},{36... | collective-permute-start | bytes 270344 | tf_op jit(solution)/shard_map/cond/branch_1_fun/ppermute | solution.py:202
  79.9 6.9 %collective-permute-done.10.refs_7_ = bf16[3,32,1408]{2,1,0:T(8,128)(2,1)S(1)} collective-permute-done((bf16[3,32,1408]{2,1,0:T(8,128)(2,1)S(1)}, bf16[3,32,1408]{2,1,0:T(8,128)(2,1)S(1)}, u32[]{:S(2)}, u32[]{:S(2)}) %collective-permute-start.10) | collective-permute-done | bytes 270368 | tf_op jit(solution)/shard_map/cond/branch_1_fun/ppermute | solution.py:199
  86.8 4.8 %collective-permute-done.11.refs_8_ = bf16[3,32,1408]{2,1,0:T(8,128)(2,1)S(1)} collective-permute-done((bf16[3,32,1408]{2,1,0:T(8,128)(2,1)S(1)}, bf16[3,32,1408]{2,1,0:T(8,128)(2,1)S(1)}, u32[]{:S(2)}, u32[]{:S(2)}) %collective-permute-start.11) | collective-permute-done | bytes 270368 | tf_op jit(solution)/shard_map/cond/branch_1_fun/ppermute | solution.py:200
  91.6 2.0 %gather_factors.1 = (bf16[8,2,32,896]{3,2,1,0:T(8,128)(2,1)S(1)}, bf16[512,128]{1,0:T(8,128)(2,1)S(1)}, bf16[8,2,32,512]{3,2,1,0:T(8,128)(2,1)}) custom-call(s32[1]{0:T(128)} %bitcast.6.c_ref, s32[1]{0:T(128)} %bitcast.7.xl_ref, s32[1]{0:T(128)} %bitcast.8.y_ref, s32[1]{0:T(128)} %bitcast.9.xh_ref, bf16[2,32,1408]{2,1,0:T(8,128)(2,1)S(1)} %get-tuple-element.61.refs_0_, ...), custom_call_target="tpu_custom_call" | custom-call | bytes 3596288 | tf_op jit(solution)/shard_map/cond/branch_1_fun/gather_factors/pallas_call | solution.py:91
  93.7 11.1 %all-to-all-done.1 = bf16[8,64,1792]{2,1,0:T(8,128)(2,1)} async-done(((bf16[8,64,1792]{2,1,0:T(8,128)(2,1)}), bf16[8,64,1792]{2,1,0:T(8,128)(2,1)}, u32[]{:S(2)}, u32[]{:S(2)}) %all-to-all-start.1) | async-done | bytes 1835040 | tf_op jit(solution)/shard_map/all_to_all | solution.py:215
  104.8 1.8 %convert_reduce_fusion = f32[64,1792]{1,0:T(8,128)S(1)} fusion(bf16[8,64,1792]{2,1,0:T(8,128)(2,1)} %all-to-all-done.1), kind=kLoop, calls=%fused_computation.2 | loop fusion | flops 1720320 | bytes 2293760 | tf_op jit(solution)/shard_map/reduce_sum | solution.py:218
  106.8 5.3 %collective-permute-start.12 = (bf16[64,896]{1,0:T(8,128)(2,1)S(1)}, bf16[64,896]{1,0:T(8,128)(2,1)S(1)}, u32[]{:S(2)}, u32[]{:S(2)}) collective-permute-start(bf16[64,896]{1,0:T(8,128)(2,1)S(1)} %pad_maximum_fusion.2), channel_id=1, source_target_pairs={{0,1},{1,0},{2,3},{3,2},{4,5},{5,4},{6,7},{7,6},{8,9},{9,8},{10,11... | collective-permute-start | bytes 344072 | tf_op jit(solution)/shard_map/ppermute | solution.py:225
  112.1 0.9 collective-permute-done.12
  113.1 0.4 convolution_convert_fusion
  113.5 16.4 %all_to_all.15 = bf16[16,64,128]{2,1,0:T(8,128)(2,1)S(1)} all-to-all(bf16[16,64,128]{2,1,0:T(8,128)(2,1)S(1)} %pad_maximum_fusion.1), channel_id=1, replica_groups=mesh['y'=8,'xl'=2,'xh'=2,'z'=8,'c'=2] {'y','xl'}, dimensions={0} | all-to-all | bytes 524288 | tf_op jit(solution)/shard_map/all_to_all | solution.py:229
  129.9 0.5 fusion.5
  (26 shorter events, 0.6 us)
Async XLA Ops:
  2.5 11.0 %copy-start = (bf16[1,32,14336]{2,1,0:T(8,128)(2,1)S(1)}, bf16[1,32,14336]{2,1,0:T(8,128)(2,1)}, u32[]{:S(2)}) copy-start(bf16[1,32,14336]{2,1,0:T(8,128)(2,1)} %param.16) | copy-start | bytes 2752516
  2.5 11.0 %copy-start.1 = (bf16[1,32,8192]{2,1,0:T(8,128)(2,1)S(1)}, bf16[1,32,8192]{2,1,0:T(8,128)(2,1)}, u32[]{:S(2)}) copy-start(bf16[1,32,8192]{2,1,0:T(8,128)(2,1)} %param.17) | copy-start | bytes 1572868
  2.5 11.0 %copy-start.2 = (bf16[512,448]{0,1:T(8,128)(2,1)S(1)}, bf16[512,448]{0,1:T(8,128)(2,1)}, u32[]{:S(2)}) copy-start(bf16[512,448]{0,1:T(8,128)(2,1)} %param.13) | copy-start | bytes 1376260
  2.5 11.0 %copy-start.3 = (bf16[128,256]{1,0:T(8,128)(2,1)S(1)}, bf16[128,256]{1,0:T(8,128)(2,1)}, u32[]{:S(2)}) copy-start(bf16[128,256]{1,0:T(8,128)(2,1)} %param.15) | copy-start | bytes 196612
  2.5 46.7 %all-to-all-start = ((bf16[8,64,1024]{2,1,0:T(8,128)(2,1)}), bf16[8,64,1024]{2,1,0:T(8,128)(2,1)S(1)}, u32[]{:S(2)}, u32[]{:S(2)}) async-start(bf16[8,64,1024]{2,1,0:T(8,128)(2,1)} %norm_rows.1), calls=%async_computation | async-start | bytes 2097152 | tf_op jit(solution)/shard_map/all_to_all | solution.py:210
  14.6 28.0 %collective-permute-start = (bf16[896,512]{1,0:T(8,128)(2,1)S(1)}, bf16[896,512]{1,0:T(8,128)(2,1)S(1)}, u32[]{:S(2)}, u32[]{:S(2)}) collective-permute-start(bf16[896,512]{1,0:T(8,128)(2,1)S(1)} %pad_maximum_fusion.mine_ref), channel_id=1, source_target_pairs={{0,16},{16,0},{1,17},{17,1},{2,18},{18,2},{3,19},{19,3},{4,20},{20... | collective-permute-start | bytes 2752520 | tf_op jit(solution)/shard_map/cond/branch_1_fun/ppermute | solution.py:181
  19.4 15.6 %collective-permute-start.1 = (bf16[2,32,1408]{2,1,0:T(8,128)(2,1)S(1)}, bf16[2,32,1408]{2,1,0:T(8,128)(2,1)}, u32[]{:S(2)}, u32[]{:S(2)}) collective-permute-start(bf16[2,32,1408]{2,1,0:T(8,128)(2,1)S(1)} %get-tuple-element.47), channel_id=1, source_target_pairs={{0,192},{16,336},{64,256},{80,400},{128,320},{144,464},{192,384},{... | collective-permute-start | bytes 540680 | tf_op jit(solution)/shard_map/cond/branch_1_fun/ppermute | solution.py:177
  24.6 10.4 %collective-permute-start.2 = (bf16[2,32,1408]{2,1,0:T(8,128)(2,1)S(1)}, bf16[2,32,1408]{2,1,0:T(8,128)(2,1)}, u32[]{:S(2)}, u32[]{:S(2)}) collective-permute-start(bf16[2,32,1408]{2,1,0:T(8,128)(2,1)S(1)} %get-tuple-element.48), channel_id=1, source_target_pairs={{0,384},{16,144},{64,448},{80,208},{128,0},{144,272},{192,64},{208... | collective-permute-start | bytes 540680 | tf_op jit(solution)/shard_map/cond/branch_1_fun/ppermute | solution.py:177
  27.8 14.8 %collective-permute-start.3 = (bf16[2,32,1408]{2,1,0:T(8,128)(2,1)S(1)}, bf16[2,32,1408]{2,1,0:T(8,128)(2,1)}, u32[]{:S(2)}, u32[]{:S(2)}) collective-permute-start(bf16[2,32,1408]{2,1,0:T(8,128)(2,1)S(1)} %get-tuple-element.49), channel_id=1, source_target_pairs={{0,64},{16,464},{64,128},{80,16},{128,192},{144,80},{192,256},{208... | collective-permute-start | bytes 540680 | tf_op jit(solution)/shard_map/cond/branch_1_fun/ppermute | solution.py:177
  31.0 15.9 %collective-permute-start.4 = (bf16[896,512]{1,0:T(8,128)(2,1)S(1)}, bf16[896,512]{1,0:T(8,128)(2,1)S(1)}, u32[]{:S(2)}, u32[]{:S(2)}) collective-permute-start(bf16[896,512]{1,0:T(8,128)(2,1)S(1)} %pad_maximum_fusion.mine_ref), channel_id=1, source_target_pairs={{0,1},{1,0},{2,3},{3,2},{4,5},{5,4},{6,7},{7,6},{8,9},{9,8},{10,11... | collective-permute-start | bytes 2752520 | tf_op jit(solution)/shard_map/cond/branch_1_fun/ppermute | solution.py:187
  42.6 4.5 %collective-permute-start.5 = (bf16[896,512]{1,0:T(8,128)(2,1)S(1)}, bf16[896,512]{1,0:T(8,128)(2,1)S(1)}, u32[]{:S(2)}, u32[]{:S(2)}) collective-permute-start(bf16[896,512]{1,0:T(8,128)(2,1)S(1)} %collective-permute-done.theirs_ref), channel_id=1, source_target_pairs={{0,1},{1,0},{2,3},{3,2},{4,5},{5,4},{6,7},{7,6},{8,9},{9,8},{10,11... | collective-permute-start | bytes 2752520 | tf_op jit(solution)/shard_map/cond/branch_1_fun/ppermute | solution.py:187
  45.0 4.1 %collective-permute-start.6 = (bf16[128,256]{1,0:T(8,128)(2,1)S(1)}, bf16[128,256]{1,0:T(8,128)(2,1)}, u32[]{:S(2)}, u32[]{:S(2)}) collective-permute-start(bf16[128,256]{1,0:T(8,128)(2,1)S(1)} %get-tuple-element.56), channel_id=1, source_target_pairs={{0,1},{1,0},{2,3},{3,2},{4,5},{5,4},{6,7},{7,6},{8,9},{9,8},{10,11... | collective-permute-start | bytes 196616 | tf_op jit(solution)/shard_map/cond/branch_1_fun/ppermute | solution.py:192
  54.8 49.9 %all-to-all-start.1 = ((bf16[8,64,1792]{2,1,0:T(8,128)(2,1)}), bf16[8,64,1792]{2,1,0:T(8,128)(2,1)}, u32[]{:S(2)}, u32[]{:S(2)}) async-start(bf16[8,64,1792]{2,1,0:T(8,128)(2,1)} %terms.1), calls=%async_computation.1 | async-start | bytes 3670016 | tf_op jit(solution)/shard_map/all_to_all | solution.py:215
  61.5 16.5 %collective-permute-start.7 = (bf16[2,32,1408]{2,1,0:T(8,128)(2,1)S(1)}, bf16[2,32,1408]{2,1,0:T(8,128)(2,1)S(1)}, u32[]{:S(2)}, u32[]{:S(2)}) collective-permute-start(bf16[2,32,1408]{2,1,0:T(8,128)(2,1)S(1)} %get-tuple-element.65), channel_id=1, source_target_pairs={{0,256},{16,272},{64,320},{80,336},{128,384},{144,400},{192,448},{... | collective-permute-start | bytes 540680 | tf_op jit(solution)/shard_map/cond/branch_1_fun/ppermute | solution.py:177
  68.4 23.3 %collective-permute-start.8 = (bf16[4,32,1408]{2,1,0:T(8,128)(2,1)S(1)}, bf16[4,32,1408]{2,1,0:T(8,128)(2,1)S(1)}, u32[]{:S(2)}, u32[]{:S(2)}) collective-permute-start(bf16[4,32,1408]{2,1,0:T(8,128)(2,1)S(1)} %get-tuple-element.66), channel_id=1, source_target_pairs={{0,32},{32,0},{1,33},{33,1},{2,34},{34,2},{3,35},{35,3},{4,36},{36... | collective-permute-start | bytes 1081352 | tf_op jit(solution)/shard_map/cond/branch_1_fun/ppermute | solution.py:201
  70.9 15.9 %collective-permute-start.10 = (bf16[3,32,1408]{2,1,0:T(8,128)(2,1)S(1)}, bf16[3,32,1408]{2,1,0:T(8,128)(2,1)S(1)}, u32[]{:S(2)}, u32[]{:S(2)}) collective-permute-start(bf16[3,32,1408]{2,1,0:T(8,128)(2,1)S(1)} %get-tuple-element.67), channel_id=1, source_target_pairs={{0,16},{16,0},{1,17},{17,1},{2,18},{18,2},{3,19},{19,3},{4,20},{20... | collective-permute-start | bytes 811016 | tf_op jit(solution)/shard_map/cond/branch_1_fun/ppermute | solution.py:199
  75.3 16.3 %collective-permute-start.11 = (bf16[3,32,1408]{2,1,0:T(8,128)(2,1)S(1)}, bf16[3,32,1408]{2,1,0:T(8,128)(2,1)S(1)}, u32[]{:S(2)}, u32[]{:S(2)}) collective-permute-start(bf16[3,32,1408]{2,1,0:T(8,128)(2,1)S(1)} %get-tuple-element.68), channel_id=1, source_target_pairs={{0,48},{16,32},{32,16},{48,0},{1,49},{17,33},{33,17},{49,1},{2,50}... | collective-permute-start | bytes 811016 | tf_op jit(solution)/shard_map/cond/branch_1_fun/ppermute | solution.py:200
  78.0 13.6 %collective-permute-start.9 = (bf16[32,1408]{1,0:T(8,128)(2,1)S(1)}, bf16[32,1408]{1,0:T(8,128)(2,1)S(1)}, u32[]{:S(2)}, u32[]{:S(2)}) collective-permute-start(bf16[32,1408]{1,0:T(8,128)(2,1)S(1)} %dynamic-slice_bitcast_fusion), channel_id=1, source_target_pairs={{0,32},{32,0},{1,33},{33,1},{2,34},{34,2},{3,35},{35,3},{4,36},{36... | collective-permute-start | bytes 270344 | tf_op jit(solution)/shard_map/cond/branch_1_fun/ppermute | solution.py:202
  106.8 6.2 %collective-permute-start.12 = (bf16[64,896]{1,0:T(8,128)(2,1)S(1)}, bf16[64,896]{1,0:T(8,128)(2,1)S(1)}, u32[]{:S(2)}, u32[]{:S(2)}) collective-permute-start(bf16[64,896]{1,0:T(8,128)(2,1)S(1)} %pad_maximum_fusion.2), channel_id=1, source_target_pairs={{0,1},{1,0},{2,3},{3,2},{4,5},{5,4},{6,7},{7,6},{8,9},{9,8},{10,11... | collective-permute-start | bytes 344072 | tf_op jit(solution)/shard_map/ppermute | solution.py:225

commit v3 on v2

--- a/solution.py
+++ b/solution.py
@@ -6,7 +6,8 @@
 from jax.sharding import Mesh
 from jax.sharding import PartitionSpec as P
 
-TRAIN = ("xh", "z")
+TRAIN = ("xh", "zh", "zl")
+DEPTH = ("zh", "zl")
 QM = ("y", "xl", "c")
 CHIPS = ("y", "xl")
 SWAP = ((0, 1), (1, 0))
@@ -16,7 +17,7 @@
 
 
 def away(step, xh):
-    sign = 1 if step % 2 else -1
+    sign = 1 if step == 3 else -1
     return step if step in (0, RING // 2) else sign * step * (1 - 2 * xh)
 
 
@@ -61,31 +62,31 @@
     )(core.reshape(1), pair.reshape(1), residual, residual, gain, gain)
 
 
-def term_kernel(rows_ref, weight_ref, out_ref):
+def term_kernel(parity_ref, rows_ref, weight_ref, *out_refs):
     peers, half, width = rows_ref.shape
-    rows = rows_ref[...].reshape(peers * half, width)
+    rows = jnp.concatenate([rows_ref[2 * i + parity_ref[0]] for i in range(peers // 2)], axis=0)
     cols = weight_ref.shape[0] // 2
-    for core in range(2):
-        at = slice(core * cols, (core + 1) * cols)
-        total = lax.dot_general(rows, weight_ref[at], (((1,), (1,)), ((), ())), preferred_element_type=jnp.float32)
-        out_ref[:, :, at] = total.astype(out_ref.dtype).reshape(peers, half, cols)
-
-
-def terms_of(rows, weight):
+    for core, out_ref in enumerate(out_refs):
+        weight = weight_ref[core * cols : (core + 1) * cols]
+        total = lax.dot_general(rows, weight, (((1,), (1,)), ((), ())), preferred_element_type=jnp.float32)
+        out_ref[...] = total.astype(out_ref.dtype).reshape(out_ref.shape)
+
+
+def terms_of(rows, weight, parity, kind):
     peers, half, width = rows.shape
     cols = weight.shape[0]
-    return pl.pallas_call(
-        term_kernel,
-        out_shape=jax.ShapeDtypeStruct((peers, half, cols), jnp.bfloat16),
-        compiler_params=pltpu.CompilerParams(vmem_limit_bytes=24 << 20),
-        cost_estimate=pl.CostEstimate(
-            flops=2 * peers * half * width * cols, bytes_accessed=2 * cols * width + 6 * peers * half * width, transcendentals=0
-        ),
-        name="terms",
-    )(rows, weight)
-
-
-def whole_kernel(body, scalars, inputs, outputs, name):
+    shape = jax.ShapeDtypeStruct((peers // 2, half, cols // 2), kind)
+    return whole_kernel(term_kernel, (parity,), (rows, weight), [shape] * 2, "terms", peers * half * width * cols)
+
+
+def add_kernel(keep_ref, beside_ref, got_ref, across_ref, out_ref):
+    cols = keep_ref.shape[2]
+    for at, (own, other) in enumerate(((keep_ref, got_ref), (beside_ref, across_ref))):
+        total = own[...] + other[...].astype(jnp.float32)
+        out_ref[:, :, at * cols : (at + 1) * cols] = total.astype(out_ref.dtype)
+
+
+def whole_kernel(body, scalars, inputs, outputs, name, flops=0):
     size = sum(v.size * v.dtype.itemsize for v in (*inputs, *outputs))
     vmem = pl.BlockSpec(memory_space=pltpu.VMEM)
     return pl.pallas_call(
@@ -94,7 +95,7 @@
         in_specs=[pl.BlockSpec(memory_space=pltpu.SMEM)] * len(scalars) + [vmem] * len(inputs),
         out_specs=[vmem] * len(outputs),
         compiler_params=pltpu.CompilerParams(vmem_limit_bytes=24 << 20),
-        cost_estimate=pl.CostEstimate(flops=0, bytes_accessed=size, transcendentals=0),
+        cost_estimate=pl.CostEstimate(flops=flops, bytes_accessed=size, transcendentals=0),
         name=name,
     )(*(v.reshape(1) for v in scalars), *inputs)
 
@@ -156,8 +157,8 @@
 
 
 def on_device(residual, norm_gain, gate_weight, up_weight, out_grad, left_factor, right_factor):
-    c, xh, xl, y = (lax.axis_index(name) for name in ("c", "xh", "xl", "y"))
-    peers, chips = lax.axis_size("z"), lax.axis_size(CHIPS)
+    c, xh, xl, y, zl = (lax.axis_index(name) for name in ("c", "xh", "xl", "y", "zl"))
+    peers, chips = lax.axis_size(DEPTH), lax.axis_size(CHIPS)
     tokens = residual.shape[0]
     cols = gate_weight.shape[1]
     rank = left_factor.shape[1]
@@ -191,9 +192,7 @@
         late = (pieces[0], pieces[STEPS - 1])
         return weight, early, late, lax.ppermute(out_grad, "c", SWAP)
 
-    def beside_sums(early, late, out_grad, beside_grad):
-        far = along_y(late[1], STEPS - 1)
-        near = [late[0]] + [early[EARLY.index(step)] for step in range(1, STEPS - 1)]
+    def beside_sums(near, far, out_grad, beside_grad):
         pieces = [like(STEPS - 1, rank, packed)] + [like(STEPS - 2, rank, packed)] * 2
         aside, across, apart = whole_kernel(give_kernel, (xl,), near, pieces, "give")
         across = lax.ppermute(across, "xh", SWAP)
@@ -207,12 +206,20 @@
 
     normed = normed_by_peer(residual, norm_gain, c, xh, peers)
     inputs, normed = lax.optimization_barrier(((gate_weight, up_weight, out_grad, left_factor, right_factor), normed))
-    rows = lax.all_to_all(normed, "z", 0, 0, tiled=True)
+    rows = lax.all_to_all(normed, DEPTH, 0, 0, tiled=True)
     weight, early, late, beside_grad = fenced(beside_tokens, *inputs)
 
-    term = terms_of(rows, weight)
-    inputs, term = lax.optimization_barrier(((early, late, out_grad, beside_grad), term))
-    summed = lax.all_to_all(term, "z", 0, 0, tiled=True)
+    give = terms_of(rows, weight, 1 - zl, jnp.bfloat16)
+    give, rows = lax.optimization_barrier((give, rows))
+    got = lax.ppermute(give[0], "zl", SWAP)
+    across = lax.ppermute(give[1], DEPTH, [(i, (i + (1 if i % 2 else -1)) % peers) for i in range(peers)])
+    keep = terms_of(rows, weight, zl, jnp.float32)
+    late, give = lax.optimization_barrier((late, give))
+    far = along_y(late[1], STEPS - 1)
+    near = [late[0]] + [early[EARLY.index(step)] for step in range(1, STEPS - 1)]
+    (term,) = whole_kernel(add_kernel, (), (*keep, got, across), [like(peers // 2, tokens // 2, 4 * cols)], "add_terms")
+    inputs, term = lax.optimization_barrier(((near, far, out_grad, beside_grad), term))
+    summed = lax.all_to_all(term, "zh", 0, 0, tiled=True)
     factors, sensed = fenced(beside_sums, *inputs)
 
     summed = jnp.sum(summed.astype(jnp.float32), axis=0)
@@ -232,7 +239,7 @@
 
 
 def solution(mesh):
-    torus = Mesh(mesh.devices.reshape(8, 2, 2, 8, 2), ("y", "xl", "xh", "z", "c"))
+    torus = Mesh(mesh.devices.reshape(8, 2, 2, 4, 2, 2), ("y", "xl", "xh", "zh", "zl", "c"))
     placed = (
         P(TRAIN, None),
         P(),

time: 131 us -> 127 us (0.969)
  waiting for transfers between devices: 31.5 us -> 19.1 us
  starting transfers between devices: 64.7 us -> 68.7 us
  Pallas kernels: 13.5 us -> 15.9 us
  blocking collectives: 16.4 us -> 18.1 us
  other arithmetic: 3.75 us -> 2.07 us
    all_to_all x2, waiting for transfers between devices: 11.1 us -> 0.78 us  [the longest x1 0.78 us: on_device(): summed = lax.all_to_all(term, 'zh', 0, 0, tiled=True)]
    pallas_call x4 -> x7, Pallas kernels: 5.33 us -> 13.4 us  [whole_kernel(): pl.pallas_call(body, out_shape=outputs, in_specs=[pl.BlockSpec(memory_spa...]
    ppermute x0 -> x2, starting transfers between devices: none -> 7.62 us  [the longest x1 4.3 us: on_device(): lax.ppermute(give[1], DEPTH, [(i, (i + (1 if i % 2 else -1)) % peers) for...]
    ppermute x1, waiting for transfers between devices: 0.01 us -> 6.53 us  [beside_sums(): lax.ppermute(lax.dynamic_index_in_dim(far, 1 - xl, 0, keepdims=False), 'x...]
    ppermute x1, waiting for transfers between devices: 6.87 us -> 0.38 us  [beside_sums(): across = lax.ppermute(across, 'xh', SWAP)]
    pallas_call x1 -> x0, Pallas kernels: 5.67 us -> none  [terms_of(): pl.pallas_call(term_kernel, out_shape=jax.ShapeDtypeStruct((peers, half,...]
    ppermute x1, waiting for transfers between devices: 4.82 us -> 0.01 us  [beside_sums(): apart = lax.ppermute(apart, ('xl', 'xh'), [(i, 3 - i) for i in range(4)])]
    all_to_all x2, starting transfers between devices: 17.6 us -> 15.2 us  [the longest x1 11 us: on_device(): rows = lax.all_to_all(normed, DEPTH, 0, 0, tiled=True)]
  transfers between devices with their start and end apart: 15 -> 17, of which waited for: 6 -> 9; matrix products, arithmetic and copies ran while one was open for 1% -> 1% of each run, Pallas kernels for 4% -> 8%
where the time goes in v3:
time: 127 us; the launch traced here: 126 us
  starting transfers between devices  68.7 us (54%)
  waiting for transfers between devices  19.1 us (15%)
  blocking collectives  18.1 us (14%)
  Pallas kernels  15.9 us (13%)
  other arithmetic  2.07 us (2%)
  matrix products  1.58 us (1%)
    all_to_all x1, blocking collectives, on_device(): lax.all_to_all(jnp.concatenate(parts, axis=1), CHIPS, 0, 0, tiled=True)  18.1 us
    ppermute x4, starting transfers between devices, along_y(): return lax.ppermute(piece, ('y', 'xh'), pairs)  16.6 us
    pallas_call x7, Pallas kernels, whole_kernel(): pl.pallas_call(body, out_shape=outputs, in_specs=[pl.BlockSpec(memory_spa...  13.4 us
    all_to_all x1, starting transfers between devices, on_device(): rows = lax.all_to_all(normed, DEPTH, 0, 0, tiled=True)  11 us
    ppermute x4, waiting for transfers between devices, along_y(): return lax.ppermute(piece, ('y', 'xh'), pairs)  9.27 us
    ppermute x1, waiting for transfers between devices, beside_sums(): lax.ppermute(lax.dynamic_index_in_dim(far, 1 - xl, 0, keepdims=False), 'x...  6.53 us
    ppermute x2, starting transfers between devices, beside_tokens(): beside = (lax.ppermute(mine, 'c', SWAP), lax.ppermute(theirs, 'c', SWAP))  6.17 us
    ppermute x1, starting transfers between devices, beside_sums(): apart = lax.ppermute(apart, ('xl', 'xh'), [(i, 3 - i) for i in range(4)])  4.8 us
  transfers between devices with their start and end apart: 17, of which 9 were waited for; matrix products, arithmetic and copies ran while one was open for 1% of the time, Pallas kernels for 8%

profile of v3, /device:TPU:1, one launch (start us, length us, event | category | flops | bytes accessed | tf_op | source)
XLA Modules:
  0.0 125.7 jit_solution(5254883925209362360)
XLA Ops:
  0.0 2.5 %norm_rows.1 = bf16[8,64,1024]{2,1,0:T(8,128)(2,1)} custom-call(s32[1]{0:T(128)} %bitcast.12.core_ref, s32[1]{0:T(128)} %bitcast.13.pair_ref, bf16[128,8192]{1,0:T(8,128)(2,1)} %other_ref.1, bf16[128,8192]{1,0:T(8,128)(2,1)} %other_ref.1, f32[1,8192]{1,0:T(1,128)} %bitcast.27, f32[1,8192]{1,0:T(1,128)} %bitcast.28), custom_call_target="tpu_custom_call" | custom-call | flops 2097152 | bytes 2097152 | tf_op jit(solution)/shard_map/norm_rows/pallas_call | solution.py:45
  2.5 11.0 %all-to-all-start = ((bf16[8,64,1024]{2,1,0:T(8,128)(2,1)}), bf16[8,64,1024]{2,1,0:T(8,128)(2,1)S(1)}, u32[]{:S(2)}, u32[]{:S(2)}) async-start(bf16[8,64,1024]{2,1,0:T(8,128)(2,1)} %norm_rows.1), calls=%async_computation | async-start | bytes 2097152 | tf_op jit(solution)/shard_map/all_to_all | solution.py:209
  13.6 35.0 %conditional.2 = (bf16[1792,1024]{1,0:T(8,128)(2,1)}, bf16[2,32,1408]{2,1,0:T(8,128)(2,1)}, bf16[2,32,1408]{2,1,0:T(8,128)(2,1)}, bf16[2,32,1408]{2,1,0:T(8,128)...) conditional(s32[]{:T(128)} %convert_element_type.19, () %tuple.27, ...), branch_computations={%region_0.0_spmd, %region_1.0_spmd} | conditional | flops 1835008 | bytes 24953168 | solution.py:171
  13.6 1.1 pad_maximum_fusion.mine_ref
  14.6 4.7 %collective-permute-start = (bf16[896,512]{1,0:T(8,128)(2,1)S(1)}, bf16[896,512]{1,0:T(8,128)(2,1)S(1)}, u32[]{:S(2)}, u32[]{:S(2)}) collective-permute-start(bf16[896,512]{1,0:T(8,128)(2,1)S(1)} %pad_maximum_fusion.mine_ref), channel_id=1, source_target_pairs={{0,16},{16,0},{1,17},{17,1},{2,18},{18,2},{3,19},{19,3},{4,20},{20... | collective-permute-start | bytes 2752520 | tf_op jit(solution)/shard_map/cond/branch_1_fun/ppermute | solution.py:182
  19.4 5.2 %collective-permute-start.1 = (bf16[2,32,1408]{2,1,0:T(8,128)(2,1)S(1)}, bf16[2,32,1408]{2,1,0:T(8,128)(2,1)}, u32[]{:S(2)}, u32[]{:S(2)}) collective-permute-start(bf16[2,32,1408]{2,1,0:T(8,128)(2,1)S(1)} %get-tuple-element.47), channel_id=1, source_target_pairs={{0,192},{16,336},{64,256},{80,400},{128,320},{144,464},{192,384},{... | collective-permute-start | bytes 540680 | tf_op jit(solution)/shard_map/cond/branch_1_fun/ppermute | solution.py:178
  24.6 3.2 %collective-permute-start.2 = (bf16[2,32,1408]{2,1,0:T(8,128)(2,1)S(1)}, bf16[2,32,1408]{2,1,0:T(8,128)(2,1)}, u32[]{:S(2)}, u32[]{:S(2)}) collective-permute-start(bf16[2,32,1408]{2,1,0:T(8,128)(2,1)S(1)} %get-tuple-element.48), channel_id=1, source_target_pairs={{0,384},{16,144},{64,448},{80,208},{128,0},{144,272},{192,64},{208... | collective-permute-start | bytes 540680 | tf_op jit(solution)/shard_map/cond/branch_1_fun/ppermute | solution.py:178
  27.8 2.4 %collective-permute-start.3 = (bf16[2,32,1408]{2,1,0:T(8,128)(2,1)S(1)}, bf16[2,32,1408]{2,1,0:T(8,128)(2,1)}, u32[]{:S(2)}, u32[]{:S(2)}) collective-permute-start(bf16[2,32,1408]{2,1,0:T(8,128)(2,1)S(1)} %get-tuple-element.49), channel_id=1, source_target_pairs={{0,448},{16,80},{64,0},{80,144},{128,64},{144,208},{192,128},{208,... | collective-permute-start | bytes 540680 | tf_op jit(solution)/shard_map/cond/branch_1_fun/ppermute | solution.py:178
  30.2 3.7 %collective-permute-start.4 = (bf16[896,512]{1,0:T(8,128)(2,1)S(1)}, bf16[896,512]{1,0:T(8,128)(2,1)S(1)}, u32[]{:S(2)}, u32[]{:S(2)}) collective-permute-start(bf16[896,512]{1,0:T(8,128)(2,1)S(1)} %pad_maximum_fusion.mine_ref), channel_id=1, source_target_pairs={{0,1},{1,0},{2,3},{3,2},{4,5},{5,4},{6,7},{7,6},{8,9},{9,8},{10,11... | collective-permute-start | bytes 2752520 | tf_op jit(solution)/shard_map/cond/branch_1_fun/ppermute | solution.py:188
  34.8 7.1 %collective-permute-done.3 = bf16[2,32,1408]{2,1,0:T(8,128)(2,1)} collective-permute-done((bf16[2,32,1408]{2,1,0:T(8,128)(2,1)S(1)}, bf16[2,32,1408]{2,1,0:T(8,128)(2,1)}, u32[]{:S(2)}, u32[]{:S(2)}) %collective-permute-start.3) | collective-permute-done | bytes 180256 | tf_op jit(solution)/shard_map/cond/branch_1_fun/ppermute | solution.py:178
  41.9 2.5 %collective-permute-start.5 = (bf16[896,512]{1,0:T(8,128)(2,1)S(1)}, bf16[896,512]{1,0:T(8,128)(2,1)S(1)}, u32[]{:S(2)}, u32[]{:S(2)}) collective-permute-start(bf16[896,512]{1,0:T(8,128)(2,1)S(1)} %collective-permute-done.theirs_ref), channel_id=1, source_target_pairs={{0,1},{1,0},{2,3},{3,2},{4,5},{5,4},{6,7},{7,6},{8,9},{9,8},{10,11... | collective-permute-start | bytes 2752520 | tf_op jit(solution)/shard_map/cond/branch_1_fun/ppermute | solution.py:188
  44.4 1.9 %collective-permute-start.6 = (bf16[128,256]{1,0:T(8,128)(2,1)S(1)}, bf16[128,256]{1,0:T(8,128)(2,1)}, u32[]{:S(2)}, u32[]{:S(2)}) collective-permute-start(bf16[128,256]{1,0:T(8,128)(2,1)S(1)} %get-tuple-element.56), channel_id=1, source_target_pairs={{0,1},{1,0},{2,3},{3,2},{4,5},{5,4},{6,7},{7,6},{8,9},{9,8},{10,11... | collective-permute-start | bytes 196616 | tf_op jit(solution)/shard_map/cond/branch_1_fun/ppermute | solution.py:193
  46.4 2.1 %weights.1 = bf16[1792,1024]{1,0:T(8,128)(2,1)} custom-call(bf16[896,512]{1,0:T(8,128)(2,1)S(1)} %pad_maximum_fusion.mine_ref, bf16[896,512]{1,0:T(8,128)(2,1)S(1)} %collective-permute-done.theirs_ref, bf16[896,512]{1,0:T(8,128)(2,1)S(1)} %collective-permute-done.4.beside_ref, bf16[896,512]{1,0:T(8,128)(2,1)S(1)} %collective-permute-done.5.across_ref), custom_call_target="tpu_custom_call" | custom-call | bytes 7340032 | tf_op jit(solution)/shard_map/cond/branch_1_fun/weights/pallas_call | solution.py:92
  48.5 3.3 %terms.2 = (bf16[4,64,896]{2,1,0:T(8,128)(2,1)S(1)}, bf16[4,64,896]{2,1,0:T(8,128)(2,1)S(1)}) custom-call(s32[1]{0:T(128)} %bitcast.15.parity_ref, bf16[8,64,1024]{2,1,0:T(8,128)(2,1)S(1)} %all-to-all-done.rows_ref, bf16[1792,1024]{1,0:T(8,128)(2,1)} %get-tuple-element.116.weight_ref), custom_call_target="tpu_custom_call" | custom-call | flops 939524096 | bytes 5636096 | tf_op jit(solution)/shard_map/terms/pallas_call | solution.py:92
  51.9 3.3 %collective-permute-start.12 = (bf16[4,64,896]{2,1,0:T(8,128)(2,1)S(1)}, bf16[4,64,896]{2,1,0:T(8,128)(2,1)S(1)}, u32[]{:S(2)}, u32[]{:S(2)}) collective-permute-start(bf16[4,64,896]{2,1,0:T(8,128)(2,1)S(1)} %get-tuple-element.119), channel_id=1, source_target_pairs={{0,2},{2,0},{1,3},{3,1},{4,6},{6,4},{5,7},{7,5},{8,10},{10,8},{9,1... | collective-permute-start | bytes 1376264 | tf_op jit(solution)/shard_map/ppermute | solution.py:214
  55.2 4.3 %collective-permute-start.13 = (bf16[4,64,896]{2,1,0:T(8,128)(2,1)S(1)}, bf16[4,64,896]{2,1,0:T(8,128)(2,1)S(1)}, u32[]{:S(2)}, u32[]{:S(2)}) collective-permute-start(bf16[4,64,896]{2,1,0:T(8,128)(2,1)S(1)} %get-tuple-element.120), channel_id=1, source_target_pairs={{0,14},{2,4},{4,2},{6,8},{8,6},{10,12},{12,10},{14,0},{1,15},{3,5}... | collective-permute-start | bytes 1376264 | tf_op jit(solution)/shard_map/ppermute | solution.py:215
  59.5 5.8 %collective-permute-start.11 = (bf16[2,32,1408]{2,1,0:T(8,128)(2,1)S(1)}, bf16[2,32,1408]{2,1,0:T(8,128)(2,1)S(1)}, u32[]{:S(2)}, u32[]{:S(2)}) collective-permute-start(bf16[2,32,1408]{2,1,0:T(8,128)(2,1)S(1)} %get-tuple-element.125), channel_id=1, source_target_pairs={{0,256},{16,272},{64,320},{80,336},{128,384},{144,400},{192,448},{... | collective-permute-start | bytes 540680 | tf_op jit(solution)/shard_map/ppermute | solution.py:178
  65.3 3.3 %terms.3 = (f32[4,64,896]{2,1,0:T(8,128)S(1)}, f32[4,64,896]{2,1,0:T(8,128)S(1)}) custom-call(s32[1]{0:T(128)} %bitcast.16.parity_ref, bf16[8,64,1024]{2,1,0:T(8,128)(2,1)S(1)} %all-to-all-done.rows_ref, bf16[1792,1024]{1,0:T(8,128)(2,1)} %get-tuple-element.116.weight_ref), custom_call_target="tpu_custom_call" | custom-call | flops 939524096 | bytes 6553600 | tf_op jit(solution)/shard_map/terms/pallas_call | solution.py:92
  69.7 1.1 add_terms.1
  70.8 1.3 %collective-permute-done.11 = bf16[2,32,1408]{2,1,0:T(8,128)(2,1)S(1)} collective-permute-done((bf16[2,32,1408]{2,1,0:T(8,128)(2,1)S(1)}, bf16[2,32,1408]{2,1,0:T(8,128)(2,1)S(1)}, u32[]{:S(2)}, u32[]{:S(2)}) %collective-permute-start.11) | collective-permute-done | bytes 180256 | tf_op jit(solution)/shard_map/ppermute | solution.py:178
  72.1 4.2 %all-to-all-start.1 = ((bf16[4,64,1792]{2,1,0:T(8,128)(2,1)}), bf16[4,64,1792]{2,1,0:T(8,128)(2,1)S(1)}, u32[]{:S(2)}, u32[]{:S(2)}) async-start(bf16[4,64,1792]{2,1,0:T(8,128)(2,1)} %add_terms.1), calls=%async_computation.1 | async-start | bytes 1835008 | tf_op jit(solution)/shard_map/all_to_all | solution.py:222
  76.3 22.5 %conditional.3 = (bf16[512,896]{1,0:T(8,128)(2,1)}, bf16[512,128]{1,0:T(8,128)(2,1)S(1)}) conditional(s32[]{:T(128)} %convert_element_type.19, () %tuple.33, (s32[]{:T(128)}, s32[]{:T(128)}, s32[]{:T(128)}, s32[]{:T(128)}, bf16[2,32,1408]{2,1,0:T(8,128)(2,1)S(1)}, /*index=5*/bf16[2,32,1408]{2,1,0:T(8,128)(2,1)}, bf16[2,32,1408]{2,1,0:T(8,128)(2,1)}, ...), branch_computations={%region_3.4_spmd, %region_4.5_spmd} | conditional | flops 4 | bytes 9363682 | solution.py:171
  76.3 1.2 give.1
  77.4 2.2 %collective-permute-start.7 = (bf16[4,32,1408]{2,1,0:T(8,128)(2,1)S(1)}, bf16[4,32,1408]{2,1,0:T(8,128)(2,1)S(1)}, u32[]{:S(2)}, u32[]{:S(2)}) collective-permute-start(bf16[4,32,1408]{2,1,0:T(8,128)(2,1)S(1)} %get-tuple-element.66), channel_id=1, source_target_pairs={{0,32},{32,0},{1,33},{33,1},{2,34},{34,2},{3,35},{35,3},{4,36},{36... | collective-permute-start | bytes 1081352 | tf_op jit(solution)/shard_map/cond/branch_1_fun/ppermute | solution.py:200
  79.6 4.8 %collective-permute-start.10 = (bf16[3,32,1408]{2,1,0:T(8,128)(2,1)S(1)}, bf16[3,32,1408]{2,1,0:T(8,128)(2,1)S(1)}, u32[]{:S(2)}, u32[]{:S(2)}) collective-permute-start(bf16[3,32,1408]{2,1,0:T(8,128)(2,1)S(1)} %get-tuple-element.68), channel_id=1, source_target_pairs={{0,48},{16,32},{32,16},{48,0},{1,49},{17,33},{33,17},{49,1},{2,50}... | collective-permute-start | bytes 811016 | tf_op jit(solution)/shard_map/cond/branch_1_fun/ppermute | solution.py:199
  84.5 3.1 %collective-permute-start.9 = (bf16[3,32,1408]{2,1,0:T(8,128)(2,1)S(1)}, bf16[3,32,1408]{2,1,0:T(8,128)(2,1)S(1)}, u32[]{:S(2)}, u32[]{:S(2)}) collective-permute-start(bf16[3,32,1408]{2,1,0:T(8,128)(2,1)S(1)} %get-tuple-element.67), channel_id=1, source_target_pairs={{0,16},{16,0},{1,17},{17,1},{2,18},{18,2},{3,19},{19,3},{4,20},{20... | collective-permute-start | bytes 811016 | tf_op jit(solution)/shard_map/cond/branch_1_fun/ppermute | solution.py:198
  87.6 1.9 %collective-permute-start.8 = (bf16[32,1408]{1,0:T(8,128)(2,1)S(1)}, bf16[32,1408]{1,0:T(8,128)(2,1)S(1)}, u32[]{:S(2)}, u32[]{:S(2)}) collective-permute-start(bf16[32,1408]{1,0:T(8,128)(2,1)S(1)} %dynamic-slice_bitcast_fusion), channel_id=1, source_target_pairs={{0,32},{32,0},{1,33},{33,1},{2,34},{34,2},{3,35},{35,3},{4,36},{36... | collective-permute-start | bytes 270344 | tf_op jit(solution)/shard_map/cond/branch_1_fun/ppermute | solution.py:201
  89.5 6.5 %collective-permute-done.8.refs_6_ = bf16[32,1408]{1,0:T(8,128)(2,1)S(1)} collective-permute-done((bf16[32,1408]{1,0:T(8,128)(2,1)S(1)}, bf16[32,1408]{1,0:T(8,128)(2,1)S(1)}, u32[]{:S(2)}, u32[]{:S(2)}) %collective-permute-start.8) | collective-permute-done | bytes 90144 | tf_op jit(solution)/shard_map/cond/branch_1_fun/ppermute | solution.py:201
  96.4 2.3 %gather_factors.1 = (bf16[8,2,32,896]{3,2,1,0:T(8,128)(2,1)}, bf16[512,128]{1,0:T(8,128)(2,1)S(1)}, bf16[8,2,32,512]{3,2,1,0:T(8,128)(2,1)}) custom-call(s32[1]{0:T(128)} %bitcast.6.c_ref, s32[1]{0:T(128)} %bitcast.7.xl_ref, s32[1]{0:T(128)} %bitcast.8.y_ref, s32[1]{0:T(128)} %bitcast.9.xh_ref, bf16[2,32,1408]{2,1,0:T(8,128)(2,1)S(1)} %get-tuple-element.61.refs_0_, ...), custom_call_target="tpu_custom_call" | custom-call | bytes 3596288 | tf_op jit(solution)/shard_map/cond/branch_1_fun/gather_factors/pallas_call | solution.py:92
  99.9 4.5 %collective-permute-start.14 = (bf16[64,896]{1,0:T(8,128)(2,1)S(1)}, bf16[64,896]{1,0:T(8,128)(2,1)S(1)}, u32[]{:S(2)}, u32[]{:S(2)}) collective-permute-start(bf16[64,896]{1,0:T(8,128)(2,1)S(1)} %pad_maximum_fusion.2), channel_id=1, source_target_pairs={{0,1},{1,0},{2,3},{3,2},{4,5},{5,4},{6,7},{7,6},{8,9},{9,8},{10,11... | collective-permute-start | bytes 344072 | tf_op jit(solution)/shard_map/ppermute | solution.py:232
  105.4 1.6 %convolution_convert_fusion = bf16[512,128]{1,0:T(8,128)(2,1)S(1)} fusion(bf16[512,896]{1,0:T(8,128)(2,1)} %get-tuple-element.140, bf16[64,896]{1,0:T(8,128)(2,1)S(1)} %get-tuple-element.147, bf16[64,896]{1,0:T(8,128)(2,1)S(1)} %get-tuple-element.146), kind=kOutput, calls=%fused_computation.3 | convolution fusion | flops 117964800 | bytes 1277952 | tf_op jit(solution)/shard_map/dot_general | solution.py:233
  107.0 18.1 %all_to_all.15 = bf16[16,64,128]{2,1,0:T(8,128)(2,1)S(1)} all-to-all(bf16[16,64,128]{2,1,0:T(8,128)(2,1)S(1)} %pad_maximum_fusion.1), channel_id=1, replica_groups=mesh['y'=8,'xl'=2,'xh'=2,'zh'=4,'zl'=2,'c'=2] {'y','xl'}, dimensions={0} | all-to-all | bytes 524288 | tf_op jit(solution)/shard_map/all_to_all | solution.py:236
  (32 shorter events, 5.2 us)
Async XLA Ops:
  2.5 11.0 %copy-start = (bf16[1,32,14336]{2,1,0:T(8,128)(2,1)S(1)}, bf16[1,32,14336]{2,1,0:T(8,128)(2,1)}, u32[]{:S(2)}) copy-start(bf16[1,32,14336]{2,1,0:T(8,128)(2,1)} %param.16) | copy-start | bytes 2752516
  2.5 11.0 %copy-start.1 = (bf16[1,32,8192]{2,1,0:T(8,128)(2,1)S(1)}, bf16[1,32,8192]{2,1,0:T(8,128)(2,1)}, u32[]{:S(2)}) copy-start(bf16[1,32,8192]{2,1,0:T(8,128)(2,1)} %param.17) | copy-start | bytes 1572868
  2.5 11.0 %copy-start.2 = (bf16[512,448]{0,1:T(8,128)(2,1)S(1)}, bf16[512,448]{0,1:T(8,128)(2,1)}, u32[]{:S(2)}) copy-start(bf16[512,448]{0,1:T(8,128)(2,1)} %param.13) | copy-start | bytes 1376260
  2.5 11.0 %copy-start.3 = (bf16[128,256]{1,0:T(8,128)(2,1)S(1)}, bf16[128,256]{1,0:T(8,128)(2,1)}, u32[]{:S(2)}) copy-start(bf16[128,256]{1,0:T(8,128)(2,1)} %param.15) | copy-start | bytes 196612
  2.5 46.0 %all-to-all-start = ((bf16[8,64,1024]{2,1,0:T(8,128)(2,1)}), bf16[8,64,1024]{2,1,0:T(8,128)(2,1)S(1)}, u32[]{:S(2)}, u32[]{:S(2)}) async-start(bf16[8,64,1024]{2,1,0:T(8,128)(2,1)} %norm_rows.1), calls=%async_computation | async-start | bytes 2097152 | tf_op jit(solution)/shard_map/all_to_all | solution.py:209
  14.6 27.3 %collective-permute-start = (bf16[896,512]{1,0:T(8,128)(2,1)S(1)}, bf16[896,512]{1,0:T(8,128)(2,1)S(1)}, u32[]{:S(2)}, u32[]{:S(2)}) collective-permute-start(bf16[896,512]{1,0:T(8,128)(2,1)S(1)} %pad_maximum_fusion.mine_ref), channel_id=1, source_target_pairs={{0,16},{16,0},{1,17},{17,1},{2,18},{18,2},{3,19},{19,3},{4,20},{20... | collective-permute-start | bytes 2752520 | tf_op jit(solution)/shard_map/cond/branch_1_fun/ppermute | solution.py:182
  19.4 15.4 %collective-permute-start.1 = (bf16[2,32,1408]{2,1,0:T(8,128)(2,1)S(1)}, bf16[2,32,1408]{2,1,0:T(8,128)(2,1)}, u32[]{:S(2)}, u32[]{:S(2)}) collective-permute-start(bf16[2,32,1408]{2,1,0:T(8,128)(2,1)S(1)} %get-tuple-element.47), channel_id=1, source_target_pairs={{0,192},{16,336},{64,256},{80,400},{128,320},{144,464},{192,384},{... | collective-permute-start | bytes 540680 | tf_op jit(solution)/shard_map/cond/branch_1_fun/ppermute | solution.py:178
  24.6 10.1 %collective-permute-start.2 = (bf16[2,32,1408]{2,1,0:T(8,128)(2,1)S(1)}, bf16[2,32,1408]{2,1,0:T(8,128)(2,1)}, u32[]{:S(2)}, u32[]{:S(2)}) collective-permute-start(bf16[2,32,1408]{2,1,0:T(8,128)(2,1)S(1)} %get-tuple-element.48), channel_id=1, source_target_pairs={{0,384},{16,144},{64,448},{80,208},{128,0},{144,272},{192,64},{208... | collective-permute-start | bytes 540680 | tf_op jit(solution)/shard_map/cond/branch_1_fun/ppermute | solution.py:178
  27.8 14.1 %collective-permute-start.3 = (bf16[2,32,1408]{2,1,0:T(8,128)(2,1)S(1)}, bf16[2,32,1408]{2,1,0:T(8,128)(2,1)}, u32[]{:S(2)}, u32[]{:S(2)}) collective-permute-start(bf16[2,32,1408]{2,1,0:T(8,128)(2,1)S(1)} %get-tuple-element.49), channel_id=1, source_target_pairs={{0,448},{16,80},{64,0},{80,144},{128,64},{144,208},{192,128},{208,... | collective-permute-start | bytes 540680 | tf_op jit(solution)/shard_map/cond/branch_1_fun/ppermute | solution.py:178
  30.2 16.1 %collective-permute-start.4 = (bf16[896,512]{1,0:T(8,128)(2,1)S(1)}, bf16[896,512]{1,0:T(8,128)(2,1)S(1)}, u32[]{:S(2)}, u32[]{:S(2)}) collective-permute-start(bf16[896,512]{1,0:T(8,128)(2,1)S(1)} %pad_maximum_fusion.mine_ref), channel_id=1, source_target_pairs={{0,1},{1,0},{2,3},{3,2},{4,5},{5,4},{6,7},{7,6},{8,9},{9,8},{10,11... | collective-permute-start | bytes 2752520 | tf_op jit(solution)/shard_map/cond/branch_1_fun/ppermute | solution.py:188
  41.9 4.5 %collective-permute-start.5 = (bf16[896,512]{1,0:T(8,128)(2,1)S(1)}, bf16[896,512]{1,0:T(8,128)(2,1)S(1)}, u32[]{:S(2)}, u32[]{:S(2)}) collective-permute-start(bf16[896,512]{1,0:T(8,128)(2,1)S(1)} %collective-permute-done.theirs_ref), channel_id=1, source_target_pairs={{0,1},{1,0},{2,3},{3,2},{4,5},{5,4},{6,7},{7,6},{8,9},{9,8},{10,11... | collective-permute-start | bytes 2752520 | tf_op jit(solution)/shard_map/cond/branch_1_fun/ppermute | solution.py:188
  44.4 4.1 %collective-permute-start.6 = (bf16[128,256]{1,0:T(8,128)(2,1)S(1)}, bf16[128,256]{1,0:T(8,128)(2,1)}, u32[]{:S(2)}, u32[]{:S(2)}) collective-permute-start(bf16[128,256]{1,0:T(8,128)(2,1)S(1)} %get-tuple-element.56), channel_id=1, source_target_pairs={{0,1},{1,0},{2,3},{3,2},{4,5},{5,4},{6,7},{7,6},{8,9},{9,8},{10,11... | collective-permute-start | bytes 196616 | tf_op jit(solution)/shard_map/cond/branch_1_fun/ppermute | solution.py:193
  51.9 16.8 %collective-permute-start.12 = (bf16[4,64,896]{2,1,0:T(8,128)(2,1)S(1)}, bf16[4,64,896]{2,1,0:T(8,128)(2,1)S(1)}, u32[]{:S(2)}, u32[]{:S(2)}) collective-permute-start(bf16[4,64,896]{2,1,0:T(8,128)(2,1)S(1)} %get-tuple-element.119), channel_id=1, source_target_pairs={{0,2},{2,0},{1,3},{3,1},{4,6},{6,4},{5,7},{7,5},{8,10},{10,8},{9,1... | collective-permute-start | bytes 1376264 | tf_op jit(solution)/shard_map/ppermute | solution.py:214
  55.2 14.5 %collective-permute-start.13 = (bf16[4,64,896]{2,1,0:T(8,128)(2,1)S(1)}, bf16[4,64,896]{2,1,0:T(8,128)(2,1)S(1)}, u32[]{:S(2)}, u32[]{:S(2)}) collective-permute-start(bf16[4,64,896]{2,1,0:T(8,128)(2,1)S(1)} %get-tuple-element.120), channel_id=1, source_target_pairs={{0,14},{2,4},{4,2},{6,8},{8,6},{10,12},{12,10},{14,0},{1,15},{3,5}... | collective-permute-start | bytes 1376264 | tf_op jit(solution)/shard_map/ppermute | solution.py:215
  59.5 12.6 %collective-permute-start.11 = (bf16[2,32,1408]{2,1,0:T(8,128)(2,1)S(1)}, bf16[2,32,1408]{2,1,0:T(8,128)(2,1)S(1)}, u32[]{:S(2)}, u32[]{:S(2)}) collective-permute-start(bf16[2,32,1408]{2,1,0:T(8,128)(2,1)S(1)} %get-tuple-element.125), channel_id=1, source_target_pairs={{0,256},{16,272},{64,320},{80,336},{128,384},{144,400},{192,448},{... | collective-permute-start | bytes 540680 | tf_op jit(solution)/shard_map/ppermute | solution.py:178
  72.1 27.5 %all-to-all-start.1 = ((bf16[4,64,1792]{2,1,0:T(8,128)(2,1)}), bf16[4,64,1792]{2,1,0:T(8,128)(2,1)S(1)}, u32[]{:S(2)}, u32[]{:S(2)}) async-start(bf16[4,64,1792]{2,1,0:T(8,128)(2,1)} %add_terms.1), calls=%async_computation.1 | async-start | bytes 1835008 | tf_op jit(solution)/shard_map/all_to_all | solution.py:222
  77.4 19.0 %collective-permute-start.7 = (bf16[4,32,1408]{2,1,0:T(8,128)(2,1)S(1)}, bf16[4,32,1408]{2,1,0:T(8,128)(2,1)S(1)}, u32[]{:S(2)}, u32[]{:S(2)}) collective-permute-start(bf16[4,32,1408]{2,1,0:T(8,128)(2,1)S(1)} %get-tuple-element.66), channel_id=1, source_target_pairs={{0,32},{32,0},{1,33},{33,1},{2,34},{34,2},{3,35},{35,3},{4,36},{36... | collective-permute-start | bytes 1081352 | tf_op jit(solution)/shard_map/cond/branch_1_fun/ppermute | solution.py:200
  79.6 16.4 %collective-permute-start.10 = (bf16[3,32,1408]{2,1,0:T(8,128)(2,1)S(1)}, bf16[3,32,1408]{2,1,0:T(8,128)(2,1)S(1)}, u32[]{:S(2)}, u32[]{:S(2)}) collective-permute-start(bf16[3,32,1408]{2,1,0:T(8,128)(2,1)S(1)} %get-tuple-element.68), channel_id=1, source_target_pairs={{0,48},{16,32},{32,16},{48,0},{1,49},{17,33},{33,17},{49,1},{2,50}... | collective-permute-start | bytes 811016 | tf_op jit(solution)/shard_map/cond/branch_1_fun/ppermute | solution.py:199
  84.5 12.0 %collective-permute-start.9 = (bf16[3,32,1408]{2,1,0:T(8,128)(2,1)S(1)}, bf16[3,32,1408]{2,1,0:T(8,128)(2,1)S(1)}, u32[]{:S(2)}, u32[]{:S(2)}) collective-permute-start(bf16[3,32,1408]{2,1,0:T(8,128)(2,1)S(1)} %get-tuple-element.67), channel_id=1, source_target_pairs={{0,16},{16,0},{1,17},{17,1},{2,18},{18,2},{3,19},{19,3},{4,20},{20... | collective-permute-start | bytes 811016 | tf_op jit(solution)/shard_map/cond/branch_1_fun/ppermute | solution.py:198
  87.6 8.5 %collective-permute-start.8 = (bf16[32,1408]{1,0:T(8,128)(2,1)S(1)}, bf16[32,1408]{1,0:T(8,128)(2,1)S(1)}, u32[]{:S(2)}, u32[]{:S(2)}) collective-permute-start(bf16[32,1408]{1,0:T(8,128)(2,1)S(1)} %dynamic-slice_bitcast_fusion), channel_id=1, source_target_pairs={{0,32},{32,0},{1,33},{33,1},{2,34},{34,2},{3,35},{35,3},{4,36},{36... | collective-permute-start | bytes 270344 | tf_op jit(solution)/shard_map/cond/branch_1_fun/ppermute | solution.py:201
  99.9 5.5 %collective-permute-start.14 = (bf16[64,896]{1,0:T(8,128)(2,1)S(1)}, bf16[64,896]{1,0:T(8,128)(2,1)S(1)}, u32[]{:S(2)}, u32[]{:S(2)}) collective-permute-start(bf16[64,896]{1,0:T(8,128)(2,1)S(1)} %pad_maximum_fusion.2), channel_id=1, source_target_pairs={{0,1},{1,0},{2,3},{3,2},{4,5},{5,4},{6,7},{7,6},{8,9},{9,8},{10,11... | collective-permute-start | bytes 344072 | tf_op jit(solution)/shard_map/ppermute | solution.py:232

commit v4 on v3

--- a/solution.py
+++ b/solution.py
@@ -62,28 +62,25 @@
     )(core.reshape(1), pair.reshape(1), residual, residual, gain, gain)
 
 
-def term_kernel(parity_ref, rows_ref, weight_ref, *out_refs):
+def term_kernel(parity_ref, rows_ref, weight_ref, out_ref):
     peers, half, width = rows_ref.shape
     rows = jnp.concatenate([rows_ref[2 * i + parity_ref[0]] for i in range(peers // 2)], axis=0)
     cols = weight_ref.shape[0] // 2
-    for core, out_ref in enumerate(out_refs):
-        weight = weight_ref[core * cols : (core + 1) * cols]
-        total = lax.dot_general(rows, weight, (((1,), (1,)), ((), ())), preferred_element_type=jnp.float32)
-        out_ref[...] = total.astype(out_ref.dtype).reshape(out_ref.shape)
+    for core in range(2):
+        at = slice(core * cols, (core + 1) * cols)
+        total = lax.dot_general(rows, weight_ref[at], (((1,), (1,)), ((), ())), preferred_element_type=jnp.float32)
+        out_ref[:, :, at] = total.astype(out_ref.dtype).reshape(peers // 2, half, cols)
 
 
 def terms_of(rows, weight, parity, kind):
     peers, half, width = rows.shape
     cols = weight.shape[0]
-    shape = jax.ShapeDtypeStruct((peers // 2, half, cols // 2), kind)
-    return whole_kernel(term_kernel, (parity,), (rows, weight), [shape] * 2, "terms", peers * half * width * cols)
-
-
-def add_kernel(keep_ref, beside_ref, got_ref, across_ref, out_ref):
-    cols = keep_ref.shape[2]
-    for at, (own, other) in enumerate(((keep_ref, got_ref), (beside_ref, across_ref))):
-        total = own[...] + other[...].astype(jnp.float32)
-        out_ref[:, :, at * cols : (at + 1) * cols] = total.astype(out_ref.dtype)
+    shape = jax.ShapeDtypeStruct((peers // 2, half, cols), kind)
+    return whole_kernel(term_kernel, (parity,), (rows, weight), [shape], "terms", peers * half * width * cols)[0]
+
+
+def add_kernel(keep_ref, got_ref, out_ref):
+    out_ref[...] = (keep_ref[...] + got_ref[...].astype(jnp.float32)).astype(out_ref.dtype)
 
 
 def whole_kernel(body, scalars, inputs, outputs, name, flops=0):
@@ -211,13 +208,17 @@
 
     give = terms_of(rows, weight, 1 - zl, jnp.bfloat16)
     give, rows = lax.optimization_barrier((give, rows))
-    got = lax.ppermute(give[0], "zl", SWAP)
-    across = lax.ppermute(give[1], DEPTH, [(i, (i + (1 if i % 2 else -1)) % peers) for i in range(peers)])
+    pairs = []
+    for z in range(peers):
+        for core in range(2):
+            side = 1 if z % 2 == core else -1
+            pairs.append((z * 2 + core, (z + side) % peers * 2 + core))
+    got = lax.ppermute(give, DEPTH + ("c",), pairs)
     keep = terms_of(rows, weight, zl, jnp.float32)
     late, give = lax.optimization_barrier((late, give))
     far = along_y(late[1], STEPS - 1)
     near = [late[0]] + [early[EARLY.index(step)] for step in range(1, STEPS - 1)]
-    (term,) = whole_kernel(add_kernel, (), (*keep, got, across), [like(peers // 2, tokens // 2, 4 * cols)], "add_terms")
+    (term,) = whole_kernel(add_kernel, (), (keep, got), [like(peers // 2, tokens // 2, 4 * cols)], "add_terms")
     inputs, term = lax.optimization_barrier(((near, far, out_grad, beside_grad), term))
     summed = lax.all_to_all(term, "zh", 0, 0, tiled=True)
     factors, sensed = fenced(beside_sums, *inputs)

time: 127 us -> 124 us (0.976)
  starting transfers between devices: 68.7 us -> 65.5 us
  waiting for transfers between devices: 19.1 us -> 20.6 us
    ppermute x2 -> x1, starting transfers between devices: 7.62 us -> 4.53 us  [on_device(): got = lax.ppermute(give, DEPTH + ('c',), pairs)]
    ppermute x1, waiting for transfers between devices: 6.53 us -> 7.93 us  [beside_sums(): lax.ppermute(lax.dynamic_index_in_dim(far, 1 - xl, 0, keepdims=False), 'x...]
  transfers between devices with their start and end apart: 17 -> 16, of which waited for: 9 -> 7; matrix products, arithmetic and copies ran while one was open for 1% -> 1% of each run, Pallas kernels for 8% -> 8%
where the time goes in v4:
time: 124 us; the launch traced here: 123 us
  starting transfers between devices  65.5 us (53%)
  waiting for transfers between devices  20.6 us (17%)
  blocking collectives  17.4 us (14%)
  Pallas kernels  15.9 us (13%)
  other arithmetic  2.07 us (2%)
  matrix products  1.58 us (1%)
    all_to_all x1, blocking collectives, on_device(): lax.all_to_all(jnp.concatenate(parts, axis=1), CHIPS, 0, 0, tiled=True)  17.4 us
    ppermute x4, starting transfers between devices, along_y(): return lax.ppermute(piece, ('y', 'xh'), pairs)  16.6 us
    pallas_call x7, Pallas kernels, whole_kernel(): pl.pallas_call(body, out_shape=outputs, in_specs=[pl.BlockSpec(memory_spa...  13.4 us
    all_to_all x1, starting transfers between devices, on_device(): rows = lax.all_to_all(normed, DEPTH, 0, 0, tiled=True)  11 us
    ppermute x4, waiting for transfers between devices, along_y(): return lax.ppermute(piece, ('y', 'xh'), pairs)  9.62 us
    ppermute x1, waiting for transfers between devices, beside_sums(): lax.ppermute(lax.dynamic_index_in_dim(far, 1 - xl, 0, keepdims=False), 'x...  7.93 us
    ppermute x2, starting transfers between devices, beside_tokens(): beside = (lax.ppermute(mine, 'c', SWAP), lax.ppermute(theirs, 'c', SWAP))  6.17 us
    all_to_all x1, starting transfers between devices, on_device(): summed = lax.all_to_all(term, 'zh', 0, 0, tiled=True)  4.96 us
  transfers between devices with their start and end apart: 16, of which 7 were waited for; matrix products, arithmetic and copies ran while one was open for 1% of the time, Pallas kernels for 8%

profile of v4, /device:TPU:1, one launch (start us, length us, event | category | flops | bytes accessed | tf_op | source)
XLA Modules:
  0.0 123.4 jit_solution(5265655784826611972)
XLA Ops:
  0.0 2.5 %norm_rows.1 = bf16[8,64,1024]{2,1,0:T(8,128)(2,1)} custom-call(s32[1]{0:T(128)} %bitcast.12.core_ref, s32[1]{0:T(128)} %bitcast.13.pair_ref, bf16[128,8192]{1,0:T(8,128)(2,1)} %other_ref.1, bf16[128,8192]{1,0:T(8,128)(2,1)} %other_ref.1, f32[1,8192]{1,0:T(1,128)} %bitcast.27, f32[1,8192]{1,0:T(1,128)} %bitcast.28), custom_call_target="tpu_custom_call" | custom-call | flops 2097152 | bytes 2097152 | tf_op jit(solution)/shard_map/norm_rows/pallas_call | solution.py:45
  2.5 11.0 %all-to-all-start = ((bf16[8,64,1024]{2,1,0:T(8,128)(2,1)}), bf16[8,64,1024]{2,1,0:T(8,128)(2,1)S(1)}, u32[]{:S(2)}, u32[]{:S(2)}) async-start(bf16[8,64,1024]{2,1,0:T(8,128)(2,1)} %norm_rows.1), calls=%async_computation | async-start | bytes 2097152 | tf_op jit(solution)/shard_map/all_to_all | solution.py:206
  13.6 35.0 %conditional.2 = (bf16[1792,1024]{1,0:T(8,128)(2,1)}, bf16[2,32,1408]{2,1,0:T(8,128)(2,1)}, bf16[2,32,1408]{2,1,0:T(8,128)(2,1)}, bf16[2,32,1408]{2,1,0:T(8,128)...) conditional(s32[]{:T(128)} %convert_element_type.19, () %tuple.27, ...), branch_computations={%region_0.0_spmd, %region_1.0_spmd} | conditional | flops 1835008 | bytes 24953168 | solution.py:168
  13.6 1.1 pad_maximum_fusion.mine_ref
  14.7 4.7 %collective-permute-start = (bf16[896,512]{1,0:T(8,128)(2,1)S(1)}, bf16[896,512]{1,0:T(8,128)(2,1)S(1)}, u32[]{:S(2)}, u32[]{:S(2)}) collective-permute-start(bf16[896,512]{1,0:T(8,128)(2,1)S(1)} %pad_maximum_fusion.mine_ref), channel_id=1, source_target_pairs={{0,16},{16,0},{1,17},{17,1},{2,18},{18,2},{3,19},{19,3},{4,20},{20... | collective-permute-start | bytes 2752520 | tf_op jit(solution)/shard_map/cond/branch_1_fun/ppermute | solution.py:179
  19.4 5.2 %collective-permute-start.1 = (bf16[2,32,1408]{2,1,0:T(8,128)(2,1)S(1)}, bf16[2,32,1408]{2,1,0:T(8,128)(2,1)}, u32[]{:S(2)}, u32[]{:S(2)}) collective-permute-start(bf16[2,32,1408]{2,1,0:T(8,128)(2,1)S(1)} %get-tuple-element.47), channel_id=1, source_target_pairs={{0,192},{16,336},{64,256},{80,400},{128,320},{144,464},{192,384},{... | collective-permute-start | bytes 540680 | tf_op jit(solution)/shard_map/cond/branch_1_fun/ppermute | solution.py:175
  24.7 3.2 %collective-permute-start.2 = (bf16[2,32,1408]{2,1,0:T(8,128)(2,1)S(1)}, bf16[2,32,1408]{2,1,0:T(8,128)(2,1)}, u32[]{:S(2)}, u32[]{:S(2)}) collective-permute-start(bf16[2,32,1408]{2,1,0:T(8,128)(2,1)S(1)} %get-tuple-element.48), channel_id=1, source_target_pairs={{0,384},{16,144},{64,448},{80,208},{128,0},{144,272},{192,64},{208... | collective-permute-start | bytes 540680 | tf_op jit(solution)/shard_map/cond/branch_1_fun/ppermute | solution.py:175
  27.8 2.4 %collective-permute-start.3 = (bf16[2,32,1408]{2,1,0:T(8,128)(2,1)S(1)}, bf16[2,32,1408]{2,1,0:T(8,128)(2,1)}, u32[]{:S(2)}, u32[]{:S(2)}) collective-permute-start(bf16[2,32,1408]{2,1,0:T(8,128)(2,1)S(1)} %get-tuple-element.49), channel_id=1, source_target_pairs={{0,448},{16,80},{64,0},{80,144},{128,64},{144,208},{192,128},{208,... | collective-permute-start | bytes 540680 | tf_op jit(solution)/shard_map/cond/branch_1_fun/ppermute | solution.py:175
  30.2 3.7 %collective-permute-start.4 = (bf16[896,512]{1,0:T(8,128)(2,1)S(1)}, bf16[896,512]{1,0:T(8,128)(2,1)S(1)}, u32[]{:S(2)}, u32[]{:S(2)}) collective-permute-start(bf16[896,512]{1,0:T(8,128)(2,1)S(1)} %pad_maximum_fusion.mine_ref), channel_id=1, source_target_pairs={{0,1},{1,0},{2,3},{3,2},{4,5},{5,4},{6,7},{7,6},{8,9},{9,8},{10,11... | collective-permute-start | bytes 2752520 | tf_op jit(solution)/shard_map/cond/branch_1_fun/ppermute | solution.py:185
  34.8 7.1 %collective-permute-done.3 = bf16[2,32,1408]{2,1,0:T(8,128)(2,1)} collective-permute-done((bf16[2,32,1408]{2,1,0:T(8,128)(2,1)S(1)}, bf16[2,32,1408]{2,1,0:T(8,128)(2,1)}, u32[]{:S(2)}, u32[]{:S(2)}) %collective-permute-start.3) | collective-permute-done | bytes 180256 | tf_op jit(solution)/shard_map/cond/branch_1_fun/ppermute | solution.py:175
  41.9 2.5 %collective-permute-start.5 = (bf16[896,512]{1,0:T(8,128)(2,1)S(1)}, bf16[896,512]{1,0:T(8,128)(2,1)S(1)}, u32[]{:S(2)}, u32[]{:S(2)}) collective-permute-start(bf16[896,512]{1,0:T(8,128)(2,1)S(1)} %collective-permute-done.theirs_ref), channel_id=1, source_target_pairs={{0,1},{1,0},{2,3},{3,2},{4,5},{5,4},{6,7},{7,6},{8,9},{9,8},{10,11... | collective-permute-start | bytes 2752520 | tf_op jit(solution)/shard_map/cond/branch_1_fun/ppermute | solution.py:185
  44.4 1.9 %collective-permute-start.6 = (bf16[128,256]{1,0:T(8,128)(2,1)S(1)}, bf16[128,256]{1,0:T(8,128)(2,1)}, u32[]{:S(2)}, u32[]{:S(2)}) collective-permute-start(bf16[128,256]{1,0:T(8,128)(2,1)S(1)} %get-tuple-element.56), channel_id=1, source_target_pairs={{0,1},{1,0},{2,3},{3,2},{4,5},{5,4},{6,7},{7,6},{8,9},{9,8},{10,11... | collective-permute-start | bytes 196616 | tf_op jit(solution)/shard_map/cond/branch_1_fun/ppermute | solution.py:190
  46.5 2.1 %weights.1 = bf16[1792,1024]{1,0:T(8,128)(2,1)} custom-call(bf16[896,512]{1,0:T(8,128)(2,1)S(1)} %pad_maximum_fusion.mine_ref, bf16[896,512]{1,0:T(8,128)(2,1)S(1)} %collective-permute-done.theirs_ref, bf16[896,512]{1,0:T(8,128)(2,1)S(1)} %collective-permute-done.4.beside_ref, bf16[896,512]{1,0:T(8,128)(2,1)S(1)} %collective-permute-done.5.across_ref), custom_call_target="tpu_custom_call" | custom-call | bytes 7340032 | tf_op jit(solution)/shard_map/cond/branch_1_fun/weights/pallas_call | solution.py:89
  48.6 3.3 %terms.2 = bf16[4,64,1792]{2,1,0:T(8,128)(2,1)S(1)} custom-call(s32[1]{0:T(128)} %bitcast.15.parity_ref, bf16[8,64,1024]{2,1,0:T(8,128)(2,1)S(1)} %all-to-all-done.rows_ref, bf16[1792,1024]{1,0:T(8,128)(2,1)} %get-tuple-element.111.weight_ref), custom_call_target="tpu_custom_call" | custom-call | flops 939524096 | bytes 5636096 | tf_op jit(solution)/shard_map/terms/pallas_call | solution.py:89
  51.9 4.5 %collective-permute-start.12 = (bf16[4,64,1792]{2,1,0:T(8,128)(2,1)S(1)}, bf16[4,64,1792]{2,1,0:T(8,128)(2,1)S(1)}, u32[]{:S(2)}, u32[]{:S(2)}) collective-permute-start(bf16[4,64,1792]{2,1,0:T(8,128)(2,1)S(1)} %terms.2), channel_id=1, source_target_pairs={{0,2},{1,15},{2,0},{3,5},{4,6},{5,3},{6,4},{7,9},{8,10},{9,7},{10,... | collective-permute-start | bytes 2752520 | tf_op jit(solution)/shard_map/ppermute | solution.py:216
  56.4 5.8 %collective-permute-start.11 = (bf16[2,32,1408]{2,1,0:T(8,128)(2,1)S(1)}, bf16[2,32,1408]{2,1,0:T(8,128)(2,1)S(1)}, u32[]{:S(2)}, u32[]{:S(2)}) collective-permute-start(bf16[2,32,1408]{2,1,0:T(8,128)(2,1)S(1)} %get-tuple-element.117), channel_id=1, source_target_pairs={{0,256},{16,272},{64,320},{80,336},{128,384},{144,400},{192,448},{... | collective-permute-start | bytes 540680 | tf_op jit(solution)/shard_map/ppermute | solution.py:175
  62.3 3.3 %terms.3.keep_ref = f32[4,64,1792]{2,1,0:T(8,128)S(1)} custom-call(s32[1]{0:T(128)} %bitcast.16.parity_ref, bf16[8,64,1024]{2,1,0:T(8,128)(2,1)S(1)} %all-to-all-done.rows_ref, bf16[1792,1024]{1,0:T(8,128)(2,1)} %get-tuple-element.111.weight_ref), custom_call_target="tpu_custom_call" | custom-call | flops 939524096 | bytes 6553600 | tf_op jit(solution)/shard_map/terms/pallas_call | solution.py:89
  65.6 1.9 %collective-permute-done.12.got_ref = bf16[4,64,1792]{2,1,0:T(8,128)(2,1)S(1)} collective-permute-done((bf16[4,64,1792]{2,1,0:T(8,128)(2,1)S(1)}, bf16[4,64,1792]{2,1,0:T(8,128)(2,1)S(1)}, u32[]{:S(2)}, u32[]{:S(2)}) %collective-permute-start.12) | collective-permute-done | bytes 917536 | tf_op jit(solution)/shard_map/ppermute | solution.py:216
  67.5 1.1 add_terms.1
  68.6 1.6 %collective-permute-done.11 = bf16[2,32,1408]{2,1,0:T(8,128)(2,1)S(1)} collective-permute-done((bf16[2,32,1408]{2,1,0:T(8,128)(2,1)S(1)}, bf16[2,32,1408]{2,1,0:T(8,128)(2,1)S(1)}, u32[]{:S(2)}, u32[]{:S(2)}) %collective-permute-start.11) | collective-permute-done | bytes 180256 | tf_op jit(solution)/shard_map/ppermute | solution.py:175
  70.3 5.0 %all-to-all-start.1 = ((bf16[4,64,1792]{2,1,0:T(8,128)(2,1)}), bf16[4,64,1792]{2,1,0:T(8,128)(2,1)S(1)}, u32[]{:S(2)}, u32[]{:S(2)}) async-start(bf16[4,64,1792]{2,1,0:T(8,128)(2,1)} %add_terms.1), calls=%async_computation.1 | async-start | bytes 1835008 | tf_op jit(solution)/shard_map/all_to_all | solution.py:223
  75.2 22.9 %conditional.3 = (bf16[512,896]{1,0:T(8,128)(2,1)}, bf16[512,128]{1,0:T(8,128)(2,1)S(1)}) conditional(s32[]{:T(128)} %convert_element_type.19, () %tuple.33, (s32[]{:T(128)}, s32[]{:T(128)}, s32[]{:T(128)}, s32[]{:T(128)}, bf16[2,32,1408]{2,1,0:T(8,128)(2,1)S(1)}, /*index=5*/bf16[2,32,1408]{2,1,0:T(8,128)(2,1)}, bf16[2,32,1408]{2,1,0:T(8,128)(2,1)}, ...), branch_computations={%region_3.4_spmd, %region_4.5_spmd} | conditional | flops 4 | bytes 9363682 | solution.py:168
  75.2 1.2 give.1
  76.4 2.2 %collective-permute-start.7 = (bf16[4,32,1408]{2,1,0:T(8,128)(2,1)S(1)}, bf16[4,32,1408]{2,1,0:T(8,128)(2,1)S(1)}, u32[]{:S(2)}, u32[]{:S(2)}) collective-permute-start(bf16[4,32,1408]{2,1,0:T(8,128)(2,1)S(1)} %get-tuple-element.66), channel_id=1, source_target_pairs={{0,32},{32,0},{1,33},{33,1},{2,34},{34,2},{3,35},{35,3},{4,36},{36... | collective-permute-start | bytes 1081352 | tf_op jit(solution)/shard_map/cond/branch_1_fun/ppermute | solution.py:197
  78.6 4.1 %collective-permute-start.10 = (bf16[3,32,1408]{2,1,0:T(8,128)(2,1)S(1)}, bf16[3,32,1408]{2,1,0:T(8,128)(2,1)S(1)}, u32[]{:S(2)}, u32[]{:S(2)}) collective-permute-start(bf16[3,32,1408]{2,1,0:T(8,128)(2,1)S(1)} %get-tuple-element.68), channel_id=1, source_target_pairs={{0,48},{16,32},{32,16},{48,0},{1,49},{17,33},{33,17},{49,1},{2,50}... | collective-permute-start | bytes 811016 | tf_op jit(solution)/shard_map/cond/branch_1_fun/ppermute | solution.py:196
  82.8 3.1 %collective-permute-start.9 = (bf16[3,32,1408]{2,1,0:T(8,128)(2,1)S(1)}, bf16[3,32,1408]{2,1,0:T(8,128)(2,1)S(1)}, u32[]{:S(2)}, u32[]{:S(2)}) collective-permute-start(bf16[3,32,1408]{2,1,0:T(8,128)(2,1)S(1)} %get-tuple-element.67), channel_id=1, source_target_pairs={{0,16},{16,0},{1,17},{17,1},{2,18},{18,2},{3,19},{19,3},{4,20},{20... | collective-permute-start | bytes 811016 | tf_op jit(solution)/shard_map/cond/branch_1_fun/ppermute | solution.py:195
  85.9 1.9 %collective-permute-start.8 = (bf16[32,1408]{1,0:T(8,128)(2,1)S(1)}, bf16[32,1408]{1,0:T(8,128)(2,1)S(1)}, u32[]{:S(2)}, u32[]{:S(2)}) collective-permute-start(bf16[32,1408]{1,0:T(8,128)(2,1)S(1)} %dynamic-slice_bitcast_fusion), channel_id=1, source_target_pairs={{0,32},{32,0},{1,33},{33,1},{2,34},{34,2},{3,35},{35,3},{4,36},{36... | collective-permute-start | bytes 270344 | tf_op jit(solution)/shard_map/cond/branch_1_fun/ppermute | solution.py:198
  87.8 7.9 %collective-permute-done.8.refs_6_ = bf16[32,1408]{1,0:T(8,128)(2,1)S(1)} collective-permute-done((bf16[32,1408]{1,0:T(8,128)(2,1)S(1)}, bf16[32,1408]{1,0:T(8,128)(2,1)S(1)}, u32[]{:S(2)}, u32[]{:S(2)}) %collective-permute-start.8) | collective-permute-done | bytes 90144 | tf_op jit(solution)/shard_map/cond/branch_1_fun/ppermute | solution.py:198
  95.8 2.4 %gather_factors.1 = (bf16[8,2,32,896]{3,2,1,0:T(8,128)(2,1)}, bf16[512,128]{1,0:T(8,128)(2,1)S(1)}, bf16[8,2,32,512]{3,2,1,0:T(8,128)(2,1)}) custom-call(s32[1]{0:T(128)} %bitcast.6.c_ref, s32[1]{0:T(128)} %bitcast.7.xl_ref, s32[1]{0:T(128)} %bitcast.8.y_ref, s32[1]{0:T(128)} %bitcast.9.xh_ref, bf16[2,32,1408]{2,1,0:T(8,128)(2,1)S(1)} %get-tuple-element.61.refs_0_, ...), custom_call_target="tpu_custom_call" | custom-call | bytes 3596288 | tf_op jit(solution)/shard_map/cond/branch_1_fun/gather_factors/pallas_call | solution.py:89
  98.5 4.3 %collective-permute-start.13 = (bf16[64,896]{1,0:T(8,128)(2,1)S(1)}, bf16[64,896]{1,0:T(8,128)(2,1)S(1)}, u32[]{:S(2)}, u32[]{:S(2)}) collective-permute-start(bf16[64,896]{1,0:T(8,128)(2,1)S(1)} %pad_maximum_fusion.2), channel_id=1, source_target_pairs={{0,1},{1,0},{2,3},{3,2},{4,5},{5,4},{6,7},{7,6},{8,9},{9,8},{10,11... | collective-permute-start | bytes 344072 | tf_op jit(solution)/shard_map/ppermute | solution.py:233
  103.8 1.6 %convolution_convert_fusion = bf16[512,128]{1,0:T(8,128)(2,1)S(1)} fusion(bf16[512,896]{1,0:T(8,128)(2,1)} %get-tuple-element.130, bf16[64,896]{1,0:T(8,128)(2,1)S(1)} %get-tuple-element.137, bf16[64,896]{1,0:T(8,128)(2,1)S(1)} %get-tuple-element.136), kind=kOutput, calls=%fused_computation.3 | convolution fusion | flops 117964800 | bytes 1277952 | tf_op jit(solution)/shard_map/dot_general | solution.py:234
  105.4 17.4 %all_to_all.15 = bf16[16,64,128]{2,1,0:T(8,128)(2,1)S(1)} all-to-all(bf16[16,64,128]{2,1,0:T(8,128)(2,1)S(1)} %pad_maximum_fusion.1), channel_id=1, replica_groups=mesh['y'=8,'xl'=2,'xh'=2,'zh'=4,'zl'=2,'c'=2] {'y','xl'}, dimensions={0} | all-to-all | bytes 524288 | tf_op jit(solution)/shard_map/all_to_all | solution.py:237
  (30 shorter events, 3.0 us)
Async XLA Ops:
  2.5 11.0 %copy-start = (bf16[1,32,14336]{2,1,0:T(8,128)(2,1)S(1)}, bf16[1,32,14336]{2,1,0:T(8,128)(2,1)}, u32[]{:S(2)}) copy-start(bf16[1,32,14336]{2,1,0:T(8,128)(2,1)} %param.16) | copy-start | bytes 2752516
  2.5 11.0 %copy-start.1 = (bf16[1,32,8192]{2,1,0:T(8,128)(2,1)S(1)}, bf16[1,32,8192]{2,1,0:T(8,128)(2,1)}, u32[]{:S(2)}) copy-start(bf16[1,32,8192]{2,1,0:T(8,128)(2,1)} %param.17) | copy-start | bytes 1572868
  2.5 11.0 %copy-start.2 = (bf16[512,448]{0,1:T(8,128)(2,1)S(1)}, bf16[512,448]{0,1:T(8,128)(2,1)}, u32[]{:S(2)}) copy-start(bf16[512,448]{0,1:T(8,128)(2,1)} %param.13) | copy-start | bytes 1376260
  2.5 11.0 %copy-start.3 = (bf16[128,256]{1,0:T(8,128)(2,1)S(1)}, bf16[128,256]{1,0:T(8,128)(2,1)}, u32[]{:S(2)}) copy-start(bf16[128,256]{1,0:T(8,128)(2,1)} %param.15) | copy-start | bytes 196612
  2.5 46.0 %all-to-all-start = ((bf16[8,64,1024]{2,1,0:T(8,128)(2,1)}), bf16[8,64,1024]{2,1,0:T(8,128)(2,1)S(1)}, u32[]{:S(2)}, u32[]{:S(2)}) async-start(bf16[8,64,1024]{2,1,0:T(8,128)(2,1)} %norm_rows.1), calls=%async_computation | async-start | bytes 2097152 | tf_op jit(solution)/shard_map/all_to_all | solution.py:206
  14.7 27.3 %collective-permute-start = (bf16[896,512]{1,0:T(8,128)(2,1)S(1)}, bf16[896,512]{1,0:T(8,128)(2,1)S(1)}, u32[]{:S(2)}, u32[]{:S(2)}) collective-permute-start(bf16[896,512]{1,0:T(8,128)(2,1)S(1)} %pad_maximum_fusion.mine_ref), channel_id=1, source_target_pairs={{0,16},{16,0},{1,17},{17,1},{2,18},{18,2},{3,19},{19,3},{4,20},{20... | collective-permute-start | bytes 2752520 | tf_op jit(solution)/shard_map/cond/branch_1_fun/ppermute | solution.py:179
  19.4 15.4 %collective-permute-start.1 = (bf16[2,32,1408]{2,1,0:T(8,128)(2,1)S(1)}, bf16[2,32,1408]{2,1,0:T(8,128)(2,1)}, u32[]{:S(2)}, u32[]{:S(2)}) collective-permute-start(bf16[2,32,1408]{2,1,0:T(8,128)(2,1)S(1)} %get-tuple-element.47), channel_id=1, source_target_pairs={{0,192},{16,336},{64,256},{80,400},{128,320},{144,464},{192,384},{... | collective-permute-start | bytes 540680 | tf_op jit(solution)/shard_map/cond/branch_1_fun/ppermute | solution.py:175
  24.7 10.1 %collective-permute-start.2 = (bf16[2,32,1408]{2,1,0:T(8,128)(2,1)S(1)}, bf16[2,32,1408]{2,1,0:T(8,128)(2,1)}, u32[]{:S(2)}, u32[]{:S(2)}) collective-permute-start(bf16[2,32,1408]{2,1,0:T(8,128)(2,1)S(1)} %get-tuple-element.48), channel_id=1, source_target_pairs={{0,384},{16,144},{64,448},{80,208},{128,0},{144,272},{192,64},{208... | collective-permute-start | bytes 540680 | tf_op jit(solution)/shard_map/cond/branch_1_fun/ppermute | solution.py:175
  27.8 14.1 %collective-permute-start.3 = (bf16[2,32,1408]{2,1,0:T(8,128)(2,1)S(1)}, bf16[2,32,1408]{2,1,0:T(8,128)(2,1)}, u32[]{:S(2)}, u32[]{:S(2)}) collective-permute-start(bf16[2,32,1408]{2,1,0:T(8,128)(2,1)S(1)} %get-tuple-element.49), channel_id=1, source_target_pairs={{0,448},{16,80},{64,0},{80,144},{128,64},{144,208},{192,128},{208,... | collective-permute-start | bytes 540680 | tf_op jit(solution)/shard_map/cond/branch_1_fun/ppermute | solution.py:175
  30.2 16.1 %collective-permute-start.4 = (bf16[896,512]{1,0:T(8,128)(2,1)S(1)}, bf16[896,512]{1,0:T(8,128)(2,1)S(1)}, u32[]{:S(2)}, u32[]{:S(2)}) collective-permute-start(bf16[896,512]{1,0:T(8,128)(2,1)S(1)} %pad_maximum_fusion.mine_ref), channel_id=1, source_target_pairs={{0,1},{1,0},{2,3},{3,2},{4,5},{5,4},{6,7},{7,6},{8,9},{9,8},{10,11... | collective-permute-start | bytes 2752520 | tf_op jit(solution)/shard_map/cond/branch_1_fun/ppermute | solution.py:185
  41.9 4.5 %collective-permute-start.5 = (bf16[896,512]{1,0:T(8,128)(2,1)S(1)}, bf16[896,512]{1,0:T(8,128)(2,1)S(1)}, u32[]{:S(2)}, u32[]{:S(2)}) collective-permute-start(bf16[896,512]{1,0:T(8,128)(2,1)S(1)} %collective-permute-done.theirs_ref), channel_id=1, source_target_pairs={{0,1},{1,0},{2,3},{3,2},{4,5},{5,4},{6,7},{7,6},{8,9},{9,8},{10,11... | collective-permute-start | bytes 2752520 | tf_op jit(solution)/shard_map/cond/branch_1_fun/ppermute | solution.py:185
  44.4 4.2 %collective-permute-start.6 = (bf16[128,256]{1,0:T(8,128)(2,1)S(1)}, bf16[128,256]{1,0:T(8,128)(2,1)}, u32[]{:S(2)}, u32[]{:S(2)}) collective-permute-start(bf16[128,256]{1,0:T(8,128)(2,1)S(1)} %get-tuple-element.56), channel_id=1, source_target_pairs={{0,1},{1,0},{2,3},{3,2},{4,5},{5,4},{6,7},{7,6},{8,9},{9,8},{10,11... | collective-permute-start | bytes 196616 | tf_op jit(solution)/shard_map/cond/branch_1_fun/ppermute | solution.py:190
  51.9 15.6 %collective-permute-start.12 = (bf16[4,64,1792]{2,1,0:T(8,128)(2,1)S(1)}, bf16[4,64,1792]{2,1,0:T(8,128)(2,1)S(1)}, u32[]{:S(2)}, u32[]{:S(2)}) collective-permute-start(bf16[4,64,1792]{2,1,0:T(8,128)(2,1)S(1)} %terms.2), channel_id=1, source_target_pairs={{0,2},{1,15},{2,0},{3,5},{4,6},{5,3},{6,4},{7,9},{8,10},{9,7},{10,... | collective-permute-start | bytes 2752520 | tf_op jit(solution)/shard_map/ppermute | solution.py:216
  56.4 13.8 %collective-permute-start.11 = (bf16[2,32,1408]{2,1,0:T(8,128)(2,1)S(1)}, bf16[2,32,1408]{2,1,0:T(8,128)(2,1)S(1)}, u32[]{:S(2)}, u32[]{:S(2)}) collective-permute-start(bf16[2,32,1408]{2,1,0:T(8,128)(2,1)S(1)} %get-tuple-element.117), channel_id=1, source_target_pairs={{0,256},{16,272},{64,320},{80,336},{128,384},{144,400},{192,448},{... | collective-permute-start | bytes 540680 | tf_op jit(solution)/shard_map/ppermute | solution.py:175
  70.3 27.9 %all-to-all-start.1 = ((bf16[4,64,1792]{2,1,0:T(8,128)(2,1)}), bf16[4,64,1792]{2,1,0:T(8,128)(2,1)S(1)}, u32[]{:S(2)}, u32[]{:S(2)}) async-start(bf16[4,64,1792]{2,1,0:T(8,128)(2,1)} %add_terms.1), calls=%async_computation.1 | async-start | bytes 1835008 | tf_op jit(solution)/shard_map/all_to_all | solution.py:223
  76.4 19.4 %collective-permute-start.7 = (bf16[4,32,1408]{2,1,0:T(8,128)(2,1)S(1)}, bf16[4,32,1408]{2,1,0:T(8,128)(2,1)S(1)}, u32[]{:S(2)}, u32[]{:S(2)}) collective-permute-start(bf16[4,32,1408]{2,1,0:T(8,128)(2,1)S(1)} %get-tuple-element.66), channel_id=1, source_target_pairs={{0,32},{32,0},{1,33},{33,1},{2,34},{34,2},{3,35},{35,3},{4,36},{36... | collective-permute-start | bytes 1081352 | tf_op jit(solution)/shard_map/cond/branch_1_fun/ppermute | solution.py:197
  78.6 17.1 %collective-permute-start.10 = (bf16[3,32,1408]{2,1,0:T(8,128)(2,1)S(1)}, bf16[3,32,1408]{2,1,0:T(8,128)(2,1)S(1)}, u32[]{:S(2)}, u32[]{:S(2)}) collective-permute-start(bf16[3,32,1408]{2,1,0:T(8,128)(2,1)S(1)} %get-tuple-element.68), channel_id=1, source_target_pairs={{0,48},{16,32},{32,16},{48,0},{1,49},{17,33},{33,17},{49,1},{2,50}... | collective-permute-start | bytes 811016 | tf_op jit(solution)/shard_map/cond/branch_1_fun/ppermute | solution.py:196
  82.8 13.0 %collective-permute-start.9 = (bf16[3,32,1408]{2,1,0:T(8,128)(2,1)S(1)}, bf16[3,32,1408]{2,1,0:T(8,128)(2,1)S(1)}, u32[]{:S(2)}, u32[]{:S(2)}) collective-permute-start(bf16[3,32,1408]{2,1,0:T(8,128)(2,1)S(1)} %get-tuple-element.67), channel_id=1, source_target_pairs={{0,16},{16,0},{1,17},{17,1},{2,18},{18,2},{3,19},{19,3},{4,20},{20... | collective-permute-start | bytes 811016 | tf_op jit(solution)/shard_map/cond/branch_1_fun/ppermute | solution.py:195
  85.9 9.9 %collective-permute-start.8 = (bf16[32,1408]{1,0:T(8,128)(2,1)S(1)}, bf16[32,1408]{1,0:T(8,128)(2,1)S(1)}, u32[]{:S(2)}, u32[]{:S(2)}) collective-permute-start(bf16[32,1408]{1,0:T(8,128)(2,1)S(1)} %dynamic-slice_bitcast_fusion), channel_id=1, source_target_pairs={{0,32},{32,0},{1,33},{33,1},{2,34},{34,2},{3,35},{35,3},{4,36},{36... | collective-permute-start | bytes 270344 | tf_op jit(solution)/shard_map/cond/branch_1_fun/ppermute | solution.py:198
  98.5 5.2 %collective-permute-start.13 = (bf16[64,896]{1,0:T(8,128)(2,1)S(1)}, bf16[64,896]{1,0:T(8,128)(2,1)S(1)}, u32[]{:S(2)}, u32[]{:S(2)}) collective-permute-start(bf16[64,896]{1,0:T(8,128)(2,1)S(1)} %pad_maximum_fusion.2), channel_id=1, source_target_pairs={{0,1},{1,0},{2,3},{3,2},{4,5},{5,4},{6,7},{7,6},{8,9},{9,8},{10,11... | collective-permute-start | bytes 344072 | tf_op jit(solution)/shard_map/ppermute | solution.py:233

commit v5 on v4

--- a/solution.py
+++ b/solution.py
@@ -13,7 +13,7 @@
 SWAP = ((0, 1), (1, 0))
 RING = 8
 STEPS = RING // 2 + 1
-EARLY = (3, 2, 1)
+EARLY = (2, 3, 1)
 
 
 def away(step, xh):

time: 124 us -> 124 us (level)
    ppermute x1, starting transfers between devices: 4.53 us -> 7.65 us  [on_device(): got = lax.ppermute(give, DEPTH + ('c',), pairs)]
    ppermute x4, waiting for transfers between devices: 9.62 us -> 7.08 us  [along_y(): return lax.ppermute(piece, ('y', 'xh'), pairs)]
    ppermute x1, starting transfers between devices: 4.13 us -> 1.92 us  [beside_sums(): apart = lax.ppermute(apart, ('xl', 'xh'), [(i, 3 - i) for i in range(4)])]
    ppermute x1, starting transfers between devices: 3.09 us -> 4.84 us  [beside_sums(): across = lax.ppermute(across, 'xh', SWAP)]
    ppermute x4, starting transfers between devices: 16.6 us -> 15.2 us  [along_y(): return lax.ppermute(piece, ('y', 'xh'), pairs)]
    ppermute x1, waiting for transfers between devices: 1.94 us -> 3.35 us  [on_device(): got = lax.ppermute(give, DEPTH + ('c',), pairs)]
    ppermute x2, starting transfers between devices: 6.17 us -> 7.42 us  [beside_tokens(): beside = (lax.ppermute(mine, 'c', SWAP), lax.ppermute(theirs, 'c', SWAP))]
  transfers between devices with their start and end apart: 16 -> 16, of which waited for: 7 -> 8; matrix products, arithmetic and copies ran while one was open for 1% -> 1% of each run, Pallas kernels for 8% -> 8%
where the time goes in v5:
time: 124 us; the launch traced here: 123 us
  starting transfers between devices  66.7 us (54%)
  waiting for transfers between devices  19.5 us (16%)
  blocking collectives  17 us (14%)
  Pallas kernels  15.9 us (13%)
  other arithmetic  2.07 us (2%)
  matrix products  1.58 us (1%)
    all_to_all x1, blocking collectives, on_device(): lax.all_to_all(jnp.concatenate(parts, axis=1), CHIPS, 0, 0, tiled=True)  17 us
    ppermute x4, starting transfers between devices, along_y(): return lax.ppermute(piece, ('y', 'xh'), pairs)  15.2 us
    pallas_call x7, Pallas kernels, whole_kernel(): pl.pallas_call(body, out_shape=outputs, in_specs=[pl.BlockSpec(memory_spa...  13.4 us
    all_to_all x1, starting transfers between devices, on_device(): rows = lax.all_to_all(normed, DEPTH, 0, 0, tiled=True)  11 us
    ppermute x1, starting transfers between devices, on_device(): got = lax.ppermute(give, DEPTH + ('c',), pairs)  7.65 us
    ppermute x2, starting transfers between devices, beside_tokens(): beside = (lax.ppermute(mine, 'c', SWAP), lax.ppermute(theirs, 'c', SWAP))  7.42 us
    ppermute x1, waiting for transfers between devices, beside_sums(): lax.ppermute(lax.dynamic_index_in_dim(far, 1 - xl, 0, keepdims=False), 'x...  7.23 us
    ppermute x4, waiting for transfers between devices, along_y(): return lax.ppermute(piece, ('y', 'xh'), pairs)  7.08 us
  transfers between devices with their start and end apart: 16, of which 8 were waited for; matrix products, arithmetic and copies ran while one was open for 1% of the time, Pallas kernels for 8%

profile of v5, /device:TPU:1, one launch (start us, length us, event | category | flops | bytes accessed | tf_op | source)
XLA Modules:
  0.0 123.2 jit_solution(12467060064570714184)
XLA Ops:
  0.0 2.5 %norm_rows.1 = bf16[8,64,1024]{2,1,0:T(8,128)(2,1)} custom-call(s32[1]{0:T(128)} %bitcast.12.core_ref, s32[1]{0:T(128)} %bitcast.13.pair_ref, bf16[128,8192]{1,0:T(8,128)(2,1)} %other_ref.1, bf16[128,8192]{1,0:T(8,128)(2,1)} %other_ref.1, f32[1,8192]{1,0:T(1,128)} %bitcast.27, f32[1,8192]{1,0:T(1,128)} %bitcast.28), custom_call_target="tpu_custom_call" | custom-call | flops 2097152 | bytes 2097152 | tf_op jit(solution)/shard_map/norm_rows/pallas_call | solution.py:45
  2.5 11.0 %all-to-all-start = ((bf16[8,64,1024]{2,1,0:T(8,128)(2,1)}), bf16[8,64,1024]{2,1,0:T(8,128)(2,1)S(1)}, u32[]{:S(2)}, u32[]{:S(2)}) async-start(bf16[8,64,1024]{2,1,0:T(8,128)(2,1)} %norm_rows.1), calls=%async_computation | async-start | bytes 2097152 | tf_op jit(solution)/shard_map/all_to_all | solution.py:206
  13.6 33.3 %conditional.2 = (bf16[1792,1024]{1,0:T(8,128)(2,1)}, bf16[2,32,1408]{2,1,0:T(8,128)(2,1)}, bf16[2,32,1408]{2,1,0:T(8,128)(2,1)}, bf16[2,32,1408]{2,1,0:T(8,128)...) conditional(s32[]{:T(128)} %convert_element_type.19, () %tuple.27, ...), branch_computations={%region_0.0_spmd, %region_1.0_spmd} | conditional | flops 1835008 | bytes 24953168 | solution.py:168
  13.6 1.1 pad_maximum_fusion.mine_ref
  14.7 4.7 %collective-permute-start = (bf16[896,512]{1,0:T(8,128)(2,1)S(1)}, bf16[896,512]{1,0:T(8,128)(2,1)S(1)}, u32[]{:S(2)}, u32[]{:S(2)}) collective-permute-start(bf16[896,512]{1,0:T(8,128)(2,1)S(1)} %pad_maximum_fusion.mine_ref), channel_id=1, source_target_pairs={{0,16},{16,0},{1,17},{17,1},{2,18},{18,2},{3,19},{19,3},{4,20},{20... | collective-permute-start | bytes 2752520 | tf_op jit(solution)/shard_map/cond/branch_1_fun/ppermute | solution.py:179
  19.4 5.9 %collective-permute-start.1 = (bf16[2,32,1408]{2,1,0:T(8,128)(2,1)S(1)}, bf16[2,32,1408]{2,1,0:T(8,128)(2,1)}, u32[]{:S(2)}, u32[]{:S(2)}) collective-permute-start(bf16[2,32,1408]{2,1,0:T(8,128)(2,1)S(1)} %get-tuple-element.47), channel_id=1, source_target_pairs={{0,384},{16,144},{64,448},{80,208},{128,0},{144,272},{192,64},{208... | collective-permute-start | bytes 540680 | tf_op jit(solution)/shard_map/cond/branch_1_fun/ppermute | solution.py:175
  25.3 1.9 %collective-permute-start.2 = (bf16[2,32,1408]{2,1,0:T(8,128)(2,1)S(1)}, bf16[2,32,1408]{2,1,0:T(8,128)(2,1)}, u32[]{:S(2)}, u32[]{:S(2)}) collective-permute-start(bf16[2,32,1408]{2,1,0:T(8,128)(2,1)S(1)} %get-tuple-element.48), channel_id=1, source_target_pairs={{0,192},{16,336},{64,256},{80,400},{128,320},{144,464},{192,384},{... | collective-permute-start | bytes 540680 | tf_op jit(solution)/shard_map/cond/branch_1_fun/ppermute | solution.py:175
  27.2 3.0 %collective-permute-start.3 = (bf16[2,32,1408]{2,1,0:T(8,128)(2,1)S(1)}, bf16[2,32,1408]{2,1,0:T(8,128)(2,1)}, u32[]{:S(2)}, u32[]{:S(2)}) collective-permute-start(bf16[2,32,1408]{2,1,0:T(8,128)(2,1)S(1)} %get-tuple-element.49), channel_id=1, source_target_pairs={{0,448},{16,80},{64,0},{80,144},{128,64},{144,208},{192,128},{208,... | collective-permute-start | bytes 540680 | tf_op jit(solution)/shard_map/cond/branch_1_fun/ppermute | solution.py:175
  30.2 3.7 %collective-permute-start.4 = (bf16[896,512]{1,0:T(8,128)(2,1)S(1)}, bf16[896,512]{1,0:T(8,128)(2,1)S(1)}, u32[]{:S(2)}, u32[]{:S(2)}) collective-permute-start(bf16[896,512]{1,0:T(8,128)(2,1)S(1)} %pad_maximum_fusion.mine_ref), channel_id=1, source_target_pairs={{0,1},{1,0},{2,3},{3,2},{4,5},{5,4},{6,7},{7,6},{8,9},{9,8},{10,11... | collective-permute-start | bytes 2752520 | tf_op jit(solution)/shard_map/cond/branch_1_fun/ppermute | solution.py:185
  34.0 4.7 %collective-permute-done.2 = bf16[2,32,1408]{2,1,0:T(8,128)(2,1)} collective-permute-done((bf16[2,32,1408]{2,1,0:T(8,128)(2,1)S(1)}, bf16[2,32,1408]{2,1,0:T(8,128)(2,1)}, u32[]{:S(2)}, u32[]{:S(2)}) %collective-permute-start.2) | collective-permute-done | bytes 180256 | tf_op jit(solution)/shard_map/cond/branch_1_fun/ppermute | solution.py:175
  39.0 3.7 %collective-permute-start.5 = (bf16[896,512]{1,0:T(8,128)(2,1)S(1)}, bf16[896,512]{1,0:T(8,128)(2,1)S(1)}, u32[]{:S(2)}, u32[]{:S(2)}) collective-permute-start(bf16[896,512]{1,0:T(8,128)(2,1)S(1)} %collective-permute-done.theirs_ref), channel_id=1, source_target_pairs={{0,1},{1,0},{2,3},{3,2},{4,5},{5,4},{6,7},{7,6},{8,9},{9,8},{10,11... | collective-permute-start | bytes 2752520 | tf_op jit(solution)/shard_map/cond/branch_1_fun/ppermute | solution.py:185
  42.8 1.9 %collective-permute-start.6 = (bf16[128,256]{1,0:T(8,128)(2,1)S(1)}, bf16[128,256]{1,0:T(8,128)(2,1)}, u32[]{:S(2)}, u32[]{:S(2)}) collective-permute-start(bf16[128,256]{1,0:T(8,128)(2,1)S(1)} %get-tuple-element.56), channel_id=1, source_target_pairs={{0,1},{1,0},{2,3},{3,2},{4,5},{5,4},{6,7},{7,6},{8,9},{9,8},{10,11... | collective-permute-start | bytes 196616 | tf_op jit(solution)/shard_map/cond/branch_1_fun/ppermute | solution.py:190
  44.8 2.1 %weights.1 = bf16[1792,1024]{1,0:T(8,128)(2,1)} custom-call(bf16[896,512]{1,0:T(8,128)(2,1)S(1)} %pad_maximum_fusion.mine_ref, bf16[896,512]{1,0:T(8,128)(2,1)S(1)} %collective-permute-done.theirs_ref, bf16[896,512]{1,0:T(8,128)(2,1)S(1)} %collective-permute-done.4.beside_ref, bf16[896,512]{1,0:T(8,128)(2,1)S(1)} %collective-permute-done.5.across_ref), custom_call_target="tpu_custom_call" | custom-call | bytes 7340032 | tf_op jit(solution)/shard_map/cond/branch_1_fun/weights/pallas_call | solution.py:89
  46.9 3.3 %terms.2 = bf16[4,64,1792]{2,1,0:T(8,128)(2,1)S(1)} custom-call(s32[1]{0:T(128)} %bitcast.15.parity_ref, bf16[8,64,1024]{2,1,0:T(8,128)(2,1)S(1)} %all-to-all-done.rows_ref, bf16[1792,1024]{1,0:T(8,128)(2,1)} %get-tuple-element.111.weight_ref), custom_call_target="tpu_custom_call" | custom-call | flops 939524096 | bytes 5636096 | tf_op jit(solution)/shard_map/terms/pallas_call | solution.py:89
  50.2 7.6 %collective-permute-start.12 = (bf16[4,64,1792]{2,1,0:T(8,128)(2,1)S(1)}, bf16[4,64,1792]{2,1,0:T(8,128)(2,1)S(1)}, u32[]{:S(2)}, u32[]{:S(2)}) collective-permute-start(bf16[4,64,1792]{2,1,0:T(8,128)(2,1)S(1)} %terms.2), channel_id=1, source_target_pairs={{0,2},{1,15},{2,0},{3,5},{4,6},{5,3},{6,4},{7,9},{8,10},{9,7},{10,... | collective-permute-start | bytes 2752520 | tf_op jit(solution)/shard_map/ppermute | solution.py:216
  57.9 4.4 %collective-permute-start.11 = (bf16[2,32,1408]{2,1,0:T(8,128)(2,1)S(1)}, bf16[2,32,1408]{2,1,0:T(8,128)(2,1)S(1)}, u32[]{:S(2)}, u32[]{:S(2)}) collective-permute-start(bf16[2,32,1408]{2,1,0:T(8,128)(2,1)S(1)} %get-tuple-element.117), channel_id=1, source_target_pairs={{0,256},{16,272},{64,320},{80,336},{128,384},{144,400},{192,448},{... | collective-permute-start | bytes 540680 | tf_op jit(solution)/shard_map/ppermute | solution.py:175
  62.3 3.3 %terms.3.keep_ref = f32[4,64,1792]{2,1,0:T(8,128)S(1)} custom-call(s32[1]{0:T(128)} %bitcast.16.parity_ref, bf16[8,64,1024]{2,1,0:T(8,128)(2,1)S(1)} %all-to-all-done.rows_ref, bf16[1792,1024]{1,0:T(8,128)(2,1)} %get-tuple-element.111.weight_ref), custom_call_target="tpu_custom_call" | custom-call | flops 939524096 | bytes 6553600 | tf_op jit(solution)/shard_map/terms/pallas_call | solution.py:89
  65.6 3.4 %collective-permute-done.12.got_ref = bf16[4,64,1792]{2,1,0:T(8,128)(2,1)S(1)} collective-permute-done((bf16[4,64,1792]{2,1,0:T(8,128)(2,1)S(1)}, bf16[4,64,1792]{2,1,0:T(8,128)(2,1)S(1)}, u32[]{:S(2)}, u32[]{:S(2)}) %collective-permute-start.12) | collective-permute-done | bytes 917536 | tf_op jit(solution)/shard_map/ppermute | solution.py:216
  69.0 1.1 add_terms.1
  70.1 2.4 %collective-permute-done.11 = bf16[2,32,1408]{2,1,0:T(8,128)(2,1)S(1)} collective-permute-done((bf16[2,32,1408]{2,1,0:T(8,128)(2,1)S(1)}, bf16[2,32,1408]{2,1,0:T(8,128)(2,1)S(1)}, u32[]{:S(2)}, u32[]{:S(2)}) %collective-permute-start.11) | collective-permute-done | bytes 180256 | tf_op jit(solution)/shard_map/ppermute | solution.py:175
  72.5 4.2 %all-to-all-start.1 = ((bf16[4,64,1792]{2,1,0:T(8,128)(2,1)}), bf16[4,64,1792]{2,1,0:T(8,128)(2,1)S(1)}, u32[]{:S(2)}, u32[]{:S(2)}) async-start(bf16[4,64,1792]{2,1,0:T(8,128)(2,1)} %add_terms.1), calls=%async_computation.1 | async-start | bytes 1835008 | tf_op jit(solution)/shard_map/all_to_all | solution.py:223
  76.7 22.0 %conditional.3 = (bf16[512,896]{1,0:T(8,128)(2,1)}, bf16[512,128]{1,0:T(8,128)(2,1)S(1)}) conditional(s32[]{:T(128)} %convert_element_type.19, () %tuple.33, (s32[]{:T(128)}, s32[]{:T(128)}, s32[]{:T(128)}, s32[]{:T(128)}, bf16[2,32,1408]{2,1,0:T(8,128)(2,1)S(1)}, /*index=5*/bf16[2,32,1408]{2,1,0:T(8,128)(2,1)}, bf16[2,32,1408]{2,1,0:T(8,128)(2,1)}, ...), branch_computations={%region_3.4_spmd, %region_4.5_spmd} | conditional | flops 4 | bytes 9363682 | solution.py:168
  76.7 1.2 give.1
  77.9 2.2 %collective-permute-start.7 = (bf16[4,32,1408]{2,1,0:T(8,128)(2,1)S(1)}, bf16[4,32,1408]{2,1,0:T(8,128)(2,1)S(1)}, u32[]{:S(2)}, u32[]{:S(2)}) collective-permute-start(bf16[4,32,1408]{2,1,0:T(8,128)(2,1)S(1)} %get-tuple-element.66), channel_id=1, source_target_pairs={{0,32},{32,0},{1,33},{33,1},{2,34},{34,2},{3,35},{35,3},{4,36},{36... | collective-permute-start | bytes 1081352 | tf_op jit(solution)/shard_map/cond/branch_1_fun/ppermute | solution.py:197
  80.1 1.9 %collective-permute-start.10 = (bf16[3,32,1408]{2,1,0:T(8,128)(2,1)S(1)}, bf16[3,32,1408]{2,1,0:T(8,128)(2,1)S(1)}, u32[]{:S(2)}, u32[]{:S(2)}) collective-permute-start(bf16[3,32,1408]{2,1,0:T(8,128)(2,1)S(1)} %get-tuple-element.68), channel_id=1, source_target_pairs={{0,48},{16,32},{32,16},{48,0},{1,49},{17,33},{33,17},{49,1},{2,50}... | collective-permute-start | bytes 811016 | tf_op jit(solution)/shard_map/cond/branch_1_fun/ppermute | solution.py:196
  82.0 4.8 %collective-permute-start.9 = (bf16[3,32,1408]{2,1,0:T(8,128)(2,1)S(1)}, bf16[3,32,1408]{2,1,0:T(8,128)(2,1)S(1)}, u32[]{:S(2)}, u32[]{:S(2)}) collective-permute-start(bf16[3,32,1408]{2,1,0:T(8,128)(2,1)S(1)} %get-tuple-element.67), channel_id=1, source_target_pairs={{0,16},{16,0},{1,17},{17,1},{2,18},{18,2},{3,19},{19,3},{4,20},{20... | collective-permute-start | bytes 811016 | tf_op jit(solution)/shard_map/cond/branch_1_fun/ppermute | solution.py:195
  86.9 2.2 %collective-permute-start.8 = (bf16[32,1408]{1,0:T(8,128)(2,1)S(1)}, bf16[32,1408]{1,0:T(8,128)(2,1)S(1)}, u32[]{:S(2)}, u32[]{:S(2)}) collective-permute-start(bf16[32,1408]{1,0:T(8,128)(2,1)S(1)} %dynamic-slice_bitcast_fusion), channel_id=1, source_target_pairs={{0,32},{32,0},{1,33},{33,1},{2,34},{34,2},{3,35},{35,3},{4,36},{36... | collective-permute-start | bytes 270344 | tf_op jit(solution)/shard_map/cond/branch_1_fun/ppermute | solution.py:198
  89.1 7.2 %collective-permute-done.8.refs_6_ = bf16[32,1408]{1,0:T(8,128)(2,1)S(1)} collective-permute-done((bf16[32,1408]{1,0:T(8,128)(2,1)S(1)}, bf16[32,1408]{1,0:T(8,128)(2,1)S(1)}, u32[]{:S(2)}, u32[]{:S(2)}) %collective-permute-start.8) | collective-permute-done | bytes 90144 | tf_op jit(solution)/shard_map/cond/branch_1_fun/ppermute | solution.py:198
  96.4 2.4 %gather_factors.1 = (bf16[8,2,32,896]{3,2,1,0:T(8,128)(2,1)}, bf16[512,128]{1,0:T(8,128)(2,1)S(1)}, bf16[8,2,32,512]{3,2,1,0:T(8,128)(2,1)}) custom-call(s32[1]{0:T(128)} %bitcast.6.c_ref, s32[1]{0:T(128)} %bitcast.7.xl_ref, s32[1]{0:T(128)} %bitcast.8.y_ref, s32[1]{0:T(128)} %bitcast.9.xh_ref, bf16[2,32,1408]{2,1,0:T(8,128)(2,1)S(1)} %get-tuple-element.61.refs_0_, ...), custom_call_target="tpu_custom_call" | custom-call | bytes 3596288 | tf_op jit(solution)/shard_map/cond/branch_1_fun/gather_factors/pallas_call | solution.py:89
  99.5 3.5 %collective-permute-start.13 = (bf16[64,896]{1,0:T(8,128)(2,1)S(1)}, bf16[64,896]{1,0:T(8,128)(2,1)S(1)}, u32[]{:S(2)}, u32[]{:S(2)}) collective-permute-start(bf16[64,896]{1,0:T(8,128)(2,1)S(1)} %pad_maximum_fusion.2), channel_id=1, source_target_pairs={{0,1},{1,0},{2,3},{3,2},{4,5},{5,4},{6,7},{7,6},{8,9},{9,8},{10,11... | collective-permute-start | bytes 344072 | tf_op jit(solution)/shard_map/ppermute | solution.py:233
  104.0 1.6 %convolution_convert_fusion = bf16[512,128]{1,0:T(8,128)(2,1)S(1)} fusion(bf16[512,896]{1,0:T(8,128)(2,1)} %get-tuple-element.130, bf16[64,896]{1,0:T(8,128)(2,1)S(1)} %get-tuple-element.137, bf16[64,896]{1,0:T(8,128)(2,1)S(1)} %get-tuple-element.136), kind=kOutput, calls=%fused_computation.3 | convolution fusion | flops 117964800 | bytes 1277952 | tf_op jit(solution)/shard_map/dot_general | solution.py:234
  105.6 17.0 %all_to_all.15 = bf16[16,64,128]{2,1,0:T(8,128)(2,1)S(1)} all-to-all(bf16[16,64,128]{2,1,0:T(8,128)(2,1)S(1)} %pad_maximum_fusion.1), channel_id=1, replica_groups=mesh['y'=8,'xl'=2,'xh'=2,'zh'=4,'zl'=2,'c'=2] {'y','xl'}, dimensions={0} | all-to-all | bytes 524288 | tf_op jit(solution)/shard_map/all_to_all | solution.py:237
  (30 shorter events, 3.0 us)
Async XLA Ops:
  2.5 11.0 %copy-start = (bf16[1,32,14336]{2,1,0:T(8,128)(2,1)S(1)}, bf16[1,32,14336]{2,1,0:T(8,128)(2,1)}, u32[]{:S(2)}) copy-start(bf16[1,32,14336]{2,1,0:T(8,128)(2,1)} %param.16) | copy-start | bytes 2752516
  2.5 11.0 %copy-start.1 = (bf16[1,32,8192]{2,1,0:T(8,128)(2,1)S(1)}, bf16[1,32,8192]{2,1,0:T(8,128)(2,1)}, u32[]{:S(2)}) copy-start(bf16[1,32,8192]{2,1,0:T(8,128)(2,1)} %param.17) | copy-start | bytes 1572868
  2.5 11.0 %copy-start.2 = (bf16[512,448]{0,1:T(8,128)(2,1)S(1)}, bf16[512,448]{0,1:T(8,128)(2,1)}, u32[]{:S(2)}) copy-start(bf16[512,448]{0,1:T(8,128)(2,1)} %param.13) | copy-start | bytes 1376260
  2.5 11.0 %copy-start.3 = (bf16[128,256]{1,0:T(8,128)(2,1)S(1)}, bf16[128,256]{1,0:T(8,128)(2,1)}, u32[]{:S(2)}) copy-start(bf16[128,256]{1,0:T(8,128)(2,1)} %param.15) | copy-start | bytes 196612
  2.5 44.4 %all-to-all-start = ((bf16[8,64,1024]{2,1,0:T(8,128)(2,1)}), bf16[8,64,1024]{2,1,0:T(8,128)(2,1)S(1)}, u32[]{:S(2)}, u32[]{:S(2)}) async-start(bf16[8,64,1024]{2,1,0:T(8,128)(2,1)} %norm_rows.1), calls=%async_computation | async-start | bytes 2097152 | tf_op jit(solution)/shard_map/all_to_all | solution.py:206
  14.7 24.3 %collective-permute-start = (bf16[896,512]{1,0:T(8,128)(2,1)S(1)}, bf16[896,512]{1,0:T(8,128)(2,1)S(1)}, u32[]{:S(2)}, u32[]{:S(2)}) collective-permute-start(bf16[896,512]{1,0:T(8,128)(2,1)S(1)} %pad_maximum_fusion.mine_ref), channel_id=1, source_target_pairs={{0,16},{16,0},{1,17},{17,1},{2,18},{18,2},{3,19},{19,3},{4,20},{20... | collective-permute-start | bytes 2752520 | tf_op jit(solution)/shard_map/cond/branch_1_fun/ppermute | solution.py:179
  19.4 14.5 %collective-permute-start.1 = (bf16[2,32,1408]{2,1,0:T(8,128)(2,1)S(1)}, bf16[2,32,1408]{2,1,0:T(8,128)(2,1)}, u32[]{:S(2)}, u32[]{:S(2)}) collective-permute-start(bf16[2,32,1408]{2,1,0:T(8,128)(2,1)S(1)} %get-tuple-element.47), channel_id=1, source_target_pairs={{0,384},{16,144},{64,448},{80,208},{128,0},{144,272},{192,64},{208... | collective-permute-start | bytes 540680 | tf_op jit(solution)/shard_map/cond/branch_1_fun/ppermute | solution.py:175
  25.3 13.3 %collective-permute-start.2 = (bf16[2,32,1408]{2,1,0:T(8,128)(2,1)S(1)}, bf16[2,32,1408]{2,1,0:T(8,128)(2,1)}, u32[]{:S(2)}, u32[]{:S(2)}) collective-permute-start(bf16[2,32,1408]{2,1,0:T(8,128)(2,1)S(1)} %get-tuple-element.48), channel_id=1, source_target_pairs={{0,192},{16,336},{64,256},{80,400},{128,320},{144,464},{192,384},{... | collective-permute-start | bytes 540680 | tf_op jit(solution)/shard_map/cond/branch_1_fun/ppermute | solution.py:175
  27.2 11.4 %collective-permute-start.3 = (bf16[2,32,1408]{2,1,0:T(8,128)(2,1)S(1)}, bf16[2,32,1408]{2,1,0:T(8,128)(2,1)}, u32[]{:S(2)}, u32[]{:S(2)}) collective-permute-start(bf16[2,32,1408]{2,1,0:T(8,128)(2,1)S(1)} %get-tuple-element.49), channel_id=1, source_target_pairs={{0,448},{16,80},{64,0},{80,144},{128,64},{144,208},{192,128},{208,... | collective-permute-start | bytes 540680 | tf_op jit(solution)/shard_map/cond/branch_1_fun/ppermute | solution.py:175
  30.2 14.5 %collective-permute-start.4 = (bf16[896,512]{1,0:T(8,128)(2,1)S(1)}, bf16[896,512]{1,0:T(8,128)(2,1)S(1)}, u32[]{:S(2)}, u32[]{:S(2)}) collective-permute-start(bf16[896,512]{1,0:T(8,128)(2,1)S(1)} %pad_maximum_fusion.mine_ref), channel_id=1, source_target_pairs={{0,1},{1,0},{2,3},{3,2},{4,5},{5,4},{6,7},{7,6},{8,9},{9,8},{10,11... | collective-permute-start | bytes 2752520 | tf_op jit(solution)/shard_map/cond/branch_1_fun/ppermute | solution.py:185
  39.0 5.8 %collective-permute-start.5 = (bf16[896,512]{1,0:T(8,128)(2,1)S(1)}, bf16[896,512]{1,0:T(8,128)(2,1)S(1)}, u32[]{:S(2)}, u32[]{:S(2)}) collective-permute-start(bf16[896,512]{1,0:T(8,128)(2,1)S(1)} %collective-permute-done.theirs_ref), channel_id=1, source_target_pairs={{0,1},{1,0},{2,3},{3,2},{4,5},{5,4},{6,7},{7,6},{8,9},{9,8},{10,11... | collective-permute-start | bytes 2752520 | tf_op jit(solution)/shard_map/cond/branch_1_fun/ppermute | solution.py:185
  42.8 4.2 %collective-permute-start.6 = (bf16[128,256]{1,0:T(8,128)(2,1)S(1)}, bf16[128,256]{1,0:T(8,128)(2,1)}, u32[]{:S(2)}, u32[]{:S(2)}) collective-permute-start(bf16[128,256]{1,0:T(8,128)(2,1)S(1)} %get-tuple-element.56), channel_id=1, source_target_pairs={{0,1},{1,0},{2,3},{3,2},{4,5},{5,4},{6,7},{7,6},{8,9},{9,8},{10,11... | collective-permute-start | bytes 196616 | tf_op jit(solution)/shard_map/cond/branch_1_fun/ppermute | solution.py:190
  50.2 18.7 %collective-permute-start.12 = (bf16[4,64,1792]{2,1,0:T(8,128)(2,1)S(1)}, bf16[4,64,1792]{2,1,0:T(8,128)(2,1)S(1)}, u32[]{:S(2)}, u32[]{:S(2)}) collective-permute-start(bf16[4,64,1792]{2,1,0:T(8,128)(2,1)S(1)} %terms.2), channel_id=1, source_target_pairs={{0,2},{1,15},{2,0},{3,5},{4,6},{5,3},{6,4},{7,9},{8,10},{9,7},{10,... | collective-permute-start | bytes 2752520 | tf_op jit(solution)/shard_map/ppermute | solution.py:216
  57.9 14.6 %collective-permute-start.11 = (bf16[2,32,1408]{2,1,0:T(8,128)(2,1)S(1)}, bf16[2,32,1408]{2,1,0:T(8,128)(2,1)S(1)}, u32[]{:S(2)}, u32[]{:S(2)}) collective-permute-start(bf16[2,32,1408]{2,1,0:T(8,128)(2,1)S(1)} %get-tuple-element.117), channel_id=1, source_target_pairs={{0,256},{16,272},{64,320},{80,336},{128,384},{144,400},{192,448},{... | collective-permute-start | bytes 540680 | tf_op jit(solution)/shard_map/ppermute | solution.py:175
  72.5 26.6 %all-to-all-start.1 = ((bf16[4,64,1792]{2,1,0:T(8,128)(2,1)}), bf16[4,64,1792]{2,1,0:T(8,128)(2,1)S(1)}, u32[]{:S(2)}, u32[]{:S(2)}) async-start(bf16[4,64,1792]{2,1,0:T(8,128)(2,1)} %add_terms.1), calls=%async_computation.1 | async-start | bytes 1835008 | tf_op jit(solution)/shard_map/all_to_all | solution.py:223
  77.9 18.5 %collective-permute-start.7 = (bf16[4,32,1408]{2,1,0:T(8,128)(2,1)S(1)}, bf16[4,32,1408]{2,1,0:T(8,128)(2,1)S(1)}, u32[]{:S(2)}, u32[]{:S(2)}) collective-permute-start(bf16[4,32,1408]{2,1,0:T(8,128)(2,1)S(1)} %get-tuple-element.66), channel_id=1, source_target_pairs={{0,32},{32,0},{1,33},{33,1},{2,34},{34,2},{3,35},{35,3},{4,36},{36... | collective-permute-start | bytes 1081352 | tf_op jit(solution)/shard_map/cond/branch_1_fun/ppermute | solution.py:197
  80.1 16.3 %collective-permute-start.10 = (bf16[3,32,1408]{2,1,0:T(8,128)(2,1)S(1)}, bf16[3,32,1408]{2,1,0:T(8,128)(2,1)S(1)}, u32[]{:S(2)}, u32[]{:S(2)}) collective-permute-start(bf16[3,32,1408]{2,1,0:T(8,128)(2,1)S(1)} %get-tuple-element.68), channel_id=1, source_target_pairs={{0,48},{16,32},{32,16},{48,0},{1,49},{17,33},{33,17},{49,1},{2,50}... | collective-permute-start | bytes 811016 | tf_op jit(solution)/shard_map/cond/branch_1_fun/ppermute | solution.py:196
  82.0 14.3 %collective-permute-start.9 = (bf16[3,32,1408]{2,1,0:T(8,128)(2,1)S(1)}, bf16[3,32,1408]{2,1,0:T(8,128)(2,1)S(1)}, u32[]{:S(2)}, u32[]{:S(2)}) collective-permute-start(bf16[3,32,1408]{2,1,0:T(8,128)(2,1)S(1)} %get-tuple-element.67), channel_id=1, source_target_pairs={{0,16},{16,0},{1,17},{17,1},{2,18},{18,2},{3,19},{19,3},{4,20},{20... | collective-permute-start | bytes 811016 | tf_op jit(solution)/shard_map/cond/branch_1_fun/ppermute | solution.py:195
  86.9 9.5 %collective-permute-start.8 = (bf16[32,1408]{1,0:T(8,128)(2,1)S(1)}, bf16[32,1408]{1,0:T(8,128)(2,1)S(1)}, u32[]{:S(2)}, u32[]{:S(2)}) collective-permute-start(bf16[32,1408]{1,0:T(8,128)(2,1)S(1)} %dynamic-slice_bitcast_fusion), channel_id=1, source_target_pairs={{0,32},{32,0},{1,33},{33,1},{2,34},{34,2},{3,35},{35,3},{4,36},{36... | collective-permute-start | bytes 270344 | tf_op jit(solution)/shard_map/cond/branch_1_fun/ppermute | solution.py:198
  99.5 4.5 %collective-permute-start.13 = (bf16[64,896]{1,0:T(8,128)(2,1)S(1)}, bf16[64,896]{1,0:T(8,128)(2,1)S(1)}, u32[]{:S(2)}, u32[]{:S(2)}) collective-permute-start(bf16[64,896]{1,0:T(8,128)(2,1)S(1)} %pad_maximum_fusion.2), channel_id=1, source_target_pairs={{0,1},{1,0},{2,3},{3,2},{4,5},{5,4},{6,7},{7,6},{8,9},{9,8},{10,11... | collective-permute-start | bytes 344072 | tf_op jit(solution)/shard_map/ppermute | solution.py:233

commit v6 on v5

--- a/solution.py
+++ b/solution.py
@@ -62,25 +62,40 @@
     )(core.reshape(1), pair.reshape(1), residual, residual, gain, gain)
 
 
-def term_kernel(parity_ref, rows_ref, weight_ref, out_ref):
+def term_kernel(parity_ref, rows_ref, weight_ref, beside_ref, out_ref, beside_vmem, sem):
+    copy = pltpu.make_async_copy(beside_ref, beside_vmem, sem)
+    copy.start()
     peers, half, width = rows_ref.shape
     rows = jnp.concatenate([rows_ref[2 * i + parity_ref[0]] for i in range(peers // 2)], axis=0)
-    cols = weight_ref.shape[0] // 2
-    for core in range(2):
-        at = slice(core * cols, (core + 1) * cols)
-        total = lax.dot_general(rows, weight_ref[at], (((1,), (1,)), ((), ())), preferred_element_type=jnp.float32)
-        out_ref[:, :, at] = total.astype(out_ref.dtype).reshape(peers // 2, half, cols)
-
-
-def terms_of(rows, weight, parity, kind):
+    cols = weight_ref.shape[0]
+    for core, ref in enumerate((weight_ref, beside_vmem)):
+        if core:
+            copy.wait()
+        total = lax.dot_general(rows, ref[...], (((1,), (1,)), ((), ())), preferred_element_type=jnp.float32)
+        total = total.astype(out_ref.dtype).reshape(peers // 2, half, cols)
+        out_ref[:, :, core * cols : (core + 1) * cols] = total
+
+
+def terms_of(rows, weights, parity):
     peers, half, width = rows.shape
-    cols = weight.shape[0]
-    shape = jax.ShapeDtypeStruct((peers // 2, half, cols), kind)
-    return whole_kernel(term_kernel, (parity,), (rows, weight), [shape], "terms", peers * half * width * cols)[0]
+    cols = weights[0].shape[0]
+    vmem = pl.BlockSpec(memory_space=pltpu.VMEM)
+    return pl.pallas_call(
+        term_kernel,
+        out_shape=jax.ShapeDtypeStruct((peers // 2, half, 2 * cols), jnp.bfloat16),
+        in_specs=[pl.BlockSpec(memory_space=pltpu.SMEM), vmem, vmem, pl.BlockSpec(memory_space=pl.ANY)],
+        out_specs=vmem,
+        scratch_shapes=[pltpu.VMEM(weights[1].shape, jnp.bfloat16), pltpu.SemaphoreType.DMA(())],
+        compiler_params=pltpu.CompilerParams(vmem_limit_bytes=24 << 20),
+        cost_estimate=pl.CostEstimate(
+            flops=2 * peers * half * width * cols, bytes_accessed=6 * peers * half * width, transcendentals=0
+        ),
+        name="terms",
+    )(parity.reshape(1), rows, *weights)
 
 
 def add_kernel(keep_ref, got_ref, out_ref):
-    out_ref[...] = (keep_ref[...] + got_ref[...].astype(jnp.float32)).astype(out_ref.dtype)
+    out_ref[...] = (keep_ref[...].astype(jnp.float32) + got_ref[...].astype(jnp.float32)).astype(out_ref.dtype)
 
 
 def whole_kernel(body, scalars, inputs, outputs, name, flops=0):
@@ -97,11 +112,10 @@
     )(*(v.reshape(1) for v in scalars), *inputs)
 
 
-def weight_kernel(mine_ref, theirs_ref, beside_ref, across_ref, out_ref):
-    cols, depth = mine_ref.shape
-    for row, refs in enumerate(((mine_ref, theirs_ref), (beside_ref, across_ref))):
-        for col, ref in enumerate(refs):
-            out_ref[row * cols : (row + 1) * cols, col * depth : (col + 1) * depth] = ref[...]
+def weight_kernel(own_ref, partner_ref, out_ref):
+    depth = own_ref.shape[1]
+    out_ref[:, :depth] = own_ref[...]
+    out_ref[:, depth:] = partner_ref[...]
 
 
 def pack_kernel(y_ref, xh_ref, left_ref, right_ref, *out_refs):
@@ -183,11 +197,10 @@
         early = tuple(along_y(pieces[step], step) for step in EARLY)
         theirs, early = lax.optimization_barrier((theirs, early))
         beside = (lax.ppermute(mine, "c", SWAP), lax.ppermute(theirs, "c", SWAP))
-        (weight,) = whole_kernel(
-            weight_kernel, (), (mine, theirs, *beside), [like(4 * cols, 2 * gate_weight.shape[0])], "weights"
-        )
+        shape = like(2 * cols, 2 * gate_weight.shape[0])
+        weights = [whole_kernel(weight_kernel, (), pair, [shape], "weights")[0] for pair in ((mine, theirs), beside)]
         late = (pieces[0], pieces[STEPS - 1])
-        return weight, early, late, lax.ppermute(out_grad, "c", SWAP)
+        return weights, early, late, lax.ppermute(out_grad, "c", SWAP)
 
     def beside_sums(near, far, out_grad, beside_grad):
         pieces = [like(STEPS - 1, rank, packed)] + [like(STEPS - 2, rank, packed)] * 2
@@ -204,9 +217,9 @@
     normed = normed_by_peer(residual, norm_gain, c, xh, peers)
     inputs, normed = lax.optimization_barrier(((gate_weight, up_weight, out_grad, left_factor, right_factor), normed))
     rows = lax.all_to_all(normed, DEPTH, 0, 0, tiled=True)
-    weight, early, late, beside_grad = fenced(beside_tokens, *inputs)
-
-    give = terms_of(rows, weight, 1 - zl, jnp.bfloat16)
+    weights, early, late, beside_grad = fenced(beside_tokens, *inputs)
+
+    give = terms_of(rows, weights, 1 - zl)
     give, rows = lax.optimization_barrier((give, rows))
     pairs = []
     for z in range(peers):
@@ -214,7 +227,7 @@
             side = 1 if z % 2 == core else -1
             pairs.append((z * 2 + core, (z + side) % peers * 2 + core))
     got = lax.ppermute(give, DEPTH + ("c",), pairs)
-    keep = terms_of(rows, weight, zl, jnp.float32)
+    keep = terms_of(rows, weights, zl)
     late, give = lax.optimization_barrier((late, give))
     far = along_y(late[1], STEPS - 1)
     near = [late[0]] + [early[EARLY.index(step)] for step in range(1, STEPS - 1)]

time: 124 us -> 124 us (level)
    pallas_call x7 -> x6, Pallas kernels: 13.4 us -> 6.76 us  [whole_kernel(): pl.pallas_call(body, out_shape=outputs, in_specs=[pl.BlockSpec(memory_spa...]
    pallas_call x0 -> x2, Pallas kernels: none -> 5.6 us  [terms_of(): pl.pallas_call(term_kernel, out_shape=jax.ShapeDtypeStruct((peers // 2, h...]
  transfers between devices with their start and end apart: 16 -> 16, of which waited for: 8 -> 6; matrix products, arithmetic and copies ran while one was open for 1% -> 2% of each run, Pallas kernels for 8% -> 8%
where the time goes in v6:
time: 124 us
  starting transfers between devices  65.8 us (53%)
  waiting for transfers between devices  20 us (16%)
  blocking collectives  17.8 us (14%)
  Pallas kernels  14.8 us (12%)
  other arithmetic  2.31 us (2%)
  matrix products  1.58 us (1%)
    all_to_all x1, blocking collectives, on_device(): lax.all_to_all(jnp.concatenate(parts, axis=1), CHIPS, 0, 0, tiled=True)  17.8 us
    ppermute x4, starting transfers between devices, along_y(): return lax.ppermute(piece, ('y', 'xh'), pairs)  14.8 us
    all_to_all x1, starting transfers between devices, on_device(): rows = lax.all_to_all(normed, DEPTH, 0, 0, tiled=True)  11 us
    ppermute x1, starting transfers between devices, on_device(): got = lax.ppermute(give, DEPTH + ('c',), pairs)  8.29 us
    ppermute x4, waiting for transfers between devices, along_y(): return lax.ppermute(piece, ('y', 'xh'), pairs)  7.36 us
    ppermute x2, starting transfers between devices, beside_tokens(): beside = (lax.ppermute(mine, 'c', SWAP), lax.ppermute(theirs, 'c', SWAP))  7.19 us
    pallas_call x6, Pallas kernels, whole_kernel(): pl.pallas_call(body, out_shape=outputs, in_specs=[pl.BlockSpec(memory_spa...  6.76 us
    ppermute x1, waiting for transfers between devices, beside_sums(): lax.ppermute(lax.dynamic_index_in_dim(far, 1 - xl, 0, keepdims=False), 'x...  6.2 us
  transfers between devices with their start and end apart: 16, of which 6 were waited for; matrix products, arithmetic and copies ran while one was open for 2% of the time, Pallas kernels for 8%

profile of v6, /device:TPU:1, one launch (start us, length us, event | category | flops | bytes accessed | tf_op | source)
XLA Modules:
  0.0 123.6 jit_solution(11931090068548853175)
XLA Ops:
  0.0 2.5 %norm_rows.1 = bf16[8,64,1024]{2,1,0:T(8,128)(2,1)} custom-call(s32[1]{0:T(128)} %bitcast.12.core_ref, s32[1]{0:T(128)} %bitcast.13.pair_ref, bf16[128,8192]{1,0:T(8,128)(2,1)} %other_ref.1, bf16[128,8192]{1,0:T(8,128)(2,1)} %other_ref.1, f32[1,8192]{1,0:T(1,128)} %bitcast.27, f32[1,8192]{1,0:T(1,128)} %bitcast.28), custom_call_target="tpu_custom_call" | custom-call | flops 2097152 | bytes 2097152 | tf_op jit(solution)/shard_map/norm_rows/pallas_call | solution.py:45
  2.5 11.0 %all-to-all-start = ((bf16[8,64,1024]{2,1,0:T(8,128)(2,1)}), bf16[8,64,1024]{2,1,0:T(8,128)(2,1)S(1)}, u32[]{:S(2)}, u32[]{:S(2)}) async-start(bf16[8,64,1024]{2,1,0:T(8,128)(2,1)} %norm_rows.1), calls=%async_computation | async-start | bytes 2097152 | tf_op jit(solution)/shard_map/all_to_all | solution.py:219
  13.5 33.0 %conditional.2 = (bf16[896,1024]{1,0:T(8,128)(2,1)S(1)}, bf16[896,1024]{1,0:T(8,128)(2,1)}, bf16[2,32,1408]{2,1,0:T(8,128)(2,1)S(1)}, bf16[2,32,1408]{2,1,0:T(8,...) conditional(s32[]{:T(128)} %convert_element_type.19, () %tuple.27, ...), branch_computations={%region_0.0_spmd, %region_1.0_spmd} | conditional | flops 1835008 | bytes 35045944 | solution.py:182
  13.5 1.3 %pad_maximum_fusion.own_ref = bf16[896,512]{1,0:T(8,128)(2,1)S(1)} fusion(bf16[448,512]{1,0:T(8,128)(2,1)} %bitcast.26, bf16[448,512]{1,0:T(8,128)(2,1)} %bitcast.25), kind=kLoop, calls=%fused_computation | loop fusion | flops 1835008 | bytes 1835008 | tf_op jit(solution)/shard_map/cond/branch_1_fun/concatenate | solution.py:192
  14.9 4.7 %collective-permute-start = (bf16[896,512]{1,0:T(8,128)(2,1)S(1)}, bf16[896,512]{1,0:T(8,128)(2,1)S(1)}, u32[]{:S(2)}, u32[]{:S(2)}) collective-permute-start(bf16[896,512]{1,0:T(8,128)(2,1)S(1)} %pad_maximum_fusion.own_ref), channel_id=1, source_target_pairs={{0,16},{16,0},{1,17},{17,1},{2,18},{18,2},{3,19},{19,3},{4,20},{20... | collective-permute-start | bytes 2752520 | tf_op jit(solution)/shard_map/cond/branch_1_fun/ppermute | solution.py:193
  20.4 5.9 %collective-permute-start.1 = (bf16[2,32,1408]{2,1,0:T(8,128)(2,1)S(1)}, bf16[2,32,1408]{2,1,0:T(8,128)(2,1)S(1)}, u32[]{:S(2)}, u32[]{:S(2)}) collective-permute-start(bf16[2,32,1408]{2,1,0:T(8,128)(2,1)S(1)} %get-tuple-element.47), channel_id=1, source_target_pairs={{0,384},{16,144},{64,448},{80,208},{128,0},{144,272},{192,64},{208... | collective-permute-start | bytes 540680 | tf_op jit(solution)/shard_map/cond/branch_1_fun/ppermute | solution.py:189
  26.2 1.9 %collective-permute-start.2 = (bf16[2,32,1408]{2,1,0:T(8,128)(2,1)S(1)}, bf16[2,32,1408]{2,1,0:T(8,128)(2,1)S(1)}, u32[]{:S(2)}, u32[]{:S(2)}) collective-permute-start(bf16[2,32,1408]{2,1,0:T(8,128)(2,1)S(1)} %get-tuple-element.48), channel_id=1, source_target_pairs={{0,192},{16,336},{64,256},{80,400},{128,320},{144,464},{192,384},{... | collective-permute-start | bytes 540680 | tf_op jit(solution)/shard_map/cond/branch_1_fun/ppermute | solution.py:189
  28.2 3.0 %collective-permute-start.3 = (bf16[2,32,1408]{2,1,0:T(8,128)(2,1)S(1)}, bf16[2,32,1408]{2,1,0:T(8,128)(2,1)S(1)}, u32[]{:S(2)}, u32[]{:S(2)}) collective-permute-start(bf16[2,32,1408]{2,1,0:T(8,128)(2,1)S(1)} %get-tuple-element.49), channel_id=1, source_target_pairs={{0,448},{16,80},{64,0},{80,144},{128,64},{144,208},{192,128},{208,... | collective-permute-start | bytes 540680 | tf_op jit(solution)/shard_map/cond/branch_1_fun/ppermute | solution.py:189
  31.1 3.7 %collective-permute-start.4 = (bf16[896,512]{1,0:T(8,128)(2,1)S(1)}, bf16[896,512]{1,0:T(8,128)(2,1)S(1)}, u32[]{:S(2)}, u32[]{:S(2)}) collective-permute-start(bf16[896,512]{1,0:T(8,128)(2,1)S(1)} %pad_maximum_fusion.own_ref), channel_id=1, source_target_pairs={{0,1},{1,0},{2,3},{3,2},{4,5},{5,4},{6,7},{7,6},{8,9},{9,8},{10,11... | collective-permute-start | bytes 2752520 | tf_op jit(solution)/shard_map/cond/branch_1_fun/ppermute | solution.py:199
  34.9 4.5 %collective-permute-done.2 = bf16[2,32,1408]{2,1,0:T(8,128)(2,1)S(1)} collective-permute-done((bf16[2,32,1408]{2,1,0:T(8,128)(2,1)S(1)}, bf16[2,32,1408]{2,1,0:T(8,128)(2,1)S(1)}, u32[]{:S(2)}, u32[]{:S(2)}) %collective-permute-start.2) | collective-permute-done | bytes 180256 | tf_op jit(solution)/shard_map/cond/branch_1_fun/ppermute | solution.py:189
  39.4 3.5 %collective-permute-start.5 = (bf16[896,512]{1,0:T(8,128)(2,1)S(1)}, bf16[896,512]{1,0:T(8,128)(2,1)S(1)}, u32[]{:S(2)}, u32[]{:S(2)}) collective-permute-start(bf16[896,512]{1,0:T(8,128)(2,1)S(1)} %collective-permute-done.partner_ref), channel_id=1, source_target_pairs={{0,1},{1,0},{2,3},{3,2},{4,5},{5,4},{6,7},{7,6},{8,9},{9,8},{10,11... | collective-permute-start | bytes 2752520 | tf_op jit(solution)/shard_map/cond/branch_1_fun/ppermute | solution.py:199
  42.9 1.9 %collective-permute-start.6 = (bf16[128,256]{1,0:T(8,128)(2,1)S(1)}, bf16[128,256]{1,0:T(8,128)(2,1)}, u32[]{:S(2)}, u32[]{:S(2)}) collective-permute-start(bf16[128,256]{1,0:T(8,128)(2,1)S(1)} %get-tuple-element.56), channel_id=1, source_target_pairs={{0,1},{1,0},{2,3},{3,2},{4,5},{5,4},{6,7},{7,6},{8,9},{9,8},{10,11... | collective-permute-start | bytes 196616 | tf_op jit(solution)/shard_map/cond/branch_1_fun/ppermute | solution.py:203
  45.1 1.4 %weights.3 = bf16[896,1024]{1,0:T(8,128)(2,1)} custom-call(bf16[896,512]{1,0:T(8,128)(2,1)S(1)} %collective-permute-done.4.own_ref, bf16[896,512]{1,0:T(8,128)(2,1)S(1)} %collective-permute-done.5.partner_ref), custom_call_target="tpu_custom_call" | custom-call | bytes 3670016 | tf_op jit(solution)/shard_map/cond/branch_1_fun/weights/pallas_call | solution.py:104
  46.5 2.8 %terms.2 = bf16[4,64,1792]{2,1,0:T(8,128)(2,1)S(1)} custom-call(s32[1]{0:T(128)} %bitcast.15.parity_ref, bf16[8,64,1024]{2,1,0:T(8,128)(2,1)S(1)} %all-to-all-done.rows_ref, bf16[896,1024]{1,0:T(8,128)(2,1)S(1)} %get-tuple-element.112.weight_ref, bf16[896,1024]{1,0:T(8,128)(2,1)} %get-tuple-element.113.beside_ref), custom_call_target="tpu_custom_call" | custom-call | flops 939524096 | bytes 3145728 | tf_op jit(solution)/shard_map/terms/pallas_call | solution.py:83
  49.3 8.3 %collective-permute-start.12 = (bf16[4,64,1792]{2,1,0:T(8,128)(2,1)S(1)}, bf16[4,64,1792]{2,1,0:T(8,128)(2,1)S(1)}, u32[]{:S(2)}, u32[]{:S(2)}) collective-permute-start(bf16[4,64,1792]{2,1,0:T(8,128)(2,1)S(1)} %terms.2), channel_id=1, source_target_pairs={{0,2},{1,15},{2,0},{3,5},{4,6},{5,3},{6,4},{7,9},{8,10},{9,7},{10,... | collective-permute-start | bytes 2752520 | tf_op jit(solution)/shard_map/ppermute | solution.py:229
  57.6 4.0 %collective-permute-start.11 = (bf16[2,32,1408]{2,1,0:T(8,128)(2,1)}, bf16[2,32,1408]{2,1,0:T(8,128)(2,1)}, u32[]{:S(2)}, u32[]{:S(2)}) collective-permute-start(bf16[2,32,1408]{2,1,0:T(8,128)(2,1)} %get-tuple-element.119), channel_id=1, source_target_pairs={{0,256},{16,272},{64,320},{80,336},{128,384},{144,400},{192,448},{... | collective-permute-start | bytes 540680 | tf_op jit(solution)/shard_map/ppermute | solution.py:189
  61.7 2.8 %terms.3.keep_ref = bf16[4,64,1792]{2,1,0:T(8,128)(2,1)S(1)} custom-call(s32[1]{0:T(128)} %bitcast.16.parity_ref, bf16[8,64,1024]{2,1,0:T(8,128)(2,1)S(1)} %all-to-all-done.rows_ref, bf16[896,1024]{1,0:T(8,128)(2,1)S(1)} %get-tuple-element.112.weight_ref, bf16[896,1024]{1,0:T(8,128)(2,1)} %get-tuple-element.113.beside_ref), custom_call_target="tpu_custom_call" | custom-call | flops 939524096 | bytes 3145728 | tf_op jit(solution)/shard_map/terms/pallas_call | solution.py:83
  64.5 4.3 %collective-permute-done.12.got_ref = bf16[4,64,1792]{2,1,0:T(8,128)(2,1)S(1)} collective-permute-done((bf16[4,64,1792]{2,1,0:T(8,128)(2,1)S(1)}, bf16[4,64,1792]{2,1,0:T(8,128)(2,1)S(1)}, u32[]{:S(2)}, u32[]{:S(2)}) %collective-permute-start.12) | collective-permute-done | bytes 917536 | tf_op jit(solution)/shard_map/ppermute | solution.py:229
  68.8 1.1 add_terms.1
  69.9 2.8 %collective-permute-done.11 = bf16[2,32,1408]{2,1,0:T(8,128)(2,1)} collective-permute-done((bf16[2,32,1408]{2,1,0:T(8,128)(2,1)}, bf16[2,32,1408]{2,1,0:T(8,128)(2,1)}, u32[]{:S(2)}, u32[]{:S(2)}) %collective-permute-start.11) | collective-permute-done | bytes 180256 | tf_op jit(solution)/shard_map/ppermute | solution.py:189
  72.7 3.8 %all-to-all-start.1 = ((bf16[4,64,1792]{2,1,0:T(8,128)(2,1)}), bf16[4,64,1792]{2,1,0:T(8,128)(2,1)S(1)}, u32[]{:S(2)}, u32[]{:S(2)}) async-start(bf16[4,64,1792]{2,1,0:T(8,128)(2,1)} %add_terms.1), calls=%async_computation.1 | async-start | bytes 1835008 | tf_op jit(solution)/shard_map/all_to_all | solution.py:236
  76.6 21.6 %conditional.3 = (bf16[512,896]{1,0:T(8,128)(2,1)}, bf16[512,128]{1,0:T(8,128)(2,1)S(1)}) conditional(s32[]{:T(128)} %convert_element_type.19, () %tuple.33, (s32[]{:T(128)}, s32[]{:T(128)}, s32[]{:T(128)}, s32[]{:T(128)}, bf16[2,32,1408]{2,1,0:T(8,128)(2,1)}, /*index=5*/bf16[2,32,1408]{2,1,0:T(8,128)(2,1)S(1)}, bf16[2,32,1408]{2,1,0:T(8,128)(2,1)S(1)}, ...), branch_computations={%region_3.4_spmd, %region_4.5_spmd} | conditional | flops 4 | bytes 9363682 | solution.py:182
  77.6 2.2 %collective-permute-start.7 = (bf16[4,32,1408]{2,1,0:T(8,128)(2,1)S(1)}, bf16[4,32,1408]{2,1,0:T(8,128)(2,1)S(1)}, u32[]{:S(2)}, u32[]{:S(2)}) collective-permute-start(bf16[4,32,1408]{2,1,0:T(8,128)(2,1)S(1)} %get-tuple-element.66), channel_id=1, source_target_pairs={{0,32},{32,0},{1,33},{33,1},{2,34},{34,2},{3,35},{35,3},{4,36},{36... | collective-permute-start | bytes 1081352 | tf_op jit(solution)/shard_map/cond/branch_1_fun/ppermute | solution.py:210
  79.8 1.9 %collective-permute-start.10 = (bf16[3,32,1408]{2,1,0:T(8,128)(2,1)S(1)}, bf16[3,32,1408]{2,1,0:T(8,128)(2,1)S(1)}, u32[]{:S(2)}, u32[]{:S(2)}) collective-permute-start(bf16[3,32,1408]{2,1,0:T(8,128)(2,1)S(1)} %get-tuple-element.68), channel_id=1, source_target_pairs={{0,48},{16,32},{32,16},{48,0},{1,49},{17,33},{33,17},{49,1},{2,50}... | collective-permute-start | bytes 811016 | tf_op jit(solution)/shard_map/cond/branch_1_fun/ppermute | solution.py:209
  81.7 4.8 %collective-permute-start.9 = (bf16[3,32,1408]{2,1,0:T(8,128)(2,1)S(1)}, bf16[3,32,1408]{2,1,0:T(8,128)(2,1)S(1)}, u32[]{:S(2)}, u32[]{:S(2)}) collective-permute-start(bf16[3,32,1408]{2,1,0:T(8,128)(2,1)S(1)} %get-tuple-element.67), channel_id=1, source_target_pairs={{0,16},{16,0},{1,17},{17,1},{2,18},{18,2},{3,19},{19,3},{4,20},{20... | collective-permute-start | bytes 811016 | tf_op jit(solution)/shard_map/cond/branch_1_fun/ppermute | solution.py:208
  87.5 2.2 %collective-permute-start.8 = (bf16[32,1408]{1,0:T(8,128)(2,1)S(1)}, bf16[32,1408]{1,0:T(8,128)(2,1)S(1)}, u32[]{:S(2)}, u32[]{:S(2)}) collective-permute-start(bf16[32,1408]{1,0:T(8,128)(2,1)S(1)} %dynamic-slice_bitcast_fusion), channel_id=1, source_target_pairs={{0,32},{32,0},{1,33},{33,1},{2,34},{34,2},{3,35},{35,3},{4,36},{36... | collective-permute-start | bytes 270344 | tf_op jit(solution)/shard_map/cond/branch_1_fun/ppermute | solution.py:211
  89.7 6.2 %collective-permute-done.8.refs_6_ = bf16[32,1408]{1,0:T(8,128)(2,1)S(1)} collective-permute-done((bf16[32,1408]{1,0:T(8,128)(2,1)S(1)}, bf16[32,1408]{1,0:T(8,128)(2,1)S(1)}, u32[]{:S(2)}, u32[]{:S(2)}) %collective-permute-start.8) | collective-permute-done | bytes 90144 | tf_op jit(solution)/shard_map/cond/branch_1_fun/ppermute | solution.py:211
  95.9 2.3 %gather_factors.1 = (bf16[8,2,32,896]{3,2,1,0:T(8,128)(2,1)}, bf16[512,128]{1,0:T(8,128)(2,1)S(1)}, bf16[8,2,32,512]{3,2,1,0:T(8,128)(2,1)}) custom-call(s32[1]{0:T(128)} %bitcast.6.c_ref, s32[1]{0:T(128)} %bitcast.7.xl_ref, s32[1]{0:T(128)} %bitcast.8.y_ref, s32[1]{0:T(128)} %bitcast.9.xh_ref, bf16[2,32,1408]{2,1,0:T(8,128)(2,1)} %get-tuple-element.61.refs_0_, ...), custom_call_target="tpu_custom_call" | custom-call | bytes 3596288 | tf_op jit(solution)/shard_map/cond/branch_1_fun/gather_factors/pallas_call | solution.py:104
  98.2 1.1 all-to-all-done.1
  99.7 2.9 %collective-permute-start.13 = (bf16[64,896]{1,0:T(8,128)(2,1)S(1)}, bf16[64,896]{1,0:T(8,128)(2,1)S(1)}, u32[]{:S(2)}, u32[]{:S(2)}) collective-permute-start(bf16[64,896]{1,0:T(8,128)(2,1)S(1)} %pad_maximum_fusion.2), channel_id=1, source_target_pairs={{0,1},{1,0},{2,3},{3,2},{4,5},{5,4},{6,7},{7,6},{8,9},{9,8},{10,11... | collective-permute-start | bytes 344072 | tf_op jit(solution)/shard_map/ppermute | solution.py:246
  103.6 1.6 %convolution_convert_fusion = bf16[512,128]{1,0:T(8,128)(2,1)S(1)} fusion(bf16[512,896]{1,0:T(8,128)(2,1)} %get-tuple-element.132, bf16[64,896]{1,0:T(8,128)(2,1)S(1)} %get-tuple-element.139, bf16[64,896]{1,0:T(8,128)(2,1)S(1)} %get-tuple-element.138), kind=kOutput, calls=%fused_computation.3 | convolution fusion | flops 117964800 | bytes 1277952 | tf_op jit(solution)/shard_map/dot_general | solution.py:247
  105.2 17.8 %all_to_all.15 = bf16[16,64,128]{2,1,0:T(8,128)(2,1)S(1)} all-to-all(bf16[16,64,128]{2,1,0:T(8,128)(2,1)S(1)} %pad_maximum_fusion.1), channel_id=1, replica_groups=mesh['y'=8,'xl'=2,'xh'=2,'zh'=4,'zl'=2,'c'=2] {'y','xl'}, dimensions={0} | all-to-all | bytes 524288 | tf_op jit(solution)/shard_map/all_to_all | solution.py:250
  (41 shorter events, 4.8 us)
Async XLA Ops:
  2.5 11.0 %copy-start.8 = (bf16[128,256]{1,0:T(8,128)(2,1)S(1)}, bf16[128,256]{1,0:T(8,128)(2,1)}, u32[]{:S(2)}) copy-start(bf16[128,256]{1,0:T(8,128)(2,1)} %param.15) | copy-start | bytes 196612
  2.5 44.0 %all-to-all-start = ((bf16[8,64,1024]{2,1,0:T(8,128)(2,1)}), bf16[8,64,1024]{2,1,0:T(8,128)(2,1)S(1)}, u32[]{:S(2)}, u32[]{:S(2)}) async-start(bf16[8,64,1024]{2,1,0:T(8,128)(2,1)} %norm_rows.1), calls=%async_computation | async-start | bytes 2097152 | tf_op jit(solution)/shard_map/all_to_all | solution.py:219
  13.5 6.0 %copy-start.6 = (bf16[1,32,14336]{2,1,0:T(8,128)(2,1)S(1)}, bf16[1,32,14336]{2,1,0:T(8,128)(2,1)}, u32[]{:S(2)}) copy-start(bf16[1,32,14336]{2,1,0:T(8,128)(2,1)} %get-tuple-element.45) | copy-start | bytes 2752516 | tf_op jit(solution)/shard_map/cond
  13.5 6.0 %copy-start.7 = (bf16[1,32,8192]{2,1,0:T(8,128)(2,1)S(1)}, bf16[1,32,8192]{2,1,0:T(8,128)(2,1)}, u32[]{:S(2)}) copy-start(bf16[1,32,8192]{2,1,0:T(8,128)(2,1)} %get-tuple-element.46) | copy-start | bytes 1572868 | tf_op jit(solution)/shard_map/cond
  14.9 24.6 %collective-permute-start = (bf16[896,512]{1,0:T(8,128)(2,1)S(1)}, bf16[896,512]{1,0:T(8,128)(2,1)S(1)}, u32[]{:S(2)}, u32[]{:S(2)}) collective-permute-start(bf16[896,512]{1,0:T(8,128)(2,1)S(1)} %pad_maximum_fusion.own_ref), channel_id=1, source_target_pairs={{0,16},{16,0},{1,17},{17,1},{2,18},{18,2},{3,19},{19,3},{4,20},{20... | collective-permute-start | bytes 2752520 | tf_op jit(solution)/shard_map/cond/branch_1_fun/ppermute | solution.py:193
  20.4 14.5 %collective-permute-start.1 = (bf16[2,32,1408]{2,1,0:T(8,128)(2,1)S(1)}, bf16[2,32,1408]{2,1,0:T(8,128)(2,1)S(1)}, u32[]{:S(2)}, u32[]{:S(2)}) collective-permute-start(bf16[2,32,1408]{2,1,0:T(8,128)(2,1)S(1)} %get-tuple-element.47), channel_id=1, source_target_pairs={{0,384},{16,144},{64,448},{80,208},{128,0},{144,272},{192,64},{208... | collective-permute-start | bytes 540680 | tf_op jit(solution)/shard_map/cond/branch_1_fun/ppermute | solution.py:189
  26.2 13.2 %collective-permute-start.2 = (bf16[2,32,1408]{2,1,0:T(8,128)(2,1)S(1)}, bf16[2,32,1408]{2,1,0:T(8,128)(2,1)S(1)}, u32[]{:S(2)}, u32[]{:S(2)}) collective-permute-start(bf16[2,32,1408]{2,1,0:T(8,128)(2,1)S(1)} %get-tuple-element.48), channel_id=1, source_target_pairs={{0,192},{16,336},{64,256},{80,400},{128,320},{144,464},{192,384},{... | collective-permute-start | bytes 540680 | tf_op jit(solution)/shard_map/cond/branch_1_fun/ppermute | solution.py:189
  28.2 11.3 %collective-permute-start.3 = (bf16[2,32,1408]{2,1,0:T(8,128)(2,1)S(1)}, bf16[2,32,1408]{2,1,0:T(8,128)(2,1)S(1)}, u32[]{:S(2)}, u32[]{:S(2)}) collective-permute-start(bf16[2,32,1408]{2,1,0:T(8,128)(2,1)S(1)} %get-tuple-element.49), channel_id=1, source_target_pairs={{0,448},{16,80},{64,0},{80,144},{128,64},{144,208},{192,128},{208,... | collective-permute-start | bytes 540680 | tf_op jit(solution)/shard_map/cond/branch_1_fun/ppermute | solution.py:189
  31.1 13.9 %collective-permute-start.4 = (bf16[896,512]{1,0:T(8,128)(2,1)S(1)}, bf16[896,512]{1,0:T(8,128)(2,1)S(1)}, u32[]{:S(2)}, u32[]{:S(2)}) collective-permute-start(bf16[896,512]{1,0:T(8,128)(2,1)S(1)} %pad_maximum_fusion.own_ref), channel_id=1, source_target_pairs={{0,1},{1,0},{2,3},{3,2},{4,5},{5,4},{6,7},{7,6},{8,9},{9,8},{10,11... | collective-permute-start | bytes 2752520 | tf_op jit(solution)/shard_map/cond/branch_1_fun/ppermute | solution.py:199
  34.9 10.1 %copy-start = (bf16[2,32,1408]{2,1,0:T(8,128)(2,1)}, bf16[2,32,1408]{2,1,0:T(8,128)(2,1)S(1)}, u32[]{:S(2)}) copy-start(bf16[2,32,1408]{2,1,0:T(8,128)(2,1)S(1)} %collective-permute-done.1) | copy-start | bytes 540676 | tf_op jit(solution)/shard_map/cond
  39.4 5.6 %copy-start.2 = (bf16[2,32,1408]{2,1,0:T(8,128)(2,1)}, bf16[2,32,1408]{2,1,0:T(8,128)(2,1)S(1)}, u32[]{:S(2)}) copy-start(bf16[2,32,1408]{2,1,0:T(8,128)(2,1)S(1)} %collective-permute-done.2) | copy-start | bytes 540676 | tf_op jit(solution)/shard_map/cond
  39.4 5.6 %copy-start.4 = (bf16[2,32,1408]{2,1,0:T(8,128)(2,1)}, bf16[2,32,1408]{2,1,0:T(8,128)(2,1)S(1)}, u32[]{:S(2)}) copy-start(bf16[2,32,1408]{2,1,0:T(8,128)(2,1)S(1)} %collective-permute-done.3) | copy-start | bytes 540676 | tf_op jit(solution)/shard_map/cond
  39.4 5.6 %collective-permute-start.5 = (bf16[896,512]{1,0:T(8,128)(2,1)S(1)}, bf16[896,512]{1,0:T(8,128)(2,1)S(1)}, u32[]{:S(2)}, u32[]{:S(2)}) collective-permute-start(bf16[896,512]{1,0:T(8,128)(2,1)S(1)} %collective-permute-done.partner_ref), channel_id=1, source_target_pairs={{0,1},{1,0},{2,3},{3,2},{4,5},{5,4},{6,7},{7,6},{8,9},{9,8},{10,11... | collective-permute-start | bytes 2752520 | tf_op jit(solution)/shard_map/cond/branch_1_fun/ppermute | solution.py:199
  42.9 3.6 %collective-permute-start.6 = (bf16[128,256]{1,0:T(8,128)(2,1)S(1)}, bf16[128,256]{1,0:T(8,128)(2,1)}, u32[]{:S(2)}, u32[]{:S(2)}) collective-permute-start(bf16[128,256]{1,0:T(8,128)(2,1)S(1)} %get-tuple-element.56), channel_id=1, source_target_pairs={{0,1},{1,0},{2,3},{3,2},{4,5},{5,4},{6,7},{7,6},{8,9},{9,8},{10,11... | collective-permute-start | bytes 196616 | tf_op jit(solution)/shard_map/cond/branch_1_fun/ppermute | solution.py:203
  45.0 1.4 %copy-start.1 = (bf16[2,32,1408]{2,1,0:T(8,128)(2,1)S(1)}, bf16[2,32,1408]{2,1,0:T(8,128)(2,1)}, u32[]{:S(2)}) copy-start(bf16[2,32,1408]{2,1,0:T(8,128)(2,1)} %copy-done) | copy-start | bytes 540676 | tf_op jit(solution)/shard_map/cond
  45.1 1.4 %copy-start.3 = (bf16[2,32,1408]{2,1,0:T(8,128)(2,1)S(1)}, bf16[2,32,1408]{2,1,0:T(8,128)(2,1)}, u32[]{:S(2)}) copy-start(bf16[2,32,1408]{2,1,0:T(8,128)(2,1)} %copy-done.2) | copy-start | bytes 540676 | tf_op jit(solution)/shard_map/cond
  45.1 1.4 %copy-start.5 = (bf16[2,32,1408]{2,1,0:T(8,128)(2,1)S(1)}, bf16[2,32,1408]{2,1,0:T(8,128)(2,1)}, u32[]{:S(2)}) copy-start(bf16[2,32,1408]{2,1,0:T(8,128)(2,1)} %copy-done.4) | copy-start | bytes 540676 | tf_op jit(solution)/shard_map/cond
  49.3 19.5 %collective-permute-start.12 = (bf16[4,64,1792]{2,1,0:T(8,128)(2,1)S(1)}, bf16[4,64,1792]{2,1,0:T(8,128)(2,1)S(1)}, u32[]{:S(2)}, u32[]{:S(2)}) collective-permute-start(bf16[4,64,1792]{2,1,0:T(8,128)(2,1)S(1)} %terms.2), channel_id=1, source_target_pairs={{0,2},{1,15},{2,0},{3,5},{4,6},{5,3},{6,4},{7,9},{8,10},{9,7},{10,... | collective-permute-start | bytes 2752520 | tf_op jit(solution)/shard_map/ppermute | solution.py:229
  57.6 15.1 %collective-permute-start.11 = (bf16[2,32,1408]{2,1,0:T(8,128)(2,1)}, bf16[2,32,1408]{2,1,0:T(8,128)(2,1)}, u32[]{:S(2)}, u32[]{:S(2)}) collective-permute-start(bf16[2,32,1408]{2,1,0:T(8,128)(2,1)} %get-tuple-element.119), channel_id=1, source_target_pairs={{0,256},{16,272},{64,320},{80,336},{128,384},{144,400},{192,448},{... | collective-permute-start | bytes 540680 | tf_op jit(solution)/shard_map/ppermute | solution.py:189
  72.7 26.5 %all-to-all-start.1 = ((bf16[4,64,1792]{2,1,0:T(8,128)(2,1)}), bf16[4,64,1792]{2,1,0:T(8,128)(2,1)S(1)}, u32[]{:S(2)}, u32[]{:S(2)}) async-start(bf16[4,64,1792]{2,1,0:T(8,128)(2,1)} %add_terms.1), calls=%async_computation.1 | async-start | bytes 1835008 | tf_op jit(solution)/shard_map/all_to_all | solution.py:236
  77.6 18.3 %collective-permute-start.7 = (bf16[4,32,1408]{2,1,0:T(8,128)(2,1)S(1)}, bf16[4,32,1408]{2,1,0:T(8,128)(2,1)S(1)}, u32[]{:S(2)}, u32[]{:S(2)}) collective-permute-start(bf16[4,32,1408]{2,1,0:T(8,128)(2,1)S(1)} %get-tuple-element.66), channel_id=1, source_target_pairs={{0,32},{32,0},{1,33},{33,1},{2,34},{34,2},{3,35},{35,3},{4,36},{36... | collective-permute-start | bytes 1081352 | tf_op jit(solution)/shard_map/cond/branch_1_fun/ppermute | solution.py:210
  79.8 16.1 %collective-permute-start.10 = (bf16[3,32,1408]{2,1,0:T(8,128)(2,1)S(1)}, bf16[3,32,1408]{2,1,0:T(8,128)(2,1)S(1)}, u32[]{:S(2)}, u32[]{:S(2)}) collective-permute-start(bf16[3,32,1408]{2,1,0:T(8,128)(2,1)S(1)} %get-tuple-element.68), channel_id=1, source_target_pairs={{0,48},{16,32},{32,16},{48,0},{1,49},{17,33},{33,17},{49,1},{2,50}... | collective-permute-start | bytes 811016 | tf_op jit(solution)/shard_map/cond/branch_1_fun/ppermute | solution.py:209
  81.7 14.2 %collective-permute-start.9 = (bf16[3,32,1408]{2,1,0:T(8,128)(2,1)S(1)}, bf16[3,32,1408]{2,1,0:T(8,128)(2,1)S(1)}, u32[]{:S(2)}, u32[]{:S(2)}) collective-permute-start(bf16[3,32,1408]{2,1,0:T(8,128)(2,1)S(1)} %get-tuple-element.67), channel_id=1, source_target_pairs={{0,16},{16,0},{1,17},{17,1},{2,18},{18,2},{3,19},{19,3},{4,20},{20... | collective-permute-start | bytes 811016 | tf_op jit(solution)/shard_map/cond/branch_1_fun/ppermute | solution.py:208
  87.5 8.4 %collective-permute-start.8 = (bf16[32,1408]{1,0:T(8,128)(2,1)S(1)}, bf16[32,1408]{1,0:T(8,128)(2,1)S(1)}, u32[]{:S(2)}, u32[]{:S(2)}) collective-permute-start(bf16[32,1408]{1,0:T(8,128)(2,1)S(1)} %dynamic-slice_bitcast_fusion), channel_id=1, source_target_pairs={{0,32},{32,0},{1,33},{33,1},{2,34},{34,2},{3,35},{35,3},{4,36},{36... | collective-permute-start | bytes 270344 | tf_op jit(solution)/shard_map/cond/branch_1_fun/ppermute | solution.py:211
  99.7 3.9 %collective-permute-start.13 = (bf16[64,896]{1,0:T(8,128)(2,1)S(1)}, bf16[64,896]{1,0:T(8,128)(2,1)S(1)}, u32[]{:S(2)}, u32[]{:S(2)}) collective-permute-start(bf16[64,896]{1,0:T(8,128)(2,1)S(1)} %pad_maximum_fusion.2), channel_id=1, source_target_pairs={{0,1},{1,0},{2,3},{3,2},{4,5},{5,4},{6,7},{7,6},{8,9},{9,8},{10,11... | collective-permute-start | bytes 344072 | tf_op jit(solution)/shard_map/ppermute | solution.py:246
